TPU v7x, 32 devices: a whole 2x2x4 slice. The times are simulated.
32 devices in a mesh: dom: 4 (over y, x), head: 8 (over z, core).
Axes of the slice: x: 2, y: 2, z: 4, core: 2. Of those that a mesh axis runs over, the one named last changes fastest.
Arguments:
- tokens: bfloat16 [24, 64, 8192], P(None, 'dom', 'head'), may hold values from -6 to 6
- parents: int32 [64], replicated, may hold values from 0 to 63, as said below
- recurrent_state: float32 [64, 128, 64, 256], P('dom', 'head'), may hold values from -6 to 6
- value_history: float32 [64, 3, 8192], P('dom', None, 'head'), may hold values from -6 to 6
- mixing_history: float32 [64, 3, 2048], P('dom', None, 'head'), may hold values from -6 to 6
- input_gain: float32 [8192], P('head'), may hold values from 0.5 to 1.5
- gate_value_weight: bfloat16 [8192, 2, 8192], P(None, None, 'head'), may hold values from -0.0625 to 0.0625
- mixing_weight: bfloat16 [8192, 2048], P(None, 'head'), may hold values from -0.0625 to 0.0625
- step_weight: bfloat16 [8192, 128], P(None, 'head'), may hold values from -0.0625 to 0.0625
- value_kernel: float32 [4, 8192], P(None, 'head'), may hold values from -3 to 3
- value_offset: float32 [8192], P('head'), may hold values from -0.5 to 0.5
- mixing_kernel: float32 [4, 2048], P(None, 'head'), may hold values from -3 to 3
- mixing_offset: float32 [2048], P('head'), may hold values from -0.5 to 0.5
- step_offset: float32 [128], P('head'), may hold values from -4 to 0
- decay_log: float32 [128], P('head'), may hold values from -2 to 1.5
- skip_gain: float32 [128], P('head'), may hold values from 0.5 to 1.5
- output_gain: float32 [8192], P('head'), may hold values from 0.5 to 1.5
- output_weight: bfloat16 [8192, 8192], P('head'), may hold values from -0.0625 to 0.0625
Outputs:
- mixed: bfloat16 [24, 64, 8192], P(None, 'dom', 'head')
Inputs may be any that keep to these rules, and one draw needn't show every extreme that they name: parents comes from systematic resampling: it never falls with i, and offspring counts are very uneven, so that a particle's parent may sit several blocks of 16 particles away.
All inputs are finite; a program needn't handle non-finite values.
Results may differ from a plain program's by a relative error of at most 0.023.
Values may be sent and summed in bfloat16 or wider, within the bound.
No kernel may reach another device: no remote copies, remote signals or barrier semaphores. Data moves between devices by JAX's collectives and lax.ppermute only.
A program may use at most 256 MiB of HBM per device.

v0:
```python
import functools

import jax
import jax.numpy as jnp
from jax import lax
from jax.experimental import pallas as pl
from jax.experimental.pallas import tpu as pltpu
from jax.sharding import PartitionSpec as P


GROUPS = 4
CHUNKS = 2
LANES = 128
EXTRA = 8
PIECES = 4
HIGH = lax.Precision.HIGHEST
F32 = jnp.float32
BF16 = jnp.bfloat16


def params(mib=48):
    return pltpu.CompilerParams(vmem_limit_bytes=mib << 20)


def cost(flops, nbytes):
    return pl.CostEstimate(flops=flops, bytes_accessed=nbytes, transcendentals=0)


def whole_spec(shape):
    return pl.BlockSpec(shape, lambda *_: (0,) * len(shape))


def silu(v):
    return v / (1.0 + jnp.exp(-v))


def prepare_kernel(tok_ref, gain_ref, out_ref):
    steps, particles, width = tok_ref.shape
    count = out_ref.shape[0]
    each = particles // count
    rows = steps * each
    padded = -(-rows // LANES) * LANES
    for k in range(count):
        x = tok_ref[...].astype(F32)[:, k * each : (k + 1) * each, :].reshape(rows, width)
        out_ref[k, :rows, :] = (x * gain_ref[...]).astype(BF16)
        sq = jnp.concatenate([x * x, jnp.zeros((padded - rows, width), F32)], axis=0)
        total = lax.dot_general(
            jnp.ones((EXTRA, width), F32),
            sq,
            (((1,), (1,)), ((), ())),
            precision=HIGH,
            preferred_element_type=F32,
        )
        high = total.astype(BF16).astype(F32)
        which = lax.broadcasted_iota(jnp.int32, total.shape, 0)
        both = jnp.where(which == 0, high, jnp.where(which == 1, total - high, 0.0))
        if padded < width:
            both = jnp.concatenate([both, jnp.zeros((EXTRA, width - padded), F32)], axis=1)
        out_ref[k, rows:, :] = both.astype(BF16)


def prepare(tokens, gain):
    steps, particles, width = tokens.shape
    rows = steps * particles // CHUNKS
    return pl.pallas_call(
        prepare_kernel,
        out_shape=jax.ShapeDtypeStruct((CHUNKS, rows + EXTRA, width), BF16),
        compiler_params=params(),
        name="prepare",
    )(tokens, gain.reshape(1, -1))


def place(hop, pairs, i, rank):
    if hop == 0:
        return rank ^ i, True
    z, core = rank >> 1, rank & 1
    a, b = z + hop, z - hop
    has_a, has_b = a < pairs, b >= 0
    near = jnp.where(has_a, 2 * a + 1 - core, rank)
    far = jnp.where(has_b, 2 * b + core, near)
    from_above = jnp.where(has_a, 2 * a + (core ^ (i & 1)), far)
    from_below = jnp.where(has_b, 2 * b + (core ^ (i & 1)), near)
    return jnp.where(i < 2, from_above, from_below), jnp.where(i < 2, has_a, has_b)


def fetch_slot(valid, xs, x_ref):
    i = pl.program_id(0)
    for k in range(len(xs) // CHUNKS):

        @pl.when((i == k) & valid)
        def _():
            for chunk in range(CHUNKS):
                x_ref[chunk] = xs[CHUNKS * k + chunk][...]


def start_sums(sums, befores):
    @pl.when(pl.program_id(0) == 0)
    def _():
        for k, ref in enumerate(sums):
            ref[...] = befores[k][...] if befores else jnp.zeros_like(ref)


def narrow_kernel(count, with_sums, where, rank, *refs):
    valid = where(pl.program_id(0), rank[0])[1]
    xs, refs = refs[:count], refs[count:]
    wm_ref, ws_ref = refs[:2]
    refs = refs[2:]
    befores, refs = (refs[:4], refs[4:]) if with_sums else ((), refs)
    mix_ref, step_ref, extra_ref, all_ref, x_ref, sem = refs
    fetch_slot(valid, xs, x_ref)
    start_sums((mix_ref, step_ref, extra_ref), befores)
    rows = mix_ref.shape[1]

    @pl.when(valid)
    def _():
        for k in range(CHUNKS):
            x = x_ref[k, :rows, :]
            mix_ref[k] += jnp.dot(x, wm_ref[...], preferred_element_type=F32)
            step_ref[k] += lax.dot_general(
                x, ws_ref[...], (((1,), (1,)), ((), ())), preferred_element_type=F32
            )
            extra_ref[k] += x_ref[k, rows:, :].astype(F32)
        block = where(pl.program_id(0), rank[0])[0]
        copy = pltpu.make_async_copy(x_ref, all_ref.at[block], sem)
        copy.start()
        copy.wait()


def split_kernel(*refs):
    w_ref, o_ref = refs[0], refs[-1]
    depth, _, width = w_ref.shape
    half = min(LANES, depth)
    row = lax.broadcasted_iota(jnp.int32, (2 * half, 2 * half), 0)
    col = lax.broadcasted_iota(jnp.int32, (2 * half, 2 * half), 1)
    source = jnp.where(row < half, 2 * row, 2 * (row - half) + 1)
    move = (source == col).astype(F32).astype(BF16)
    for i in range(depth // half):
        part = w_ref[i * half : (i + 1) * half].reshape(2 * half, width)
        moved = jnp.dot(move, part, preferred_element_type=F32).astype(BF16)
        o_ref[0, i * half : (i + 1) * half, :] = moved[:half]
        o_ref[1, i * half : (i + 1) * half, :] = moved[half:]


def split_weights(w, piece, before):
    depth, _, width = w.shape
    block = depth // (2 * PIECES)
    return pl.pallas_call(
        split_kernel,
        grid=(2,),
        in_specs=[pl.BlockSpec((block, 2, width), lambda k: (2 * piece + k, 0, 0))]
        + [pl.BlockSpec(memory_space=pl.ANY)] * len(before),
        out_specs=pl.BlockSpec((2, block, width), lambda k: (0, 2 * piece + k, 0)),
        out_shape=jax.ShapeDtypeStruct((2, depth, width), BF16),
        input_output_aliases={1 + k: k for k in range(len(before))},
        compiler_params=params(),
        cost_estimate=cost(4 * block * width * 512, 16 * block * width),
        name="split_weights",
    )(w, *before)


def wide_kernel(x_ref, w_ref, o_ref):
    rows = o_ref.shape[1]
    depth = w_ref.shape[1]
    x = x_ref[0, :, :rows, :].astype(F32).reshape(CHUNKS * rows, depth).astype(BF16)
    y = jnp.dot(x, w_ref[0], preferred_element_type=F32).reshape(o_ref.shape)

    @pl.when(pl.program_id(0) == 0)
    def _():
        o_ref[...] = y

    @pl.when(pl.program_id(0) > 0)
    def _():
        o_ref[...] += y


def project_wide(which, features, weights):
    blocks, _, ext, width = features.shape
    rows = ext - EXTRA
    channels = weights.shape[2]
    shape = (CHUNKS, rows, channels)
    return pl.pallas_call(
        wide_kernel,
        grid=(blocks,),
        in_specs=[
            pl.BlockSpec((1, CHUNKS, ext, width), lambda i: (i, 0, 0, 0)),
            pl.BlockSpec((1, width, channels), lambda i: (which, i, 0)),
        ],
        out_specs=whole_spec(shape),
        out_shape=jax.ShapeDtypeStruct(shape, F32),
        compiler_params=params(),
        cost_estimate=cost(
            2 * CHUNKS * rows * width * blocks * channels, 2 * blocks * width * channels
        ),
        name="project_wide",
    )(features, weights)


def project_narrow(where, blocks, rank, arrays, mixing_weight, step_weight_t, sums):
    ext, width = arrays[0].shape
    rows = ext - EXTRA
    columns, heads = mixing_weight.shape[1], step_weight_t.shape[0]
    count = len(arrays) // CHUNKS
    shapes = [(CHUNKS, rows, columns), (CHUNKS, rows, heads), (CHUNKS, EXTRA, width)]
    anywhere = pl.BlockSpec(memory_space=pl.ANY)
    grid_spec = pltpu.PrefetchScalarGridSpec(
        num_scalar_prefetch=1,
        grid=(count,),
        in_specs=[whole_spec((ext, width))] * len(arrays)
        + [
            pl.BlockSpec((width, columns), lambda i, rank: (where(i, rank[0])[0], 0)),
            pl.BlockSpec((heads, width), lambda i, rank: (0, where(i, rank[0])[0])),
        ]
        + [whole_spec(x.shape) for x in sums[:3]]
        + [anywhere] * len(sums[3:]),
        out_specs=[whole_spec(x) for x in shapes] + [anywhere],
        scratch_shapes=[pltpu.VMEM((CHUNKS, ext, width), BF16), pltpu.SemaphoreType.DMA],
    )
    return pl.pallas_call(
        functools.partial(narrow_kernel, len(arrays), bool(sums), where),
        grid_spec=grid_spec,
        out_shape=[jax.ShapeDtypeStruct(x, F32) for x in shapes]
        + [jax.ShapeDtypeStruct((blocks, CHUNKS, ext, width), BF16)],
        input_output_aliases={len(arrays) + 3 + k: k for k in range(len(sums))},
        compiler_params=params(),
        cost_estimate=cost(
            2 * CHUNKS * rows * width * count * (columns + heads), 2 * count * width * columns
        ),
        name="project_narrow",
    )(rank, *arrays, mixing_weight, step_weight_t, *sums)


TOGETHER = 4


def owner_kernel(low, high, c_ref, s_ref, o_ref):
    p = pl.program_id(0)
    first, last = low[p], high[p]
    _, heads, head_width, state_width = s_ref.shape
    steps = c_ref.shape[1]
    channels = heads * head_width

    @pl.when(last > first)
    def _():
        state = s_ref[0].reshape(channels, state_width).astype(BF16)

        def some(g, carry):
            base = first + g * TOGETHER
            c = c_ref[pl.ds(base, TOGETHER)].astype(F32)
            c = c.reshape(TOGETHER * steps, state_width).astype(BF16)
            r = lax.dot_general(
                c, state, (((1,), (1,)), ((), ())), preferred_element_type=F32
            ).reshape(TOGETHER, steps, channels)
            for i in range(TOGETHER):

                @pl.when(base + i < last)
                def _():
                    o_ref[base + i] = r[i].astype(BF16)

            return carry

        lax.fori_loop(0, (last - first + TOGETHER - 1) // TOGETHER, some, 0)


def owner_reads(low, high, child_mix, state):
    children, steps, state_width = child_mix.shape
    children -= TOGETHER
    particles, heads, head_width, _ = state.shape
    channels = heads * head_width
    grid_spec = pltpu.PrefetchScalarGridSpec(
        num_scalar_prefetch=2,
        grid=(particles,),
        in_specs=[
            whole_spec(child_mix.shape),
            pl.BlockSpec((1, heads, head_width, state_width), lambda p, *_: (p, 0, 0, 0)),
        ],
        out_specs=whole_spec((children, steps, channels)),
    )
    return pl.pallas_call(
        owner_kernel,
        grid_spec=grid_spec,
        out_shape=jax.ShapeDtypeStruct((children, steps, channels), BF16),
        compiler_params=params(),
        cost_estimate=cost(
            2 * children * steps * channels * state_width, 4 * particles * channels * state_width
        ),
        name="owner_reads",
    )(low, high, child_mix, state)


def local_kernel(
    v_ref, rs_ref, hist_ref, tap_ref, bias_ref, b_ref, c_ref, step_ref, decay_ref, skip_ref,
    y_ref, cum_ref, dot_ref, head_width,
):
    steps, each, channels = v_ref.shape
    taps = tap_ref.shape[0]
    for t in range(steps):
        c = c_ref[t].astype(F32)
        for s in range(t + 1):
            product = jnp.sum(c * b_ref[s].astype(F32), axis=-1, keepdims=True)
            dot_ref[t * (t + 1) // 2 + s] = jnp.broadcast_to(product, (each, LANES))

    def tile(i, carry):
        at = pl.ds(pl.multiple_of(i * LANES, LANES), LANES)
        head = lax.broadcasted_iota(jnp.int32, (LANES, LANES), 0)
        lane = lax.broadcasted_iota(jnp.int32, (LANES, LANES), 1) + i * LANES
        spread = (lane // head_width == head).astype(F32)

        def expand(x):
            return jnp.dot(x, spread, precision=HIGH, preferred_element_type=F32)

        size = expand(step_ref[...]).reshape(steps, each, LANES)
        decay = expand(decay_ref[...]).reshape(steps, each, LANES)
        skip = expand(skip_ref[...])[0:1, :]
        seq = [hist_ref[k, :, at] for k in range(taps - 1)]
        seq += [v_ref[t, :, at] * rs_ref[t] for t in range(steps)]
        tap = tap_ref[:, at]
        bias = bias_ref[:, at]
        held = []
        cum = None
        for t in range(steps):
            total = bias
            for k in range(taps):
                total = total + tap[k : k + 1, :] * seq[t + k]
            value = silu(total)
            d = decay[t]
            cum = d if t == 0 else cum * d
            cum_ref[t, :, at] = cum
            held = [h * d for h in held] + [size[t] * value]
            y = skip * value
            for s in range(t + 1):
                y = y + dot_ref[t * (t + 1) // 2 + s] * held[s]
            y_ref[t, :, at] = y
        return carry

    lax.fori_loop(0, channels // LANES, tile, 0)


def local_reads(value, rs, history, taps, bias, b, c, size, decay, skip, head_width):
    steps, each, channels = value.shape
    return pl.pallas_call(
        functools.partial(local_kernel_entry, head_width),
        out_shape=[jax.ShapeDtypeStruct((steps, each, channels), F32)] * 2,
        scratch_shapes=[pltpu.VMEM((steps * (steps + 1) // 2, each, LANES), F32)],
        compiler_params=params(),
        cost_estimate=cost(steps * steps * each * channels * 16, 12 * steps * each * channels),
        name="local_reads",
    )(value, rs, history, taps, bias, b, c, size, decay, skip)


def local_kernel_entry(head_width, *refs):
    local_kernel(*refs, head_width=head_width)


def out_kernel(idx, x_ref, w_ref, o_ref):
    o_ref[0] = jnp.dot(x_ref[...], w_ref[...], preferred_element_type=F32).astype(BF16)


def project_out(idx, x, weight, width):
    rows, channels = x.shape
    count = idx.shape[0]
    grid_spec = pltpu.PrefetchScalarGridSpec(
        num_scalar_prefetch=1,
        grid=(count,),
        in_specs=[
            whole_spec((rows, channels)),
            pl.BlockSpec((channels, width), lambda i, idx: (0, idx[i])),
        ],
        out_specs=pl.BlockSpec((1, rows, width), lambda i, idx: (i, 0, 0)),
    )
    return pl.pallas_call(
        out_kernel,
        grid_spec=grid_spec,
        out_shape=jax.ShapeDtypeStruct((count, rows, width), BF16),
        compiler_params=params(),
        cost_estimate=cost(2 * rows * channels * count * width, 2 * channels * count * width),
        name="project_out",
    )(idx, x, weight)


def conv(previous, current, kernel, shift_bias):
    window = jnp.concatenate([previous, current], axis=0)
    length = current.shape[0]
    summed = jnp.zeros_like(current)
    for k in range(kernel.shape[0]):
        summed = summed + kernel[k] * window[k : k + length]
    return silu(summed + shift_bias)


def pad_lanes(x):
    return jnp.pad(x, ((0, 0), (0, LANES - x.shape[1])))


def body(
    tokens,
    parents,
    recurrent_state,
    value_history,
    mixing_history,
    input_gain,
    gate_value_weight,
    mixing_weight,
    step_weight,
    value_kernel,
    value_offset,
    mixing_kernel,
    mixing_offset,
    step_offset,
    decay_log,
    skip_gain,
    output_gain,
    output_weight,
):
    steps, particles, width = tokens.shape
    _, heads, head_width, state_width = recurrent_state.shape
    channels = heads * head_width
    each = particles // CHUNKS
    rows = steps * each
    doms = lax.axis_size("dom")
    dom = lax.axis_index("dom")
    ranks = lax.axis_size("head")
    rank = lax.axis_index("head")
    pairs = ranks // 2
    z, core = rank // 2, rank % 2
    features = width * ranks

    def permute(x, pairs_of, axis="head"):
        return lax.ppermute(x, axis, pairs_of)

    def swap(x):
        return permute(x, [(i, i ^ 1) for i in range(ranks)])

    def up(x, first, stop):
        moves = [(2 * i + c, 2 * i + 2 + c) for i in range(first, stop) for c in (0, 1)]
        return permute(x, moves)

    def down(x, first, stop):
        moves = [(2 * i + c, 2 * i - 2 + c) for i in range(first, stop) for c in (0, 1)]
        return permute(x, moves)

    def across(x, k):
        return permute(x, [(i, i ^ k) for i in range(doms)], "dom")

    prepared = prepare(tokens, input_gain)
    step_weight_t = step_weight.T

    at = rank.astype(jnp.int32).reshape(1)
    above = [prepared[k] for k in range(CHUNKS)]
    below = list(above)
    hops = [above + [swap(x) for x in above]]
    for s in range(1, pairs):
        for k in range(CHUNKS):
            above[k] = down(above[k], 1, pairs - s + 1)
            below[k] = up(below[k], s - 1, pairs - 1)
        hops.append(
            above + [swap(x) for x in above] + below + [swap(x) for x in below]
        )

    narrow = ()
    for s in range(pairs):
        where = functools.partial(place, s, pairs)
        narrow = project_narrow(
            where, ranks, at, hops[s], mixing_weight, step_weight_t, narrow
        )
    weights = ()
    for s in range(PIECES):
        weights = (split_weights(gate_value_weight, s, weights),)

    history = jnp.concatenate(
        [jnp.moveaxis(value_history, 1, 0), jnp.moveaxis(mixing_history, 1, 0)], axis=2
    ).astype(BF16)
    history, _ = lax.optimization_barrier((history, hops[1][0]))
    history_all = jnp.concatenate([history] + [across(history, k) for k in range(1, doms)], axis=1)
    first_child = dom * particles
    own_parents = lax.dynamic_slice_in_dim(parents, first_child, particles)
    held_at = ((own_parents // particles) ^ dom) * particles + own_parents % particles
    chosen = (held_at[:, None] == jnp.arange(doms * particles)[None, :]).astype(BF16)
    inherited = jnp.einsum("cp,tpw->tcw", chosen, history_all, preferred_element_type=F32)

    per_group = ranks // GROUPS
    group = rank // per_group
    columns = mixing_weight.shape[1]
    shape = (CHUNKS, steps, each)

    mix_raw, step_raw, extra, features_all = narrow
    value_all = project_wide(1, features_all, weights[0])
    gate_all = project_wide(0, features_all, weights[0])
    squares = (extra[:, 0] + extra[:, 1])[:, :rows].reshape(*shape, 1)
    rs = lax.rsqrt(squares / features + 1e-05)
    mixing = jnp.stack(
        [
            conv(
                inherited[:, k * each : (k + 1) * each, channels:],
                mix_raw[k].reshape(steps, each, columns) * rs[k],
                mixing_kernel,
                mixing_offset,
            ).astype(BF16)
            for k in range(CHUNKS)
        ]
    )
    if columns == state_width and per_group == 2:
        moves = [(g, 2 * g) for g in range(GROUPS)]
        moves += [(GROUPS + g, 2 * g + 1) for g in range(GROUPS)]
        mine = permute(mixing, moves)
        other = swap(mine)
        b_all = jnp.where(core == 0, mine, other)
        c_all = jnp.where(core == 0, other, mine)
    else:
        every = lax.all_gather(mixing, "head", axis=3, tiled=True)
        b_all = lax.dynamic_slice_in_dim(every, group * state_width, state_width, 3)
        c_all = lax.dynamic_slice_in_dim(every, (GROUPS + group) * state_width, state_width, 3)
    size_all = jax.nn.softplus(step_raw.reshape(*shape, heads) * rs + step_offset)
    decay_all = jnp.exp(-size_all * jnp.exp(decay_log))

    c_child = jnp.swapaxes(c_all, 1, 2)
    slabs = [c_child] + [across(c_child, j) for j in range(1, doms)]
    stacked = jnp.stack(slabs)
    by_dom = jnp.stack(
        [lax.dynamic_index_in_dim(stacked, dom ^ d, 0, False) for d in range(doms)]
    )

    child_mix = by_dom.reshape(doms * particles, steps, state_width)
    child_mix = jnp.pad(child_mix, ((0, TOGETHER), (0, 0), (0, 0)))
    local = parents - first_child
    held = jnp.arange(particles)[:, None]
    low = jnp.sum((local[None, :] < held).astype(jnp.int32), axis=1)
    high = jnp.sum((local[None, :] <= held).astype(jnp.int32), axis=1)
    state_reads = owner_reads(low, high, child_mix, recurrent_state)
    state_reads = state_reads.reshape(doms, CHUNKS, each, steps, channels)

    def read_states(k):
        holder = lax.dynamic_slice_in_dim(own_parents, k * each, each) // particles
        parts = [
            lax.dynamic_index_in_dim(state_reads[:, k], dom ^ j, 0, False) for j in range(doms)
        ]
        result = parts[0]
        for j in range(1, doms):
            received = across(parts[j], j)
            result = jnp.where((holder == (dom ^ j))[:, None, None], received, result)
        return jnp.moveaxis(result, 1, 0)


    def finish(k, inherited_reads):
        part = slice(k * each, (k + 1) * each)
        y, cumulative = local_reads(
            value_all[k].reshape(steps, each, channels),
            jnp.broadcast_to(rs[k], (steps, each, LANES)),
            inherited[:, part, :channels],
            value_kernel,
            value_offset.reshape(1, -1),
            b_all[k],
            c_all[k],
            pad_lanes(size_all[k].reshape(rows, heads)),
            pad_lanes(decay_all[k].reshape(rows, heads)),
            jnp.broadcast_to(pad_lanes(skip_gain.reshape(1, -1)), (8, LANES)),
            head_width,
        )
        read = cumulative * inherited_reads.astype(F32) + y
        gated = read * silu(gate_all[k].reshape(steps, each, channels) * rs[k])
        squares = jnp.sum(gated * gated, axis=2)
        total = squares
        for r in range(1, per_group):
            turn = [(i, i - i % per_group + (i + r) % per_group) for i in range(ranks)]
            total = total + permute(squares, turn)
        square_mean = total / (per_group * channels)
        return (
            (gated * lax.rsqrt(square_mean + 1e-05)[..., None] * output_gain)
            .reshape(rows, channels)
            .astype(BF16)
        )

    def scatter(scaled):
        blocks = jnp.arange(pairs, dtype=jnp.int32) * 2
        away = project_out(blocks + 1 - core, scaled, output_weight, width)
        here = project_out(blocks + core, scaled, output_weight, width)
        both = here.astype(F32) + swap(away).astype(F32)
        both = both.astype(BF16)

        def block(d):
            return lax.dynamic_index_in_dim(both, jnp.clip(d, 0, pairs - 1), 0, False).astype(F32)

        above = below = None
        for s in range(1, pairs):
            to_down = block(z - (pairs - s))
            to_up = block(z + (pairs - s))
            if s > 1:
                to_down, to_up = to_down + above.astype(F32), to_up + below.astype(F32)
            above = down(to_down.astype(BF16), pairs - s, pairs)
            below = up(to_up.astype(BF16), 0, s)
        result = block(z) + above.astype(F32) + below.astype(F32)
        return result.astype(BF16).reshape(steps, each, width)

    reads = [read_states(k) for k in range(CHUNKS)]
    outputs, scaled = [], ()
    for k in range(CHUNKS):
        inherited_reads, _ = lax.optimization_barrier((reads[k], scaled))
        scaled = finish(k, inherited_reads)
        outputs.append(scatter(scaled))
    return jnp.concatenate(outputs, axis=1)


def solution(mesh):
    return jax.shard_map(
        body,
        mesh=mesh,
        in_specs=(
            P(None, "dom", "head"),
            P(),
            P("dom", "head", None, None),
            P("dom", None, "head"),
            P("dom", None, "head"),
            P("head"),
            P(None, None, "head"),
            P(None, "head"),
            P(None, "head"),
            P(None, "head"),
            P("head"),
            P(None, "head"),
            P("head"),
            P("head"),
            P("head"),
            P("head"),
            P("head"),
            P("head", None),
        ),
        out_specs=P(None, "dom", "head"),
        check_vma=False,
    )
```

profile of v0, /device:TPU:0, one launch (start us, length us, event | category | flops | bytes accessed | tf_op | source)
XLA Modules:
  0.0 313.2 jit_solution(1430398603428869896)
XLA Ops:
  1.8 1.4 prepare.1
  3.3 1.3 collective-permute-start
  4.6 5.6 %collective-permute-start.8 = (bf16[200,1024]{1,0:T(8,128)(2,1)S(1)}, bf16[200,1024]{1,0:T(8,128)(2,1)S(1)}, u32[]{:S(2)}, u32[]{:S(2)}) collective-permute-start(bf16[200,1024]{1,0:T(8,128)(2,1)S(1)} %get-tuple-element.86.refs_0_), channel_id=1, source_target_pairs={{0,2},{1,3},{2,4},{3,5},{4,6},{5,7},{8,10},{9,11},{10,12},{11,13},... | collective-permute-start | bytes 1228808 | tf_op jit(solution)/shard_map/ppermute | solution.py:427
  10.2 1.3 collective-permute-start.3
  11.5 5.3 %collective-permute-start.11 = (bf16[200,1024]{1,0:T(8,128)(2,1)S(1)}, bf16[200,1024]{1,0:T(8,128)(2,1)}, u32[]{:S(2)}, u32[]{:S(2)}) collective-permute-start(bf16[200,1024]{1,0:T(8,128)(2,1)S(1)} %get-tuple-element.85.refs_1_), channel_id=1, source_target_pairs={{0,2},{1,3},{2,4},{3,5},{4,6},{5,7},{8,10},{9,11},{10,12},{11,13},... | collective-permute-start | bytes 1228808 | tf_op jit(solution)/shard_map/ppermute | solution.py:427
  18.7 6.9 %split_weights.4.refs_1_ = bf16[2,8192,1024]{2,1,0:T(8,128)(2,1)} custom-call(bf16[8192,2,1024]{2,1,0:T(2,128)(2,1)} %refs_0_.7), custom_call_target="tpu_custom_call" | custom-call | flops 2147483648 | bytes 16777216 | tf_op jit(solution)/shard_map/split_weights/pallas_call | solution.py:147
  26.5 2.6 collective-permute-start.28
  30.0 7.0 %split_weights.5.refs_1_ = bf16[2,8192,1024]{2,1,0:T(8,128)(2,1)} custom-call(bf16[8192,2,1024]{2,1,0:T(2,128)(2,1)} %refs_0_.7, bf16[2,8192,1024]{2,1,0:T(8,128)(2,1)} %split_weights.4.refs_1_), custom_call_target="tpu_custom_call", output_to_operand_aliasing={{}: (1, {})} | custom-call | flops 2147483648 | bytes 16777216 | tf_op jit(solution)/shard_map/split_weights/pallas_call | solution.py:147
  37.0 1.3 collective-permute-start.1
  38.4 1.3 collective-permute-start.4
  39.7 1.4 collective-permute-start.9
  41.2 1.4 collective-permute-start.12
  42.6 7.0 %split_weights.6.refs_1_ = bf16[2,8192,1024]{2,1,0:T(8,128)(2,1)} custom-call(bf16[8192,2,1024]{2,1,0:T(2,128)(2,1)} %refs_0_.7, bf16[2,8192,1024]{2,1,0:T(8,128)(2,1)} %split_weights.5.refs_1_), custom_call_target="tpu_custom_call", output_to_operand_aliasing={{}: (1, {})} | custom-call | flops 2147483648 | bytes 16777216 | tf_op jit(solution)/shard_map/split_weights/pallas_call | solution.py:147
  51.3 6.8 %collective-permute-done.4.refs_1_ = bf16[200,1024]{1,0:T(8,128)(2,1)} collective-permute-done((bf16[200,1024]{1,0:T(8,128)(2,1)S(1)}, bf16[200,1024]{1,0:T(8,128)(2,1)}, u32[]{:S(2)}, u32[]{:S(2)}) %collective-permute-start.4) | collective-permute-done | bytes 409632 | tf_op jit(solution)/shard_map/ppermute | solution.py:427
  60.0 1.3 collective-permute-start.5
  61.3 6.8 %split_weights.7.w_ref = bf16[2,8192,1024]{2,1,0:T(8,128)(2,1)} custom-call(bf16[8192,2,1024]{2,1,0:T(2,128)(2,1)} %refs_0_.7, bf16[2,8192,1024]{2,1,0:T(8,128)(2,1)} %split_weights.6.refs_1_), custom_call_target="tpu_custom_call", output_to_operand_aliasing={{}: (1, {})} | custom-call | flops 2147483648 | bytes 16777216 | tf_op jit(solution)/shard_map/split_weights/pallas_call | solution.py:147
  71.5 1.4 collective-permute-start.10
  72.9 4.8 %collective-permute-done.2.refs_0_ = bf16[200,1024]{1,0:T(8,128)(2,1)} collective-permute-done((bf16[200,1024]{1,0:T(8,128)(2,1)}, bf16[200,1024]{1,0:T(8,128)(2,1)}, u32[]{:S(2)}, u32[]{:S(2)}) %collective-permute-start.2) | collective-permute-done | bytes 409632 | tf_op jit(solution)/shard_map/ppermute | solution.py:427
  77.7 7.7 %collective-permute-done.5.refs_1_ = bf16[200,1024]{1,0:T(8,128)(2,1)} collective-permute-done((bf16[200,1024]{1,0:T(8,128)(2,1)}, bf16[200,1024]{1,0:T(8,128)(2,1)}, u32[]{:S(2)}, u32[]{:S(2)}) %collective-permute-start.5) | collective-permute-done | bytes 409632 | tf_op jit(solution)/shard_map/ppermute | solution.py:427
  85.4 1.4 collective-permute-start.13
  88.0 3.8 %project_narrow.4 = (f32[2,192,256]{2,1,0:T(8,128)S(1)}, f32[2,192,16]{2,1,0:T(8,128)S(1)}, f32[2,8,1024]{2,1,0:T(8,128)S(1)}, bf16[8,2,200,1024]{3,2,1,0:T(8,128)(2,1)}) custom-call(s32[1]{0:T(128)} %bitcast.rank, bf16[200,1024]{1,0:T(8,128)(2,1)S(1)} %get-tuple-element.86.refs_0_, bf16[200,1024]{1,0:T(8,128)(2,1)S(1)} %get-tuple-element.85.refs_1_, ...), custom_call_target="tpu_custom_call" | custom-call | flops 427819008 | bytes 1048576 | tf_op jit(solution)/shard_map/project_narrow/pallas_call | solution.py:218
  94.0 4.0 %project_narrow.5 = (f32[2,192,256]{2,1,0:T(8,128)S(1)}, f32[2,192,16]{2,1,0:T(8,128)S(1)}, f32[2,8,1024]{2,1,0:T(8,128)S(1)}, bf16[8,2,200,1024]{3,2,1,0:T(8,128)(2,1)}) custom-call(s32[1]{0:T(128)} %bitcast.rank, bf16[200,1024]{1,0:T(8,128)(2,1)S(1)} %collective-permute-done.refs_0_, ...), custom_call_target="tpu_custom_call", output_to_operand_aliasing={{0}: (11, {}), {1}: (12, {}), {2}: (13, {}), {3}: (14, {})} | custom-call | flops 855638016 | bytes 2097152 | tf_op jit(solution)/shard_map/project_narrow/pallas_call | solution.py:218
  98.0 4.7 %project_narrow.6 = (f32[2,192,256]{2,1,0:T(8,128)S(1)}, f32[2,192,16]{2,1,0:T(8,128)S(1)}, f32[2,8,1024]{2,1,0:T(8,128)S(1)}, bf16[8,2,200,1024]{3,2,1,0:T(8,128)(2,1)}) custom-call(s32[1]{0:T(128)} %bitcast.rank, bf16[200,1024]{1,0:T(8,128)(2,1)} %collective-permute-done.1.refs_0_, ...), custom_call_target="tpu_custom_call", output_to_operand_aliasing={{0}: (11, {}), {1}: (12, {}), {2}: (13, {}), {3}: (14, {})} | custom-call | flops 855638016 | bytes 2097152 | tf_op jit(solution)/shard_map/project_narrow/pallas_call | solution.py:218
  102.8 4.3 %project_narrow.7 = (f32[2,192,256]{2,1,0:T(8,128)S(1)}, f32[2,192,16]{2,1,0:T(8,128)S(1)}, f32[2,8,1024]{2,1,0:T(8,128)S(1)}, bf16[8,2,200,1024]{3,2,1,0:T(8,128)(2,1)}) custom-call(s32[1]{0:T(128)} %bitcast.rank, bf16[200,1024]{1,0:T(8,128)(2,1)} %collective-permute-done.2.refs_0_, ...), custom_call_target="tpu_custom_call", output_to_operand_aliasing={{0}: (11, {}), {1}: (12, {}), {2}: (13, {}), {3}: (14, {})} | custom-call | flops 855638016 | bytes 2097152 | tf_op jit(solution)/shard_map/project_narrow/pallas_call | solution.py:218
  108.9 3.0 collective-permute-start.29
  111.9 13.4 %project_wide.3 = f32[2,192,1024]{2,1,0:T(8,128)S(1)} custom-call(bf16[8,2,200,1024]{3,2,1,0:T(8,128)(2,1)} %get-tuple-element.39.x_ref, bf16[2,8192,1024]{2,1,0:T(8,128)(2,1)} %split_weights.7.w_ref), custom_call_target="tpu_custom_call" | custom-call | flops 6442450944 | bytes 16777216 | tf_op jit(solution)/shard_map/project_wide/pallas_call | solution.py:181
  125.3 13.4 %project_wide.2 = f32[2,192,1024]{2,1,0:T(8,128)S(1)} custom-call(bf16[8,2,200,1024]{3,2,1,0:T(8,128)(2,1)} %get-tuple-element.39.x_ref, bf16[2,8192,1024]{2,1,0:T(8,128)(2,1)} %split_weights.7.w_ref), custom_call_target="tpu_custom_call" | custom-call | flops 6442450944 | bytes 16777216 | tf_op jit(solution)/shard_map/project_wide/pallas_call | solution.py:181
  139.6 1.5 collective-permute-done.30
  142.1 2.2 collective-permute-start.33
  145.9 5.0 %collective-permute-done.33 = bf16[2,8,24,256]{3,1,2,0:T(8,128)(2,1)S(1)} collective-permute-done((bf16[2,8,24,256]{3,1,2,0:T(8,128)(2,1)S(1)}, bf16[2,8,24,256]{3,1,2,0:T(8,128)(2,1)S(1)}, u32[]{:S(2)}, u32[]{:S(2)}) %collective-permute-start.33) | collective-permute-done | bytes 196640 | tf_op jit(solution)/shard_map/ppermute | solution.py:427
  150.9 3.3 %collective-permute-done.32 = bf16[2,8,24,256]{3,1,2,0:T(8,128)(2,1)S(1)} collective-permute-done((bf16[2,8,24,256]{3,1,2,0:T(8,128)(2,1)S(1)}, bf16[2,8,24,256]{3,1,2,0:T(8,128)(2,1)S(1)}, u32[]{:S(2)}, u32[]{:S(2)}) %collective-permute-start.32) | collective-permute-done | bytes 196640 | tf_op jit(solution)/shard_map/ppermute | solution.py:427
  154.8 12.2 %owner_reads.1 = bf16[64,24,1024]{2,1,0:T(8,128)(2,1)S(1)} custom-call(s32[16]{0:T(128)S(1)} %get-tuple-element.52.low, s32[16]{0:T(128)S(1)} %get-tuple-element.51.high, bf16[68,24,256]{2,1,0:T(8,128)(2,1)S(1)} %pad.25.c_ref, f32[16,16,64,256]{3,2,1,0:T(8,128)} %s_ref.1), custom_call_target="tpu_custom_call" | custom-call | flops 805306368 | bytes 16777216 | tf_op jit(solution)/shard_map/owner_reads/pallas_call | solution.py:278
  167.9 4.6 %collective-permute-start.34 = (bf16[8,24,1024]{2,0,1:T(8,128)(2,1)S(1)}, bf16[8,24,1024]{2,0,1:T(8,128)(2,1)S(1)}, u32[]{:S(2)}, u32[]{:S(2)}) collective-permute-start(bf16[8,24,1024]{2,0,1:T(8,128)(2,1)S(1)} %bitcast.186), channel_id=1, source_target_pairs={{0,24},{8,16},{16,8},{24,0},{1,25},{9,17},{17,9},{25,1},{2,26},{10... | collective-permute-start | bytes 1179656 | tf_op jit(solution)/shard_map/ppermute | solution.py:427
  174.0 4.4 %local_reads.3 = (f32[24,8,1024]{2,1,0:T(8,128)S(1)}, f32[24,8,1024]{2,1,0:T(8,128)S(1)}) custom-call(f32[24,8,1024]{2,1,0:T(8,128)S(1)} %get-tuple-element.80.refs_0_, f32[24,8,128]{2,1,0:T(8,128)S(1)} %broadcast_in_dim.81.refs_1_, f32[3,8,1024]{2,1,0:T(8,128)S(1)} %get-tuple-element.96.refs_2_, f32[4,1024]{1,0:T(4,128)S(1)} %copy-done.12, ...), custom_call_target="tpu_custom_call" | custom-call | flops 75497472 | bytes 2359296 | tf_op jit(solution)/shard_map/local_reads/pallas_call | solution.py:340
  178.6 4.4 %local_reads.2 = (f32[24,8,1024]{2,1,0:T(8,128)S(1)}, f32[24,8,1024]{2,1,0:T(8,128)S(1)}) custom-call(f32[24,8,1024]{2,1,0:T(8,128)S(1)} %get-tuple-element.79.refs_0_, f32[24,8,128]{2,1,0:T(8,128)S(1)} %broadcast_in_dim.75.refs_1_, f32[3,8,1024]{2,1,0:T(8,128)S(1)} %get-tuple-element.95.refs_2_, f32[4,1024]{1,0:T(4,128)S(1)} %copy-done.12, ...), custom_call_target="tpu_custom_call" | custom-call | flops 75497472 | bytes 2359296 | tf_op jit(solution)/shard_map/local_reads/pallas_call | solution.py:340
  183.2 3.0 collective-permute-start.45
  187.4 3.7 %collective-permute-done.35 = bf16[8,24,1024]{2,0,1:T(8,128)(2,1)S(1)} collective-permute-done((bf16[8,24,1024]{2,0,1:T(8,128)(2,1)S(1)}, bf16[8,24,1024]{2,0,1:T(8,128)(2,1)S(1)}, u32[]{:S(2)}, u32[]{:S(2)}) %collective-permute-start.35) | collective-permute-done | bytes 393248 | tf_op jit(solution)/shard_map/ppermute | solution.py:427
  192.0 7.5 %collective-permute-done.45 = bf16[8,24,1024]{2,0,1:T(8,128)(2,1)S(1)} collective-permute-done((bf16[8,24,1024]{2,0,1:T(8,128)(2,1)S(1)}, bf16[8,24,1024]{2,0,1:T(8,128)(2,1)S(1)}, u32[]{:S(2)}, u32[]{:S(2)}) %collective-permute-start.45) | collective-permute-done | bytes 393248 | tf_op jit(solution)/shard_map/ppermute | solution.py:427
  199.5 7.3 %collective-permute-done.46 = bf16[8,24,1024]{2,0,1:T(8,128)(2,1)S(1)} collective-permute-done((bf16[8,24,1024]{2,0,1:T(8,128)(2,1)S(1)}, bf16[8,24,1024]{2,0,1:T(8,128)(2,1)S(1)}, u32[]{:S(2)}, u32[]{:S(2)}) %collective-permute-start.46) | collective-permute-done | bytes 393248 | tf_op jit(solution)/shard_map/ppermute | solution.py:427
  207.8 5.7 %project_out.5 = bf16[4,192,1024]{2,1,0:T(8,128)(2,1)S(1)} custom-call(s32[4]{0:T(128)S(1)} %add_subtract_fusion.idx, bf16[192,1024]{1,0:T(8,128)(2,1)S(1)} %fusion.21.x_ref, bf16[1024,8192]{1,0:T(8,128)(2,1)} %w_ref.7), custom_call_target="tpu_custom_call" | custom-call | flops 1610612736 | bytes 8388608 | tf_op jit(solution)/shard_map/project_out/pallas_call | solution.py:370
  214.3 6.7 %project_out.7 = bf16[4,192,1024]{2,1,0:T(8,128)(2,1)} custom-call(s32[4]{0:T(128)S(1)} %add_subtract_fusion.idx, bf16[192,1024]{1,0:T(8,128)(2,1)S(1)} %fusion.22.x_ref, bf16[1024,8192]{1,0:T(8,128)(2,1)} %w_ref.7), custom_call_target="tpu_custom_call" | custom-call | flops 1610612736 | bytes 8388608 | tf_op jit(solution)/shard_map/project_out/pallas_call | solution.py:370
  221.0 5.7 %project_out.4 = bf16[4,192,1024]{2,1,0:T(8,128)(2,1)S(1)} custom-call(s32[4]{0:T(128)S(1)} %fusion.60.idx, bf16[192,1024]{1,0:T(8,128)(2,1)S(1)} %fusion.21.x_ref, bf16[1024,8192]{1,0:T(8,128)(2,1)} %w_ref.7), custom_call_target="tpu_custom_call" | custom-call | flops 1610612736 | bytes 8388608 | tf_op jit(solution)/shard_map/project_out/pallas_call | solution.py:370
  226.8 5.7 %project_out.6 = bf16[4,192,1024]{2,1,0:T(8,128)(2,1)S(1)} custom-call(s32[4]{0:T(128)S(1)} %fusion.60.idx, bf16[192,1024]{1,0:T(8,128)(2,1)S(1)} %fusion.22.x_ref, bf16[1024,8192]{1,0:T(8,128)(2,1)} %w_ref.7), custom_call_target="tpu_custom_call" | custom-call | flops 1610612736 | bytes 8388608 | tf_op jit(solution)/shard_map/project_out/pallas_call | solution.py:370
  232.6 2.1 add_convert_fusion.1
  235.6 1.6 collective-permute-start.39
  237.2 2.1 add_convert_fusion
  240.1 1.4 collective-permute-start.50
  241.6 12.9 %collective-permute-start.42 = (bf16[192,1024]{1,0:T(8,128)(2,1)}, bf16[192,1024]{1,0:T(8,128)(2,1)}, u32[]{:S(2)}, u32[]{:S(2)}) collective-permute-start(bf16[192,1024]{1,0:T(8,128)(2,1)} %get-tuple-element.70), channel_id=1, source_target_pairs={{0,2},{1,3},{8,10},{9,11},{16,18},{17,19},{24,26},{25,27}} | collective-permute-start | bytes 1179656 | tf_op jit(solution)/shard_map/ppermute | solution.py:427
  254.5 1.9 fusion.10
  256.4 1.4 collective-permute-start.40
  257.8 2.1 collective-permute-start.53
  259.9 1.9 fusion.4
  261.8 1.4 collective-permute-start.51
  263.5 2.3 fusion.11
  265.9 11.3 %collective-permute-start.43 = (bf16[192,1024]{1,0:T(8,128)(2,1)}, bf16[192,1024]{1,0:T(8,128)(2,1)}, u32[]{:S(2)}, u32[]{:S(2)}) collective-permute-start(bf16[192,1024]{1,0:T(8,128)(2,1)} %get-tuple-element.68), channel_id=1, source_target_pairs={{0,2},{1,3},{2,4},{3,5},{8,10},{9,11},{10,12},{11,13},{16,18},{17,... | collective-permute-start | bytes 1179656 | tf_op jit(solution)/shard_map/ppermute | solution.py:427
  277.1 2.3 fusion.5
  279.4 6.1 %collective-permute-start.54 = (bf16[192,1024]{1,0:T(8,128)(2,1)}, bf16[192,1024]{1,0:T(8,128)(2,1)}, u32[]{:S(2)}, u32[]{:S(2)}) collective-permute-start(bf16[192,1024]{1,0:T(8,128)(2,1)} %get-tuple-element.72), channel_id=1, source_target_pairs={{0,2},{1,3},{2,4},{3,5},{8,10},{9,11},{10,12},{11,13},{16,18},{17,... | collective-permute-start | bytes 1179656 | tf_op jit(solution)/shard_map/ppermute | solution.py:427
  286.8 1.9 fusion.9
  288.7 6.1 %collective-permute-start.44 = (bf16[192,1024]{1,0:T(8,128)(2,1)}, bf16[192,1024]{1,0:T(8,128)(2,1)}, u32[]{:S(2)}, u32[]{:S(2)}) collective-permute-start(bf16[192,1024]{1,0:T(8,128)(2,1)} %fusion.9), channel_id=1, source_target_pairs={{0,2},{1,3},{2,4},{3,5},{4,6},{5,7},{8,10},{9,11},{10,12},{11,13},... | collective-permute-start | bytes 1179656 | tf_op jit(solution)/shard_map/ppermute | solution.py:427
  296.1 1.9 fusion.3
  297.9 5.3 %collective-permute-start.55 = (bf16[192,1024]{1,0:T(8,128)(2,1)}, bf16[192,1024]{1,0:T(8,128)(2,1)}, u32[]{:S(2)}, u32[]{:S(2)}) collective-permute-start(bf16[192,1024]{1,0:T(8,128)(2,1)} %fusion.3), channel_id=1, source_target_pairs={{0,2},{1,3},{2,4},{3,5},{4,6},{5,7},{8,10},{9,11},{10,12},{11,13},... | collective-permute-start | bytes 1179656 | tf_op jit(solution)/shard_map/ppermute | solution.py:427
  304.4 3.4 %collective-permute-done.52 = bf16[192,1024]{1,0:T(8,128)(2,1)} collective-permute-done((bf16[192,1024]{1,0:T(8,128)(2,1)}, bf16[192,1024]{1,0:T(8,128)(2,1)}, u32[]{:S(2)}, u32[]{:S(2)}) %collective-permute-start.52) | collective-permute-done | bytes 393248 | tf_op jit(solution)/shard_map/ppermute | solution.py:427
  307.8 3.1 collective-permute-done.55
  310.9 1.3 fusion.24
  (240 shorter events, 34.7 us)
Async XLA Ops:
  3.3 15.3 %collective-permute-start = (bf16[200,1024]{1,0:T(8,128)(2,1)S(1)}, bf16[200,1024]{1,0:T(8,128)(2,1)S(1)}, u32[]{:S(2)}, u32[]{:S(2)}) collective-permute-start(bf16[200,1024]{1,0:T(8,128)(2,1)S(1)} %get-tuple-element.86.refs_0_), channel_id=1, source_target_pairs={{2,0},{3,1},{4,2},{5,3},{6,4},{7,5},{10,8},{11,9},{12,10},{13,11},... | collective-permute-start | bytes 1228808 | tf_op jit(solution)/shard_map/ppermute | solution.py:427
  4.6 24.5 %collective-permute-start.8 = (bf16[200,1024]{1,0:T(8,128)(2,1)S(1)}, bf16[200,1024]{1,0:T(8,128)(2,1)S(1)}, u32[]{:S(2)}, u32[]{:S(2)}) collective-permute-start(bf16[200,1024]{1,0:T(8,128)(2,1)S(1)} %get-tuple-element.86.refs_0_), channel_id=1, source_target_pairs={{0,2},{1,3},{2,4},{3,5},{4,6},{5,7},{8,10},{9,11},{10,12},{11,13},... | collective-permute-start | bytes 1228808 | tf_op jit(solution)/shard_map/ppermute | solution.py:427
  10.2 16.3 %collective-permute-start.3 = (bf16[200,1024]{1,0:T(8,128)(2,1)S(1)}, bf16[200,1024]{1,0:T(8,128)(2,1)S(1)}, u32[]{:S(2)}, u32[]{:S(2)}) collective-permute-start(bf16[200,1024]{1,0:T(8,128)(2,1)S(1)} %get-tuple-element.85.refs_1_), channel_id=1, source_target_pairs={{2,0},{3,1},{4,2},{5,3},{6,4},{7,5},{10,8},{11,9},{12,10},{13,11},... | collective-permute-start | bytes 1228808 | tf_op jit(solution)/shard_map/ppermute | solution.py:427
  11.5 18.1 %collective-permute-start.11 = (bf16[200,1024]{1,0:T(8,128)(2,1)S(1)}, bf16[200,1024]{1,0:T(8,128)(2,1)}, u32[]{:S(2)}, u32[]{:S(2)}) collective-permute-start(bf16[200,1024]{1,0:T(8,128)(2,1)S(1)} %get-tuple-element.85.refs_1_), channel_id=1, source_target_pairs={{0,2},{1,3},{2,4},{3,5},{4,6},{5,7},{8,10},{9,11},{10,12},{11,13},... | collective-permute-start | bytes 1228808 | tf_op jit(solution)/shard_map/ppermute | solution.py:427
  16.8 20.2 %collective-permute-start.24 = (bf16[200,1024]{1,0:T(8,128)(2,1)S(1)}, bf16[200,1024]{1,0:T(8,128)(2,1)S(1)}, u32[]{:S(2)}, u32[]{:S(2)}) collective-permute-start(bf16[200,1024]{1,0:T(8,128)(2,1)S(1)} %get-tuple-element.86.refs_0_), channel_id=1, source_target_pairs={{0,1},{1,0},{2,3},{3,2},{4,5},{5,4},{6,7},{7,6},{8,9},{9,8},{10,11... | collective-permute-start | bytes 1228808 | tf_op jit(solution)/shard_map/ppermute | solution.py:427
  18.5 19.8 %collective-permute-start.25 = (bf16[200,1024]{1,0:T(8,128)(2,1)S(1)}, bf16[200,1024]{1,0:T(8,128)(2,1)S(1)}, u32[]{:S(2)}, u32[]{:S(2)}) collective-permute-start(bf16[200,1024]{1,0:T(8,128)(2,1)S(1)} %get-tuple-element.85.refs_1_), channel_id=1, source_target_pairs={{0,1},{1,0},{2,3},{3,2},{4,5},{5,4},{6,7},{7,6},{8,9},{9,8},{10,11... | collective-permute-start | bytes 1228808 | tf_op jit(solution)/shard_map/ppermute | solution.py:427
  26.5 24.9 %copy-start.2 = (bf16[200,1024]{1,0:T(8,128)(2,1)}, bf16[200,1024]{1,0:T(8,128)(2,1)S(1)}, u32[]{:S(2)}) copy-start(bf16[200,1024]{1,0:T(8,128)(2,1)S(1)} %collective-permute-done.3.refs_1_) | copy-start | bytes 1228804
  26.5 11.9 %collective-permute-start.28 = (bf16[3,16,1280]{2,1,0:T(8,128)(2,1)S(1)}, bf16[3,16,1280]{2,1,0:T(8,128)(2,1)S(1)}, u32[]{:S(2)}, u32[]{:S(2)}) collective-permute-start(bf16[3,16,1280]{2,1,0:T(8,128)(2,1)S(1)} %pad_maximum_fusion.6), channel_id=1, source_target_pairs={{0,24},{8,16},{16,8},{24,0},{1,25},{9,17},{17,9},{25,1},{2,26},{10... | collective-permute-start | bytes 368648 | tf_op jit(solution)/shard_map/ppermute | solution.py:427
  29.1 10.6 %collective-permute-start.27 = (bf16[3,16,1280]{2,1,0:T(8,128)(2,1)S(1)}, bf16[3,16,1280]{2,1,0:T(8,128)(2,1)S(1)}, u32[]{:S(2)}, u32[]{:S(2)}) collective-permute-start(bf16[3,16,1280]{2,1,0:T(8,128)(2,1)S(1)} %pad_maximum_fusion.6), channel_id=1, source_target_pairs={{0,16},{8,24},{16,0},{24,8},{1,17},{9,25},{17,1},{25,9},{2,18},{10... | collective-permute-start | bytes 368648 | tf_op jit(solution)/shard_map/ppermute | solution.py:427
  29.6 11.6 %collective-permute-start.26 = (bf16[3,16,1280]{2,1,0:T(8,128)(2,1)S(1)}, bf16[3,16,1280]{2,1,0:T(8,128)(2,1)S(1)}, u32[]{:S(2)}, u32[]{:S(2)}) collective-permute-start(bf16[3,16,1280]{2,1,0:T(8,128)(2,1)S(1)} %pad_maximum_fusion.6), channel_id=1, source_target_pairs={{0,8},{8,0},{16,24},{24,16},{1,9},{9,1},{17,25},{25,17},{2,10},{10... | collective-permute-start | bytes 368648 | tf_op jit(solution)/shard_map/ppermute | solution.py:427
  37.0 14.3 %collective-permute-start.1 = (bf16[200,1024]{1,0:T(8,128)(2,1)S(1)}, bf16[200,1024]{1,0:T(8,128)(2,1)}, u32[]{:S(2)}, u32[]{:S(2)}) collective-permute-start(bf16[200,1024]{1,0:T(8,128)(2,1)S(1)} %collective-permute-done.refs_0_), channel_id=1, source_target_pairs={{2,0},{3,1},{4,2},{5,3},{10,8},{11,9},{12,10},{13,11},{18,16},{19,... | collective-permute-start | bytes 1228808 | tf_op jit(solution)/shard_map/ppermute | solution.py:427
  38.3 21.7 %collective-permute-start.20 = (bf16[200,1024]{1,0:T(8,128)(2,1)S(1)}, bf16[200,1024]{1,0:T(8,128)(2,1)S(1)}, u32[]{:S(2)}, u32[]{:S(2)}) collective-permute-start(bf16[200,1024]{1,0:T(8,128)(2,1)S(1)} %collective-permute-done.refs_0_), channel_id=1, source_target_pairs={{0,1},{1,0},{2,3},{3,2},{4,5},{5,4},{6,7},{7,6},{8,9},{9,8},{10,11... | collective-permute-start | bytes 1228808 | tf_op jit(solution)/shard_map/ppermute | solution.py:427
  38.4 19.7 %collective-permute-start.4 = (bf16[200,1024]{1,0:T(8,128)(2,1)S(1)}, bf16[200,1024]{1,0:T(8,128)(2,1)}, u32[]{:S(2)}, u32[]{:S(2)}) collective-permute-start(bf16[200,1024]{1,0:T(8,128)(2,1)S(1)} %collective-permute-done.3.refs_1_), channel_id=1, source_target_pairs={{2,0},{3,1},{4,2},{5,3},{10,8},{11,9},{12,10},{13,11},{18,16},{19,... | collective-permute-start | bytes 1228808 | tf_op jit(solution)/shard_map/ppermute | solution.py:427
  39.7 18.4 %collective-permute-start.9 = (bf16[200,1024]{1,0:T(8,128)(2,1)S(1)}, bf16[200,1024]{1,0:T(8,128)(2,1)}, u32[]{:S(2)}, u32[]{:S(2)}) collective-permute-start(bf16[200,1024]{1,0:T(8,128)(2,1)S(1)} %collective-permute-done.8.refs_4_), channel_id=1, source_target_pairs={{2,4},{3,5},{4,6},{5,7},{10,12},{11,13},{12,14},{13,15},{18,20},{1... | collective-permute-start | bytes 1228808 | tf_op jit(solution)/shard_map/ppermute | solution.py:427
  41.2 17.5 %collective-permute-start.12 = (bf16[200,1024]{1,0:T(8,128)(2,1)}, bf16[200,1024]{1,0:T(8,128)(2,1)}, u32[]{:S(2)}, u32[]{:S(2)}) collective-permute-start(bf16[200,1024]{1,0:T(8,128)(2,1)} %collective-permute-done.11.refs_5_), channel_id=1, source_target_pairs={{2,4},{3,5},{4,6},{5,7},{10,12},{11,13},{12,14},{13,15},{18,20},{1... | collective-permute-start | bytes 1228808 | tf_op jit(solution)/shard_map/ppermute | solution.py:427
  50.1 18.0 %copy-start.30 = (f32[4,256]{1,0:T(4,128)S(1)}, f32[4,256]{1,0:T(4,128)}, u32[]{:S(2)}) copy-start(f32[4,256]{1,0:T(4,128)} %param.29) | copy-start | bytes 12292
  50.1 36.7 %copy-start.48 = (f32[16]{0:T(128)S(1)}, f32[16]{0:T(128)}, u32[]{:S(2)}) copy-start(f32[16]{0:T(128)} %param.33) | copy-start | bytes 196
  50.1 37.2 %copy-start.49 = (f32[16]{0:T(128)S(1)}, f32[16]{0:T(128)}, u32[]{:S(2)}) copy-start(f32[16]{0:T(128)} %param.32) | copy-start | bytes 196
  50.1 37.9 %copy-start = (bf16[8192,16]{0,1:T(8,128)(2,1)S(1)}, bf16[8192,16]{0,1:T(8,128)(2,1)}, u32[]{:S(2)}) copy-start(bf16[8192,16]{0,1:T(8,128)(2,1)} %param.26) | copy-start | bytes 786436
  51.3 17.3 %collective-permute-start.21 = (bf16[200,1024]{1,0:T(8,128)(2,1)S(1)}, bf16[200,1024]{1,0:T(8,128)(2,1)S(1)}, u32[]{:S(2)}, u32[]{:S(2)}) collective-permute-start(bf16[200,1024]{1,0:T(8,128)(2,1)S(1)} %collective-permute-done.3.refs_1_), channel_id=1, source_target_pairs={{0,1},{1,0},{2,3},{3,2},{4,5},{5,4},{6,7},{7,6},{8,9},{9,8},{10,11... | collective-permute-start | bytes 1228808 | tf_op jit(solution)/shard_map/ppermute | solution.py:427
  58.1 11.3 %collective-permute-start.22 = (bf16[200,1024]{1,0:T(8,128)(2,1)S(1)}, bf16[200,1024]{1,0:T(8,128)(2,1)S(1)}, u32[]{:S(2)}, u32[]{:S(2)}) collective-permute-start(bf16[200,1024]{1,0:T(8,128)(2,1)S(1)} %collective-permute-done.8.refs_4_), channel_id=1, source_target_pairs={{0,1},{1,0},{2,3},{3,2},{4,5},{5,4},{6,7},{7,6},{8,9},{9,8},{10,11... | collective-permute-start | bytes 1228808 | tf_op jit(solution)/shard_map/ppermute | solution.py:427
  58.1 12.6 %collective-permute-start.23 = (bf16[200,1024]{1,0:T(8,128)(2,1)}, bf16[200,1024]{1,0:T(8,128)(2,1)S(1)}, u32[]{:S(2)}, u32[]{:S(2)}) collective-permute-start(bf16[200,1024]{1,0:T(8,128)(2,1)} %collective-permute-done.11.refs_5_), channel_id=1, source_target_pairs={{0,1},{1,0},{2,3},{3,2},{4,5},{5,4},{6,7},{7,6},{8,9},{9,8},{10,11... | collective-permute-start | bytes 1228808 | tf_op jit(solution)/shard_map/ppermute | solution.py:427
  58.7 19.1 %collective-permute-start.2 = (bf16[200,1024]{1,0:T(8,128)(2,1)}, bf16[200,1024]{1,0:T(8,128)(2,1)}, u32[]{:S(2)}, u32[]{:S(2)}) collective-permute-start(bf16[200,1024]{1,0:T(8,128)(2,1)} %collective-permute-done.1.refs_0_), channel_id=1, source_target_pairs={{2,0},{3,1},{10,8},{11,9},{18,16},{19,17},{26,24},{27,25}} | collective-permute-start | bytes 1228808 | tf_op jit(solution)/shard_map/ppermute | solution.py:427
  60.0 25.4 %collective-permute-start.5 = (bf16[200,1024]{1,0:T(8,128)(2,1)}, bf16[200,1024]{1,0:T(8,128)(2,1)}, u32[]{:S(2)}, u32[]{:S(2)}) collective-permute-start(bf16[200,1024]{1,0:T(8,128)(2,1)} %collective-permute-done.4.refs_1_), channel_id=1, source_target_pairs={{2,0},{3,1},{10,8},{11,9},{18,16},{19,17},{26,24},{27,25}} | collective-permute-start | bytes 1228808 | tf_op jit(solution)/shard_map/ppermute | solution.py:427
  69.4 23.3 %collective-permute-start.16 = (bf16[200,1024]{1,0:T(8,128)(2,1)}, bf16[200,1024]{1,0:T(8,128)(2,1)}, u32[]{:S(2)}, u32[]{:S(2)}) collective-permute-start(bf16[200,1024]{1,0:T(8,128)(2,1)} %collective-permute-done.1.refs_0_), channel_id=1, source_target_pairs={{0,1},{1,0},{2,3},{3,2},{4,5},{5,4},{6,7},{7,6},{8,9},{9,8},{10,11... | collective-permute-start | bytes 1228808 | tf_op jit(solution)/shard_map/ppermute | solution.py:427
  70.2 22.6 %collective-permute-start.17 = (bf16[200,1024]{1,0:T(8,128)(2,1)}, bf16[200,1024]{1,0:T(8,128)(2,1)}, u32[]{:S(2)}, u32[]{:S(2)}) collective-permute-start(bf16[200,1024]{1,0:T(8,128)(2,1)} %collective-permute-done.4.refs_1_), channel_id=1, source_target_pairs={{0,1},{1,0},{2,3},{3,2},{4,5},{5,4},{6,7},{7,6},{8,9},{9,8},{10,11... | collective-permute-start | bytes 1228808 | tf_op jit(solution)/shard_map/ppermute | solution.py:427
  71.5 20.7 %collective-permute-start.10 = (bf16[200,1024]{1,0:T(8,128)(2,1)}, bf16[200,1024]{1,0:T(8,128)(2,1)}, u32[]{:S(2)}, u32[]{:S(2)}) collective-permute-start(bf16[200,1024]{1,0:T(8,128)(2,1)} %collective-permute-done.9.refs_4_), channel_id=1, source_target_pairs={{4,6},{5,7},{12,14},{13,15},{20,22},{21,23},{28,30},{29,31}} | collective-permute-start | bytes 1228808 | tf_op jit(solution)/shard_map/ppermute | solution.py:427
  77.7 15.5 %collective-permute-start.18 = (bf16[200,1024]{1,0:T(8,128)(2,1)}, bf16[200,1024]{1,0:T(8,128)(2,1)}, u32[]{:S(2)}, u32[]{:S(2)}) collective-permute-start(bf16[200,1024]{1,0:T(8,128)(2,1)} %collective-permute-done.9.refs_4_), channel_id=1, source_target_pairs={{0,1},{1,0},{2,3},{3,2},{4,5},{5,4},{6,7},{7,6},{8,9},{9,8},{10,11... | collective-permute-start | bytes 1228808 | tf_op jit(solution)/shard_map/ppermute | solution.py:427
  85.4 6.9 %collective-permute-start.13 = (bf16[200,1024]{1,0:T(8,128)(2,1)}, bf16[200,1024]{1,0:T(8,128)(2,1)}, u32[]{:S(2)}, u32[]{:S(2)}) collective-permute-start(bf16[200,1024]{1,0:T(8,128)(2,1)} %collective-permute-done.12.refs_5_), channel_id=1, source_target_pairs={{4,6},{5,7},{12,14},{13,15},{20,22},{21,23},{28,30},{29,31}} | collective-permute-start | bytes 1228808 | tf_op jit(solution)/shard_map/ppermute | solution.py:427
  92.2 5.8 %collective-permute-start.19 = (bf16[200,1024]{1,0:T(8,128)(2,1)}, bf16[200,1024]{1,0:T(8,128)(2,1)S(1)}, u32[]{:S(2)}, u32[]{:S(2)}) collective-permute-start(bf16[200,1024]{1,0:T(8,128)(2,1)} %collective-permute-done.12.refs_5_), channel_id=1, source_target_pairs={{0,1},{1,0},{2,3},{3,2},{4,5},{5,4},{6,7},{7,6},{8,9},{9,8},{10,11... | collective-permute-start | bytes 1228808 | tf_op jit(solution)/shard_map/ppermute | solution.py:427
  92.3 10.5 %collective-permute-start.6 = (bf16[200,1024]{1,0:T(8,128)(2,1)}, bf16[200,1024]{1,0:T(8,128)(2,1)S(1)}, u32[]{:S(2)}, u32[]{:S(2)}) collective-permute-start(bf16[200,1024]{1,0:T(8,128)(2,1)} %collective-permute-done.2.refs_0_), channel_id=1, source_target_pairs={{0,1},{1,0},{2,3},{3,2},{4,5},{5,4},{6,7},{7,6},{8,9},{9,8},{10,11... | collective-permute-start | bytes 1228808 | tf_op jit(solution)/shard_map/ppermute | solution.py:427
  92.8 10.0 %collective-permute-start.7 = (bf16[200,1024]{1,0:T(8,128)(2,1)}, bf16[200,1024]{1,0:T(8,128)(2,1)S(1)}, u32[]{:S(2)}, u32[]{:S(2)}) collective-permute-start(bf16[200,1024]{1,0:T(8,128)(2,1)} %collective-permute-done.5.refs_1_), channel_id=1, source_target_pairs={{0,1},{1,0},{2,3},{3,2},{4,5},{5,4},{6,7},{7,6},{8,9},{9,8},{10,11... | collective-permute-start | bytes 1228808 | tf_op jit(solution)/shard_map/ppermute | solution.py:427
  92.8 9.9 %collective-permute-start.14 = (bf16[200,1024]{1,0:T(8,128)(2,1)}, bf16[200,1024]{1,0:T(8,128)(2,1)S(1)}, u32[]{:S(2)}, u32[]{:S(2)}) collective-permute-start(bf16[200,1024]{1,0:T(8,128)(2,1)} %collective-permute-done.10.refs_4_), channel_id=1, source_target_pairs={{0,1},{1,0},{2,3},{3,2},{4,5},{5,4},{6,7},{7,6},{8,9},{9,8},{10,11... | collective-permute-start | bytes 1228808 | tf_op jit(solution)/shard_map/ppermute | solution.py:427
  93.3 9.5 %collective-permute-start.15 = (bf16[200,1024]{1,0:T(8,128)(2,1)}, bf16[200,1024]{1,0:T(8,128)(2,1)S(1)}, u32[]{:S(2)}, u32[]{:S(2)}) collective-permute-start(bf16[200,1024]{1,0:T(8,128)(2,1)} %collective-permute-done.13.refs_5_), channel_id=1, source_target_pairs={{0,1},{1,0},{2,3},{3,2},{4,5},{5,4},{6,7},{7,6},{8,9},{9,8},{10,11... | collective-permute-start | bytes 1228808 | tf_op jit(solution)/shard_map/ppermute | solution.py:427
  108.9 30.5 %collective-permute-start.29 = (bf16[2,24,8,256]{3,2,1,0:T(8,128)(2,1)}, bf16[2,24,8,256]{3,2,1,0:T(8,128)(2,1)}, u32[]{:S(2)}, u32[]{:S(2)}) collective-permute-start(bf16[2,24,8,256]{3,2,1,0:T(8,128)(2,1)} %pad_maximum_fusion.5), channel_id=1, source_target_pairs={{0,0},{1,2},{2,4},{3,6},{4,1},{5,3},{6,5},{7,7},{8,8},{9,10},{10,1... | collective-permute-start | bytes 589832 | tf_op jit(solution)/shard_map/ppermute | solution.py:427
  139.4 1.7 collective-permute-start.30
  142.1 8.8 %collective-permute-start.33 = (bf16[2,8,24,256]{3,1,2,0:T(8,128)(2,1)S(1)}, bf16[2,8,24,256]{3,1,2,0:T(8,128)(2,1)S(1)}, u32[]{:S(2)}, u32[]{:S(2)}) collective-permute-start(bf16[2,8,24,256]{3,1,2,0:T(8,128)(2,1)S(1)} %bitcast.181), channel_id=1, source_target_pairs={{0,24},{8,16},{16,8},{24,0},{1,25},{9,17},{17,9},{25,1},{2,26},{10... | collective-permute-start | bytes 589832 | tf_op jit(solution)/shard_map/ppermute | solution.py:427
  144.3 9.9 %collective-permute-start.32 = (bf16[2,8,24,256]{3,1,2,0:T(8,128)(2,1)S(1)}, bf16[2,8,24,256]{3,1,2,0:T(8,128)(2,1)S(1)}, u32[]{:S(2)}, u32[]{:S(2)}) collective-permute-start(bf16[2,8,24,256]{3,1,2,0:T(8,128)(2,1)S(1)} %bitcast.182), channel_id=1, source_target_pairs={{0,16},{8,24},{16,0},{24,8},{1,17},{9,25},{17,1},{25,9},{2,18},{10... | collective-permute-start | bytes 589832 | tf_op jit(solution)/shard_map/ppermute | solution.py:427
  144.8 9.4 %collective-permute-start.31 = (bf16[2,8,24,256]{3,1,2,0:T(8,128)(2,1)S(1)}, bf16[2,8,24,256]{3,1,2,0:T(8,128)(2,1)S(1)}, u32[]{:S(2)}, u32[]{:S(2)}) collective-permute-start(bf16[2,8,24,256]{3,1,2,0:T(8,128)(2,1)S(1)} %bitcast.183), channel_id=1, source_target_pairs={{0,8},{8,0},{16,24},{24,16},{1,9},{9,1},{17,25},{25,17},{2,10},{10... | collective-permute-start | bytes 589832 | tf_op jit(solution)/shard_map/ppermute | solution.py:427
  167.9 18.8 %collective-permute-start.34 = (bf16[8,24,1024]{2,0,1:T(8,128)(2,1)S(1)}, bf16[8,24,1024]{2,0,1:T(8,128)(2,1)S(1)}, u32[]{:S(2)}, u32[]{:S(2)}) collective-permute-start(bf16[8,24,1024]{2,0,1:T(8,128)(2,1)S(1)} %bitcast.186), channel_id=1, source_target_pairs={{0,24},{8,16},{16,8},{24,0},{1,25},{9,17},{17,9},{25,1},{2,26},{10... | collective-permute-start | bytes 1179656 | tf_op jit(solution)/shard_map/ppermute | solution.py:427
  172.8 18.3 %collective-permute-start.35 = (bf16[8,24,1024]{2,0,1:T(8,128)(2,1)S(1)}, bf16[8,24,1024]{2,0,1:T(8,128)(2,1)S(1)}, u32[]{:S(2)}, u32[]{:S(2)}) collective-permute-start(bf16[8,24,1024]{2,0,1:T(8,128)(2,1)S(1)} %bitcast.185), channel_id=1, source_target_pairs={{0,16},{8,24},{16,0},{24,8},{1,17},{9,25},{17,1},{25,9},{2,18},{10... | collective-permute-start | bytes 1179656 | tf_op jit(solution)/shard_map/ppermute | solution.py:427
  173.1 17.9 %collective-permute-start.36 = (bf16[8,24,1024]{2,0,1:T(8,128)(2,1)S(1)}, bf16[8,24,1024]{2,0,1:T(8,128)(2,1)S(1)}, u32[]{:S(2)}, u32[]{:S(2)}) collective-permute-start(bf16[8,24,1024]{2,0,1:T(8,128)(2,1)S(1)} %bitcast.187), channel_id=1, source_target_pairs={{0,8},{8,0},{16,24},{24,16},{1,9},{9,1},{17,25},{25,17},{2,10},{10... | collective-permute-start | bytes 1179656 | tf_op jit(solution)/shard_map/ppermute | solution.py:427
  183.2 16.2 %collective-permute-start.45 = (bf16[8,24,1024]{2,0,1:T(8,128)(2,1)S(1)}, bf16[8,24,1024]{2,0,1:T(8,128)(2,1)S(1)}, u32[]{:S(2)}, u32[]{:S(2)}) collective-permute-start(bf16[8,24,1024]{2,0,1:T(8,128)(2,1)S(1)} %bitcast.188), channel_id=1, source_target_pairs={{0,24},{8,16},{16,8},{24,0},{1,25},{9,17},{17,9},{25,1},{2,26},{10... | collective-permute-start | bytes 1179656 | tf_op jit(solution)/shard_map/ppermute | solution.py:427
  186.4 20.3 %collective-permute-start.46 = (bf16[8,24,1024]{2,0,1:T(8,128)(2,1)S(1)}, bf16[8,24,1024]{2,0,1:T(8,128)(2,1)S(1)}, u32[]{:S(2)}, u32[]{:S(2)}) collective-permute-start(bf16[8,24,1024]{2,0,1:T(8,128)(2,1)S(1)} %bitcast.189), channel_id=1, source_target_pairs={{0,16},{8,24},{16,0},{24,8},{1,17},{9,25},{17,1},{25,9},{2,18},{10... | collective-permute-start | bytes 1179656 | tf_op jit(solution)/shard_map/ppermute | solution.py:427
  186.8 20.0 %collective-permute-start.47 = (bf16[8,24,1024]{2,0,1:T(8,128)(2,1)S(1)}, bf16[8,24,1024]{2,0,1:T(8,128)(2,1)S(1)}, u32[]{:S(2)}, u32[]{:S(2)}) collective-permute-start(bf16[8,24,1024]{2,0,1:T(8,128)(2,1)S(1)} %bitcast.190), channel_id=1, source_target_pairs={{0,8},{8,0},{16,24},{24,16},{1,9},{9,1},{17,25},{25,17},{2,10},{10... | collective-permute-start | bytes 1179656 | tf_op jit(solution)/shard_map/ppermute | solution.py:427
  191.4 15.4 %copy-start.31 = (pred[8]{0:T(512)(128)(4,1)S(1)}, pred[8]{0:T(512)(128)(4,1)}, u32[]{:S(2)}) copy-start(pred[8]{0:T(512)(128)(4,1)} %get-tuple-element.115) | copy-start | bytes 28
  191.4 15.3 %copy-start.32 = (pred[8]{0:T(512)(128)(4,1)S(1)}, pred[8]{0:T(512)(128)(4,1)}, u32[]{:S(2)}) copy-start(pred[8]{0:T(512)(128)(4,1)} %get-tuple-element.117) | copy-start | bytes 28
  191.4 15.3 %copy-start.33 = (pred[8]{0:T(512)(128)(4,1)S(1)}, pred[8]{0:T(512)(128)(4,1)}, u32[]{:S(2)}) copy-start(pred[8]{0:T(512)(128)(4,1)} %get-tuple-element.118) | copy-start | bytes 28
  192.0 15.1 %collective-permute-start.37 = (f32[24,8]{1,0:T(8,128)S(1)}, f32[24,8]{1,0:T(8,128)S(1)}, u32[]{:S(2)}, u32[]{:S(2)}) collective-permute-start(f32[24,8]{1,0:T(8,128)S(1)} %get-tuple-element.55), channel_id=1, source_target_pairs={{0,1},{1,0},{2,3},{3,2},{4,5},{5,4},{6,7},{7,6},{8,9},{9,8},{10,11... | collective-permute-start | bytes 2312 | tf_op jit(solution)/shard_map/ppermute | solution.py:427
  207.8 6.3 %collective-permute-start.48 = (f32[24,8]{1,0:T(8,128)S(1)}, f32[24,8]{1,0:T(8,128)S(1)}, u32[]{:S(2)}, u32[]{:S(2)}) collective-permute-start(f32[24,8]{1,0:T(8,128)S(1)} %get-tuple-element.53), channel_id=1, source_target_pairs={{0,1},{1,0},{2,3},{3,2},{4,5},{5,4},{6,7},{7,6},{8,9},{9,8},{10,11... | collective-permute-start | bytes 2312 | tf_op jit(solution)/shard_map/ppermute | solution.py:427
  213.6 19.0 %collective-permute-start.38 = (bf16[4,192,1024]{2,1,0:T(8,128)(2,1)S(1)}, bf16[4,192,1024]{2,1,0:T(8,128)(2,1)}, u32[]{:S(2)}, u32[]{:S(2)}) collective-permute-start(bf16[4,192,1024]{2,1,0:T(8,128)(2,1)S(1)} %project_out.5), channel_id=1, source_target_pairs={{0,1},{1,0},{2,3},{3,2},{4,5},{5,4},{6,7},{7,6},{8,9},{9,8},{10,11... | collective-permute-start | bytes 4718600 | tf_op jit(solution)/shard_map/ppermute | solution.py:427
  221.0 16.2 %collective-permute-start.49 = (bf16[4,192,1024]{2,1,0:T(8,128)(2,1)}, bf16[4,192,1024]{2,1,0:T(8,128)(2,1)}, u32[]{:S(2)}, u32[]{:S(2)}) collective-permute-start(bf16[4,192,1024]{2,1,0:T(8,128)(2,1)} %project_out.7), channel_id=1, source_target_pairs={{0,1},{1,0},{2,3},{3,2},{4,5},{5,4},{6,7},{7,6},{8,9},{9,8},{10,11... | collective-permute-start | bytes 4718600 | tf_op jit(solution)/shard_map/ppermute | solution.py:427
  235.6 18.9 %collective-permute-start.39 = (bf16[192,1024]{1,0:T(8,128)(2,1)}, bf16[192,1024]{1,0:T(8,128)(2,1)}, u32[]{:S(2)}, u32[]{:S(2)}) collective-permute-start(bf16[192,1024]{1,0:T(8,128)(2,1)} %get-tuple-element.69), channel_id=1, source_target_pairs={{6,4},{7,5},{14,12},{15,13},{22,20},{23,21},{30,28},{31,29}} | collective-permute-start | bytes 1179656 | tf_op jit(solution)/shard_map/ppermute | solution.py:427
  240.1 19.7 %collective-permute-start.50 = (bf16[192,1024]{1,0:T(8,128)(2,1)}, bf16[192,1024]{1,0:T(8,128)(2,1)}, u32[]{:S(2)}, u32[]{:S(2)}) collective-permute-start(bf16[192,1024]{1,0:T(8,128)(2,1)} %get-tuple-element.73), channel_id=1, source_target_pairs={{6,4},{7,5},{14,12},{15,13},{22,20},{23,21},{30,28},{31,29}} | collective-permute-start | bytes 1179656 | tf_op jit(solution)/shard_map/ppermute | solution.py:427
  241.6 22.0 %collective-permute-start.42 = (bf16[192,1024]{1,0:T(8,128)(2,1)}, bf16[192,1024]{1,0:T(8,128)(2,1)}, u32[]{:S(2)}, u32[]{:S(2)}) collective-permute-start(bf16[192,1024]{1,0:T(8,128)(2,1)} %get-tuple-element.70), channel_id=1, source_target_pairs={{0,2},{1,3},{8,10},{9,11},{16,18},{17,19},{24,26},{25,27}} | collective-permute-start | bytes 1179656 | tf_op jit(solution)/shard_map/ppermute | solution.py:427
  256.4 7.1 %collective-permute-start.40 = (bf16[192,1024]{1,0:T(8,128)(2,1)}, bf16[192,1024]{1,0:T(8,128)(2,1)}, u32[]{:S(2)}, u32[]{:S(2)}) collective-permute-start(bf16[192,1024]{1,0:T(8,128)(2,1)} %fusion.10), channel_id=1, source_target_pairs={{4,2},{5,3},{6,4},{7,5},{12,10},{13,11},{14,12},{15,13},{20,18},{2... | collective-permute-start | bytes 1179656 | tf_op jit(solution)/shard_map/ppermute | solution.py:427
  257.8 19.3 %collective-permute-start.53 = (bf16[192,1024]{1,0:T(8,128)(2,1)S(1)}, bf16[192,1024]{1,0:T(8,128)(2,1)}, u32[]{:S(2)}, u32[]{:S(2)}) collective-permute-start(bf16[192,1024]{1,0:T(8,128)(2,1)S(1)} %get-tuple-element.74), channel_id=1, source_target_pairs={{0,2},{1,3},{8,10},{9,11},{16,18},{17,19},{24,26},{25,27}} | collective-permute-start | bytes 1179656 | tf_op jit(solution)/shard_map/ppermute | solution.py:427
  261.8 15.4 %collective-permute-start.51 = (bf16[192,1024]{1,0:T(8,128)(2,1)}, bf16[192,1024]{1,0:T(8,128)(2,1)}, u32[]{:S(2)}, u32[]{:S(2)}) collective-permute-start(bf16[192,1024]{1,0:T(8,128)(2,1)} %fusion.4), channel_id=1, source_target_pairs={{4,2},{5,3},{6,4},{7,5},{12,10},{13,11},{14,12},{15,13},{20,18},{2... | collective-permute-start | bytes 1179656 | tf_op jit(solution)/shard_map/ppermute | solution.py:427
  265.9 20.9 %collective-permute-start.43 = (bf16[192,1024]{1,0:T(8,128)(2,1)}, bf16[192,1024]{1,0:T(8,128)(2,1)}, u32[]{:S(2)}, u32[]{:S(2)}) collective-permute-start(bf16[192,1024]{1,0:T(8,128)(2,1)} %get-tuple-element.68), channel_id=1, source_target_pairs={{0,2},{1,3},{2,4},{3,5},{8,10},{9,11},{10,12},{11,13},{16,18},{17,... | collective-permute-start | bytes 1179656 | tf_op jit(solution)/shard_map/ppermute | solution.py:427
  279.4 16.6 %collective-permute-start.54 = (bf16[192,1024]{1,0:T(8,128)(2,1)}, bf16[192,1024]{1,0:T(8,128)(2,1)}, u32[]{:S(2)}, u32[]{:S(2)}) collective-permute-start(bf16[192,1024]{1,0:T(8,128)(2,1)} %get-tuple-element.72), channel_id=1, source_target_pairs={{0,2},{1,3},{2,4},{3,5},{8,10},{9,11},{10,12},{11,13},{16,18},{17,... | collective-permute-start | bytes 1179656 | tf_op jit(solution)/shard_map/ppermute | solution.py:427
  285.5 17.8 %collective-permute-start.41 = (bf16[192,1024]{1,0:T(8,128)(2,1)}, bf16[192,1024]{1,0:T(8,128)(2,1)S(1)}, u32[]{:S(2)}, u32[]{:S(2)}) collective-permute-start(bf16[192,1024]{1,0:T(8,128)(2,1)} %get-tuple-element.67), channel_id=1, source_target_pairs={{2,0},{3,1},{4,2},{5,3},{6,4},{7,5},{10,8},{11,9},{12,10},{13,11},... | collective-permute-start | bytes 1179656 | tf_op jit(solution)/shard_map/ppermute | solution.py:427
  288.7 14.6 %collective-permute-start.44 = (bf16[192,1024]{1,0:T(8,128)(2,1)}, bf16[192,1024]{1,0:T(8,128)(2,1)}, u32[]{:S(2)}, u32[]{:S(2)}) collective-permute-start(bf16[192,1024]{1,0:T(8,128)(2,1)} %fusion.9), channel_id=1, source_target_pairs={{0,2},{1,3},{2,4},{3,5},{4,6},{5,7},{8,10},{9,11},{10,12},{11,13},... | collective-permute-start | bytes 1179656 | tf_op jit(solution)/shard_map/ppermute | solution.py:427
  294.8 13.1 %collective-permute-start.52 = (bf16[192,1024]{1,0:T(8,128)(2,1)}, bf16[192,1024]{1,0:T(8,128)(2,1)}, u32[]{:S(2)}, u32[]{:S(2)}) collective-permute-start(bf16[192,1024]{1,0:T(8,128)(2,1)} %get-tuple-element.71), channel_id=1, source_target_pairs={{2,0},{3,1},{4,2},{5,3},{6,4},{7,5},{10,8},{11,9},{12,10},{13,11},... | collective-permute-start | bytes 1179656 | tf_op jit(solution)/shard_map/ppermute | solution.py:427
  297.9 13.0 %collective-permute-start.55 = (bf16[192,1024]{1,0:T(8,128)(2,1)}, bf16[192,1024]{1,0:T(8,128)(2,1)}, u32[]{:S(2)}, u32[]{:S(2)}) collective-permute-start(bf16[192,1024]{1,0:T(8,128)(2,1)} %fusion.3), channel_id=1, source_target_pairs={{0,2},{1,3},{2,4},{3,5},{4,6},{5,7},{8,10},{9,11},{10,12},{11,13},... | collective-permute-start | bytes 1179656 | tf_op jit(solution)/shard_map/ppermute | solution.py:427
  (42 other events, 238.9 us)
where the time goes:
time: 316 us; the launch traced here: 313 us
  Pallas kernels  118 us (37%)
  starting transfers between devices  98.6 us (31%)
  waiting for transfers between devices  57 us (18%)
  other arithmetic  26.1 us (8%)
  local copies, waits for them, and re-layouts  12.5 us (4%)
    ppermute x56, starting transfers between devices, permute(): return lax.ppermute(x, axis, pairs_of)  98.6 us
    ppermute x56, waiting for transfers between devices, permute(): return lax.ppermute(x, axis, pairs_of)  57 us
    pallas_call x4, Pallas kernels, split_weights(): pl.pallas_call(split_kernel, grid=(2,), in_specs=[pl.BlockSpec((block, 2,...  27.7 us
    pallas_call x2, Pallas kernels, project_wide(): pl.pallas_call(wide_kernel, grid=(blocks,), in_specs=[pl.BlockSpec((1, CH...  26.8 us
    pallas_call x4, Pallas kernels, project_out(): pl.pallas_call(out_kernel, grid_spec=grid_spec, out_shape=jax.ShapeDtypeS...  24 us
    pallas_call x4, Pallas kernels, project_narrow(): pl.pallas_call(functools.partial(narrow_kernel, len(arrays), bool(sums),...  16.8 us
    pallas_call x1, Pallas kernels, owner_reads(): pl.pallas_call(owner_kernel, grid_spec=grid_spec, out_shape=jax.ShapeDtyp...  12.2 us
    pallas_call x2, Pallas kernels, local_reads(): pl.pallas_call(functools.partial(local_kernel_entry, head_width), out_sha...  8.84 us
  transfers between devices with their start and end apart: 56, of which 15 were waited for; matrix products, arithmetic and copies ran while one was open for 9% of the time, Pallas kernels for 32%

commit v1 on v0

--- a/solution.py
+++ b/solution.py
@@ -230,35 +230,42 @@
 
 
 TOGETHER = 4
+HELD = 4
 
 
 def owner_kernel(low, high, c_ref, s_ref, o_ref):
-    p = pl.program_id(0)
-    first, last = low[p], high[p]
-    _, heads, head_width, state_width = s_ref.shape
+    held, heads, head_width, state_width = s_ref.shape
     steps = c_ref.shape[1]
     channels = heads * head_width
 
-    @pl.when(last > first)
-    def _():
-        state = s_ref[0].reshape(channels, state_width).astype(BF16)
-
-        def some(g, carry):
-            base = first + g * TOGETHER
-            c = c_ref[pl.ds(base, TOGETHER)].astype(F32)
-            c = c.reshape(TOGETHER * steps, state_width).astype(BF16)
-            r = lax.dot_general(
-                c, state, (((1,), (1,)), ((), ())), preferred_element_type=F32
-            ).reshape(TOGETHER, steps, channels)
-            for i in range(TOGETHER):
-
-                @pl.when(base + i < last)
-                def _():
-                    o_ref[base + i] = r[i].astype(BF16)
-
-            return carry
-
-        lax.fori_loop(0, (last - first + TOGETHER - 1) // TOGETHER, some, 0)
+    def one(q, carry):
+        p = pl.program_id(0) * held + q
+        first, last = low[p], high[p]
+
+        @pl.when(last > first)
+        def _():
+            state = s_ref[q].reshape(channels, state_width).astype(BF16)
+
+            def some(g, carry):
+                base = first + g * TOGETHER
+                c = c_ref[pl.ds(base, TOGETHER)].astype(F32)
+                c = c.reshape(TOGETHER * steps, state_width).astype(BF16)
+                r = lax.dot_general(
+                    c, state, (((1,), (1,)), ((), ())), preferred_element_type=F32
+                ).reshape(TOGETHER, steps, channels)
+                for i in range(TOGETHER):
+
+                    @pl.when(base + i < last)
+                    def _():
+                        o_ref[base + i] = r[i].astype(BF16)
+
+                return carry
+
+            lax.fori_loop(0, (last - first + TOGETHER - 1) // TOGETHER, some, 0)
+
+        return carry
+
+    lax.fori_loop(0, held, one, 0)
 
 
 def owner_reads(low, high, child_mix, state):
@@ -268,10 +275,10 @@
     channels = heads * head_width
     grid_spec = pltpu.PrefetchScalarGridSpec(
         num_scalar_prefetch=2,
-        grid=(particles,),
+        grid=(particles // HELD,),
         in_specs=[
             whole_spec(child_mix.shape),
-            pl.BlockSpec((1, heads, head_width, state_width), lambda p, *_: (p, 0, 0, 0)),
+            pl.BlockSpec((HELD, heads, head_width, state_width), lambda p, *_: (p, 0, 0, 0)),
         ],
         out_specs=whole_spec((children, steps, channels)),
     )

time: 316 us -> 311 us (0.984)
  Pallas kernels: 118 us -> 112 us
    pallas_call x1, Pallas kernels: 12.2 us -> 6.72 us  [owner_reads(): pl.pallas_call(owner_kernel, grid_spec=grid_spec, out_shape=jax.ShapeDtyp...]
where the time goes in v1:
time: 311 us; the launch traced here: 308 us
  Pallas kernels  112 us (36%)
  starting transfers between devices  99.3 us (32%)
  waiting for transfers between devices  57 us (18%)
  other arithmetic  26.1 us (8%)
  local copies, waits for them, and re-layouts  12.5 us (4%)
    ppermute x56, starting transfers between devices, permute(): return lax.ppermute(x, axis, pairs_of)  99.3 us
    ppermute x56, waiting for transfers between devices, permute(): return lax.ppermute(x, axis, pairs_of)  57 us
    pallas_call x4, Pallas kernels, split_weights(): pl.pallas_call(split_kernel, grid=(2,), in_specs=[pl.BlockSpec((block, 2,...  27.7 us
    pallas_call x2, Pallas kernels, project_wide(): pl.pallas_call(wide_kernel, grid=(blocks,), in_specs=[pl.BlockSpec((1, CH...  26.8 us
    pallas_call x4, Pallas kernels, project_out(): pl.pallas_call(out_kernel, grid_spec=grid_spec, out_shape=jax.ShapeDtypeS...  23.9 us
    pallas_call x4, Pallas kernels, project_narrow(): pl.pallas_call(functools.partial(narrow_kernel, len(arrays), bool(sums),...  16.8 us
    pallas_call x2, Pallas kernels, local_reads(): pl.pallas_call(functools.partial(local_kernel_entry, head_width), out_sha...  8.84 us
    convert_element_type x4, other arithmetic, scatter(): above = down(to_down.astype(BF16), pairs - s, pairs)  8.42 us
  transfers between devices with their start and end apart: 56, of which 15 were waited for; matrix products, arithmetic and copies ran while one was open for 9% of the time, Pallas kernels for 32%

profile of v1, /device:TPU:0, one launch (start us, length us, event | category | flops | bytes accessed | tf_op | source)
XLA Modules:
  0.0 308.3 jit_solution(18157883302680386741)
XLA Ops:
  1.8 1.4 prepare.1
  3.3 1.3 collective-permute-start
  4.6 5.6 %collective-permute-start.8 = (bf16[200,1024]{1,0:T(8,128)(2,1)S(1)}, bf16[200,1024]{1,0:T(8,128)(2,1)S(1)}, u32[]{:S(2)}, u32[]{:S(2)}) collective-permute-start(bf16[200,1024]{1,0:T(8,128)(2,1)S(1)} %get-tuple-element.86.refs_0_), channel_id=1, source_target_pairs={{0,2},{1,3},{2,4},{3,5},{4,6},{5,7},{8,10},{9,11},{10,12},{11,13},... | collective-permute-start | bytes 1228808 | tf_op jit(solution)/shard_map/ppermute | solution.py:434
  10.2 1.3 collective-permute-start.3
  11.5 5.3 %collective-permute-start.11 = (bf16[200,1024]{1,0:T(8,128)(2,1)S(1)}, bf16[200,1024]{1,0:T(8,128)(2,1)}, u32[]{:S(2)}, u32[]{:S(2)}) collective-permute-start(bf16[200,1024]{1,0:T(8,128)(2,1)S(1)} %get-tuple-element.85.refs_1_), channel_id=1, source_target_pairs={{0,2},{1,3},{2,4},{3,5},{4,6},{5,7},{8,10},{9,11},{10,12},{11,13},... | collective-permute-start | bytes 1228808 | tf_op jit(solution)/shard_map/ppermute | solution.py:434
  18.7 6.9 %split_weights.4.refs_1_ = bf16[2,8192,1024]{2,1,0:T(8,128)(2,1)} custom-call(bf16[8192,2,1024]{2,1,0:T(2,128)(2,1)} %refs_0_.7), custom_call_target="tpu_custom_call" | custom-call | flops 2147483648 | bytes 16777216 | tf_op jit(solution)/shard_map/split_weights/pallas_call | solution.py:147
  26.5 2.6 collective-permute-start.28
  30.0 7.0 %split_weights.5.refs_1_ = bf16[2,8192,1024]{2,1,0:T(8,128)(2,1)} custom-call(bf16[8192,2,1024]{2,1,0:T(2,128)(2,1)} %refs_0_.7, bf16[2,8192,1024]{2,1,0:T(8,128)(2,1)} %split_weights.4.refs_1_), custom_call_target="tpu_custom_call", output_to_operand_aliasing={{}: (1, {})} | custom-call | flops 2147483648 | bytes 16777216 | tf_op jit(solution)/shard_map/split_weights/pallas_call | solution.py:147
  37.0 1.3 collective-permute-start.1
  38.4 1.3 collective-permute-start.4
  39.7 1.4 collective-permute-start.9
  41.2 1.4 collective-permute-start.12
  42.6 7.0 %split_weights.6.refs_1_ = bf16[2,8192,1024]{2,1,0:T(8,128)(2,1)} custom-call(bf16[8192,2,1024]{2,1,0:T(2,128)(2,1)} %refs_0_.7, bf16[2,8192,1024]{2,1,0:T(8,128)(2,1)} %split_weights.5.refs_1_), custom_call_target="tpu_custom_call", output_to_operand_aliasing={{}: (1, {})} | custom-call | flops 2147483648 | bytes 16777216 | tf_op jit(solution)/shard_map/split_weights/pallas_call | solution.py:147
  51.3 6.8 %collective-permute-done.4.refs_1_ = bf16[200,1024]{1,0:T(8,128)(2,1)} collective-permute-done((bf16[200,1024]{1,0:T(8,128)(2,1)S(1)}, bf16[200,1024]{1,0:T(8,128)(2,1)}, u32[]{:S(2)}, u32[]{:S(2)}) %collective-permute-start.4) | collective-permute-done | bytes 409632 | tf_op jit(solution)/shard_map/ppermute | solution.py:434
  60.0 1.3 collective-permute-start.5
  61.3 6.8 %split_weights.7.w_ref = bf16[2,8192,1024]{2,1,0:T(8,128)(2,1)} custom-call(bf16[8192,2,1024]{2,1,0:T(2,128)(2,1)} %refs_0_.7, bf16[2,8192,1024]{2,1,0:T(8,128)(2,1)} %split_weights.6.refs_1_), custom_call_target="tpu_custom_call", output_to_operand_aliasing={{}: (1, {})} | custom-call | flops 2147483648 | bytes 16777216 | tf_op jit(solution)/shard_map/split_weights/pallas_call | solution.py:147
  71.5 1.4 collective-permute-start.10
  72.9 4.8 %collective-permute-done.2.refs_0_ = bf16[200,1024]{1,0:T(8,128)(2,1)} collective-permute-done((bf16[200,1024]{1,0:T(8,128)(2,1)}, bf16[200,1024]{1,0:T(8,128)(2,1)}, u32[]{:S(2)}, u32[]{:S(2)}) %collective-permute-start.2) | collective-permute-done | bytes 409632 | tf_op jit(solution)/shard_map/ppermute | solution.py:434
  77.7 7.7 %collective-permute-done.5.refs_1_ = bf16[200,1024]{1,0:T(8,128)(2,1)} collective-permute-done((bf16[200,1024]{1,0:T(8,128)(2,1)}, bf16[200,1024]{1,0:T(8,128)(2,1)}, u32[]{:S(2)}, u32[]{:S(2)}) %collective-permute-start.5) | collective-permute-done | bytes 409632 | tf_op jit(solution)/shard_map/ppermute | solution.py:434
  85.4 1.4 collective-permute-start.13
  88.0 3.8 %project_narrow.4 = (f32[2,192,256]{2,1,0:T(8,128)S(1)}, f32[2,192,16]{2,1,0:T(8,128)S(1)}, f32[2,8,1024]{2,1,0:T(8,128)S(1)}, bf16[8,2,200,1024]{3,2,1,0:T(8,128)(2,1)}) custom-call(s32[1]{0:T(128)} %bitcast.rank, bf16[200,1024]{1,0:T(8,128)(2,1)S(1)} %get-tuple-element.86.refs_0_, bf16[200,1024]{1,0:T(8,128)(2,1)S(1)} %get-tuple-element.85.refs_1_, ...), custom_call_target="tpu_custom_call" | custom-call | flops 427819008 | bytes 1048576 | tf_op jit(solution)/shard_map/project_narrow/pallas_call | solution.py:218
  94.0 4.0 %project_narrow.5 = (f32[2,192,256]{2,1,0:T(8,128)S(1)}, f32[2,192,16]{2,1,0:T(8,128)S(1)}, f32[2,8,1024]{2,1,0:T(8,128)S(1)}, bf16[8,2,200,1024]{3,2,1,0:T(8,128)(2,1)}) custom-call(s32[1]{0:T(128)} %bitcast.rank, bf16[200,1024]{1,0:T(8,128)(2,1)S(1)} %collective-permute-done.refs_0_, ...), custom_call_target="tpu_custom_call", output_to_operand_aliasing={{0}: (11, {}), {1}: (12, {}), {2}: (13, {}), {3}: (14, {})} | custom-call | flops 855638016 | bytes 2097152 | tf_op jit(solution)/shard_map/project_narrow/pallas_call | solution.py:218
  98.0 4.7 %project_narrow.6 = (f32[2,192,256]{2,1,0:T(8,128)S(1)}, f32[2,192,16]{2,1,0:T(8,128)S(1)}, f32[2,8,1024]{2,1,0:T(8,128)S(1)}, bf16[8,2,200,1024]{3,2,1,0:T(8,128)(2,1)}) custom-call(s32[1]{0:T(128)} %bitcast.rank, bf16[200,1024]{1,0:T(8,128)(2,1)} %collective-permute-done.1.refs_0_, ...), custom_call_target="tpu_custom_call", output_to_operand_aliasing={{0}: (11, {}), {1}: (12, {}), {2}: (13, {}), {3}: (14, {})} | custom-call | flops 855638016 | bytes 2097152 | tf_op jit(solution)/shard_map/project_narrow/pallas_call | solution.py:218
  102.8 4.3 %project_narrow.7 = (f32[2,192,256]{2,1,0:T(8,128)S(1)}, f32[2,192,16]{2,1,0:T(8,128)S(1)}, f32[2,8,1024]{2,1,0:T(8,128)S(1)}, bf16[8,2,200,1024]{3,2,1,0:T(8,128)(2,1)}) custom-call(s32[1]{0:T(128)} %bitcast.rank, bf16[200,1024]{1,0:T(8,128)(2,1)} %collective-permute-done.2.refs_0_, ...), custom_call_target="tpu_custom_call", output_to_operand_aliasing={{0}: (11, {}), {1}: (12, {}), {2}: (13, {}), {3}: (14, {})} | custom-call | flops 855638016 | bytes 2097152 | tf_op jit(solution)/shard_map/project_narrow/pallas_call | solution.py:218
  108.9 3.0 collective-permute-start.29
  111.9 13.4 %project_wide.3 = f32[2,192,1024]{2,1,0:T(8,128)S(1)} custom-call(bf16[8,2,200,1024]{3,2,1,0:T(8,128)(2,1)} %get-tuple-element.39.x_ref, bf16[2,8192,1024]{2,1,0:T(8,128)(2,1)} %split_weights.7.w_ref), custom_call_target="tpu_custom_call" | custom-call | flops 6442450944 | bytes 16777216 | tf_op jit(solution)/shard_map/project_wide/pallas_call | solution.py:181
  125.3 13.4 %project_wide.2 = f32[2,192,1024]{2,1,0:T(8,128)S(1)} custom-call(bf16[8,2,200,1024]{3,2,1,0:T(8,128)(2,1)} %get-tuple-element.39.x_ref, bf16[2,8192,1024]{2,1,0:T(8,128)(2,1)} %split_weights.7.w_ref), custom_call_target="tpu_custom_call" | custom-call | flops 6442450944 | bytes 16777216 | tf_op jit(solution)/shard_map/project_wide/pallas_call | solution.py:181
  139.6 1.5 collective-permute-done.30
  142.1 2.2 collective-permute-start.33
  145.9 5.0 %collective-permute-done.33 = bf16[2,8,24,256]{3,1,2,0:T(8,128)(2,1)S(1)} collective-permute-done((bf16[2,8,24,256]{3,1,2,0:T(8,128)(2,1)S(1)}, bf16[2,8,24,256]{3,1,2,0:T(8,128)(2,1)S(1)}, u32[]{:S(2)}, u32[]{:S(2)}) %collective-permute-start.33) | collective-permute-done | bytes 196640 | tf_op jit(solution)/shard_map/ppermute | solution.py:434
  150.9 3.3 %collective-permute-done.32 = bf16[2,8,24,256]{3,1,2,0:T(8,128)(2,1)S(1)} collective-permute-done((bf16[2,8,24,256]{3,1,2,0:T(8,128)(2,1)S(1)}, bf16[2,8,24,256]{3,1,2,0:T(8,128)(2,1)S(1)}, u32[]{:S(2)}, u32[]{:S(2)}) %collective-permute-start.32) | collective-permute-done | bytes 196640 | tf_op jit(solution)/shard_map/ppermute | solution.py:434
  154.8 6.7 %owner_reads.1 = bf16[64,24,1024]{2,1,0:T(8,128)(2,1)S(1)} custom-call(s32[16]{0:T(128)S(1)} %get-tuple-element.52.low, s32[16]{0:T(128)S(1)} %get-tuple-element.51.high, bf16[68,24,256]{2,1,0:T(8,128)(2,1)S(1)} %pad.25.c_ref, f32[16,16,64,256]{3,2,1,0:T(8,128)} %s_ref.1), custom_call_target="tpu_custom_call" | custom-call | flops 805306368 | bytes 16777216 | tf_op jit(solution)/shard_map/owner_reads/pallas_call | solution.py:285
  162.4 5.3 %collective-permute-start.34 = (bf16[8,24,1024]{2,0,1:T(8,128)(2,1)S(1)}, bf16[8,24,1024]{2,0,1:T(8,128)(2,1)S(1)}, u32[]{:S(2)}, u32[]{:S(2)}) collective-permute-start(bf16[8,24,1024]{2,0,1:T(8,128)(2,1)S(1)} %bitcast.186), channel_id=1, source_target_pairs={{0,24},{8,16},{16,8},{24,0},{1,25},{9,17},{17,9},{25,1},{2,26},{10... | collective-permute-start | bytes 1179656 | tf_op jit(solution)/shard_map/ppermute | solution.py:434
  169.2 4.4 %local_reads.3 = (f32[24,8,1024]{2,1,0:T(8,128)S(1)}, f32[24,8,1024]{2,1,0:T(8,128)S(1)}) custom-call(f32[24,8,1024]{2,1,0:T(8,128)S(1)} %get-tuple-element.80.refs_0_, f32[24,8,128]{2,1,0:T(8,128)S(1)} %broadcast_in_dim.81.refs_1_, f32[3,8,1024]{2,1,0:T(8,128)S(1)} %get-tuple-element.96.refs_2_, f32[4,1024]{1,0:T(4,128)S(1)} %copy-done.12, ...), custom_call_target="tpu_custom_call" | custom-call | flops 75497472 | bytes 2359296 | tf_op jit(solution)/shard_map/local_reads/pallas_call | solution.py:347
  173.8 4.4 %local_reads.2 = (f32[24,8,1024]{2,1,0:T(8,128)S(1)}, f32[24,8,1024]{2,1,0:T(8,128)S(1)}) custom-call(f32[24,8,1024]{2,1,0:T(8,128)S(1)} %get-tuple-element.79.refs_0_, f32[24,8,128]{2,1,0:T(8,128)S(1)} %broadcast_in_dim.75.refs_1_, f32[3,8,1024]{2,1,0:T(8,128)S(1)} %get-tuple-element.95.refs_2_, f32[4,1024]{1,0:T(4,128)S(1)} %copy-done.12, ...), custom_call_target="tpu_custom_call" | custom-call | flops 75497472 | bytes 2359296 | tf_op jit(solution)/shard_map/local_reads/pallas_call | solution.py:347
  178.4 3.0 collective-permute-start.45
  182.5 3.7 %collective-permute-done.35 = bf16[8,24,1024]{2,0,1:T(8,128)(2,1)S(1)} collective-permute-done((bf16[8,24,1024]{2,0,1:T(8,128)(2,1)S(1)}, bf16[8,24,1024]{2,0,1:T(8,128)(2,1)S(1)}, u32[]{:S(2)}, u32[]{:S(2)}) %collective-permute-start.35) | collective-permute-done | bytes 393248 | tf_op jit(solution)/shard_map/ppermute | solution.py:434
  187.2 7.5 %collective-permute-done.45 = bf16[8,24,1024]{2,0,1:T(8,128)(2,1)S(1)} collective-permute-done((bf16[8,24,1024]{2,0,1:T(8,128)(2,1)S(1)}, bf16[8,24,1024]{2,0,1:T(8,128)(2,1)S(1)}, u32[]{:S(2)}, u32[]{:S(2)}) %collective-permute-start.45) | collective-permute-done | bytes 393248 | tf_op jit(solution)/shard_map/ppermute | solution.py:434
  194.6 7.3 %collective-permute-done.46 = bf16[8,24,1024]{2,0,1:T(8,128)(2,1)S(1)} collective-permute-done((bf16[8,24,1024]{2,0,1:T(8,128)(2,1)S(1)}, bf16[8,24,1024]{2,0,1:T(8,128)(2,1)S(1)}, u32[]{:S(2)}, u32[]{:S(2)}) %collective-permute-start.46) | collective-permute-done | bytes 393248 | tf_op jit(solution)/shard_map/ppermute | solution.py:434
  203.0 5.7 %project_out.5 = bf16[4,192,1024]{2,1,0:T(8,128)(2,1)S(1)} custom-call(s32[4]{0:T(128)S(1)} %add_subtract_fusion.idx, bf16[192,1024]{1,0:T(8,128)(2,1)S(1)} %fusion.21.x_ref, bf16[1024,8192]{1,0:T(8,128)(2,1)} %w_ref.7), custom_call_target="tpu_custom_call" | custom-call | flops 1610612736 | bytes 8388608 | tf_op jit(solution)/shard_map/project_out/pallas_call | solution.py:377
  209.4 6.7 %project_out.7 = bf16[4,192,1024]{2,1,0:T(8,128)(2,1)} custom-call(s32[4]{0:T(128)S(1)} %add_subtract_fusion.idx, bf16[192,1024]{1,0:T(8,128)(2,1)S(1)} %fusion.22.x_ref, bf16[1024,8192]{1,0:T(8,128)(2,1)} %w_ref.7), custom_call_target="tpu_custom_call" | custom-call | flops 1610612736 | bytes 8388608 | tf_op jit(solution)/shard_map/project_out/pallas_call | solution.py:377
  216.2 5.7 %project_out.4 = bf16[4,192,1024]{2,1,0:T(8,128)(2,1)S(1)} custom-call(s32[4]{0:T(128)S(1)} %fusion.60.idx, bf16[192,1024]{1,0:T(8,128)(2,1)S(1)} %fusion.21.x_ref, bf16[1024,8192]{1,0:T(8,128)(2,1)} %w_ref.7), custom_call_target="tpu_custom_call" | custom-call | flops 1610612736 | bytes 8388608 | tf_op jit(solution)/shard_map/project_out/pallas_call | solution.py:377
  222.0 5.7 %project_out.6 = bf16[4,192,1024]{2,1,0:T(8,128)(2,1)S(1)} custom-call(s32[4]{0:T(128)S(1)} %fusion.60.idx, bf16[192,1024]{1,0:T(8,128)(2,1)S(1)} %fusion.22.x_ref, bf16[1024,8192]{1,0:T(8,128)(2,1)} %w_ref.7), custom_call_target="tpu_custom_call" | custom-call | flops 1610612736 | bytes 8388608 | tf_op jit(solution)/shard_map/project_out/pallas_call | solution.py:377
  227.7 2.1 add_convert_fusion.1
  230.7 1.6 collective-permute-start.39
  232.4 2.1 add_convert_fusion
  235.3 1.4 collective-permute-start.50
  236.7 12.9 %collective-permute-start.42 = (bf16[192,1024]{1,0:T(8,128)(2,1)}, bf16[192,1024]{1,0:T(8,128)(2,1)}, u32[]{:S(2)}, u32[]{:S(2)}) collective-permute-start(bf16[192,1024]{1,0:T(8,128)(2,1)} %get-tuple-element.70), channel_id=1, source_target_pairs={{0,2},{1,3},{8,10},{9,11},{16,18},{17,19},{24,26},{25,27}} | collective-permute-start | bytes 1179656 | tf_op jit(solution)/shard_map/ppermute | solution.py:434
  249.6 1.9 fusion.10
  251.6 1.4 collective-permute-start.40
  253.0 2.1 collective-permute-start.53
  255.0 1.9 fusion.4
  256.9 1.4 collective-permute-start.51
  258.7 2.3 fusion.11
  261.0 11.3 %collective-permute-start.43 = (bf16[192,1024]{1,0:T(8,128)(2,1)}, bf16[192,1024]{1,0:T(8,128)(2,1)}, u32[]{:S(2)}, u32[]{:S(2)}) collective-permute-start(bf16[192,1024]{1,0:T(8,128)(2,1)} %get-tuple-element.68), channel_id=1, source_target_pairs={{0,2},{1,3},{2,4},{3,5},{8,10},{9,11},{10,12},{11,13},{16,18},{17,... | collective-permute-start | bytes 1179656 | tf_op jit(solution)/shard_map/ppermute | solution.py:434
  272.3 2.3 fusion.5
  274.6 6.1 %collective-permute-start.54 = (bf16[192,1024]{1,0:T(8,128)(2,1)}, bf16[192,1024]{1,0:T(8,128)(2,1)}, u32[]{:S(2)}, u32[]{:S(2)}) collective-permute-start(bf16[192,1024]{1,0:T(8,128)(2,1)} %get-tuple-element.72), channel_id=1, source_target_pairs={{0,2},{1,3},{2,4},{3,5},{8,10},{9,11},{10,12},{11,13},{16,18},{17,... | collective-permute-start | bytes 1179656 | tf_op jit(solution)/shard_map/ppermute | solution.py:434
  281.9 1.9 fusion.9
  283.8 6.1 %collective-permute-start.44 = (bf16[192,1024]{1,0:T(8,128)(2,1)}, bf16[192,1024]{1,0:T(8,128)(2,1)}, u32[]{:S(2)}, u32[]{:S(2)}) collective-permute-start(bf16[192,1024]{1,0:T(8,128)(2,1)} %fusion.9), channel_id=1, source_target_pairs={{0,2},{1,3},{2,4},{3,5},{4,6},{5,7},{8,10},{9,11},{10,12},{11,13},... | collective-permute-start | bytes 1179656 | tf_op jit(solution)/shard_map/ppermute | solution.py:434
  291.2 1.9 fusion.3
  293.1 5.3 %collective-permute-start.55 = (bf16[192,1024]{1,0:T(8,128)(2,1)}, bf16[192,1024]{1,0:T(8,128)(2,1)}, u32[]{:S(2)}, u32[]{:S(2)}) collective-permute-start(bf16[192,1024]{1,0:T(8,128)(2,1)} %fusion.3), channel_id=1, source_target_pairs={{0,2},{1,3},{2,4},{3,5},{4,6},{5,7},{8,10},{9,11},{10,12},{11,13},... | collective-permute-start | bytes 1179656 | tf_op jit(solution)/shard_map/ppermute | solution.py:434
  299.6 3.4 %collective-permute-done.52 = bf16[192,1024]{1,0:T(8,128)(2,1)} collective-permute-done((bf16[192,1024]{1,0:T(8,128)(2,1)}, bf16[192,1024]{1,0:T(8,128)(2,1)}, u32[]{:S(2)}, u32[]{:S(2)}) %collective-permute-start.52) | collective-permute-done | bytes 393248 | tf_op jit(solution)/shard_map/ppermute | solution.py:434
  303.0 3.1 collective-permute-done.55
  306.1 1.3 fusion.24
  (240 shorter events, 34.7 us)
Async XLA Ops:
  3.3 15.3 %collective-permute-start = (bf16[200,1024]{1,0:T(8,128)(2,1)S(1)}, bf16[200,1024]{1,0:T(8,128)(2,1)S(1)}, u32[]{:S(2)}, u32[]{:S(2)}) collective-permute-start(bf16[200,1024]{1,0:T(8,128)(2,1)S(1)} %get-tuple-element.86.refs_0_), channel_id=1, source_target_pairs={{2,0},{3,1},{4,2},{5,3},{6,4},{7,5},{10,8},{11,9},{12,10},{13,11},... | collective-permute-start | bytes 1228808 | tf_op jit(solution)/shard_map/ppermute | solution.py:434
  4.6 24.5 %collective-permute-start.8 = (bf16[200,1024]{1,0:T(8,128)(2,1)S(1)}, bf16[200,1024]{1,0:T(8,128)(2,1)S(1)}, u32[]{:S(2)}, u32[]{:S(2)}) collective-permute-start(bf16[200,1024]{1,0:T(8,128)(2,1)S(1)} %get-tuple-element.86.refs_0_), channel_id=1, source_target_pairs={{0,2},{1,3},{2,4},{3,5},{4,6},{5,7},{8,10},{9,11},{10,12},{11,13},... | collective-permute-start | bytes 1228808 | tf_op jit(solution)/shard_map/ppermute | solution.py:434
  10.2 16.3 %collective-permute-start.3 = (bf16[200,1024]{1,0:T(8,128)(2,1)S(1)}, bf16[200,1024]{1,0:T(8,128)(2,1)S(1)}, u32[]{:S(2)}, u32[]{:S(2)}) collective-permute-start(bf16[200,1024]{1,0:T(8,128)(2,1)S(1)} %get-tuple-element.85.refs_1_), channel_id=1, source_target_pairs={{2,0},{3,1},{4,2},{5,3},{6,4},{7,5},{10,8},{11,9},{12,10},{13,11},... | collective-permute-start | bytes 1228808 | tf_op jit(solution)/shard_map/ppermute | solution.py:434
  11.5 18.1 %collective-permute-start.11 = (bf16[200,1024]{1,0:T(8,128)(2,1)S(1)}, bf16[200,1024]{1,0:T(8,128)(2,1)}, u32[]{:S(2)}, u32[]{:S(2)}) collective-permute-start(bf16[200,1024]{1,0:T(8,128)(2,1)S(1)} %get-tuple-element.85.refs_1_), channel_id=1, source_target_pairs={{0,2},{1,3},{2,4},{3,5},{4,6},{5,7},{8,10},{9,11},{10,12},{11,13},... | collective-permute-start | bytes 1228808 | tf_op jit(solution)/shard_map/ppermute | solution.py:434
  16.8 20.2 %collective-permute-start.24 = (bf16[200,1024]{1,0:T(8,128)(2,1)S(1)}, bf16[200,1024]{1,0:T(8,128)(2,1)S(1)}, u32[]{:S(2)}, u32[]{:S(2)}) collective-permute-start(bf16[200,1024]{1,0:T(8,128)(2,1)S(1)} %get-tuple-element.86.refs_0_), channel_id=1, source_target_pairs={{0,1},{1,0},{2,3},{3,2},{4,5},{5,4},{6,7},{7,6},{8,9},{9,8},{10,11... | collective-permute-start | bytes 1228808 | tf_op jit(solution)/shard_map/ppermute | solution.py:434
  18.5 19.8 %collective-permute-start.25 = (bf16[200,1024]{1,0:T(8,128)(2,1)S(1)}, bf16[200,1024]{1,0:T(8,128)(2,1)S(1)}, u32[]{:S(2)}, u32[]{:S(2)}) collective-permute-start(bf16[200,1024]{1,0:T(8,128)(2,1)S(1)} %get-tuple-element.85.refs_1_), channel_id=1, source_target_pairs={{0,1},{1,0},{2,3},{3,2},{4,5},{5,4},{6,7},{7,6},{8,9},{9,8},{10,11... | collective-permute-start | bytes 1228808 | tf_op jit(solution)/shard_map/ppermute | solution.py:434
  26.5 24.9 %copy-start.2 = (bf16[200,1024]{1,0:T(8,128)(2,1)}, bf16[200,1024]{1,0:T(8,128)(2,1)S(1)}, u32[]{:S(2)}) copy-start(bf16[200,1024]{1,0:T(8,128)(2,1)S(1)} %collective-permute-done.3.refs_1_) | copy-start | bytes 1228804
  26.5 11.9 %collective-permute-start.28 = (bf16[3,16,1280]{2,1,0:T(8,128)(2,1)S(1)}, bf16[3,16,1280]{2,1,0:T(8,128)(2,1)S(1)}, u32[]{:S(2)}, u32[]{:S(2)}) collective-permute-start(bf16[3,16,1280]{2,1,0:T(8,128)(2,1)S(1)} %pad_maximum_fusion.6), channel_id=1, source_target_pairs={{0,24},{8,16},{16,8},{24,0},{1,25},{9,17},{17,9},{25,1},{2,26},{10... | collective-permute-start | bytes 368648 | tf_op jit(solution)/shard_map/ppermute | solution.py:434
  29.1 10.6 %collective-permute-start.27 = (bf16[3,16,1280]{2,1,0:T(8,128)(2,1)S(1)}, bf16[3,16,1280]{2,1,0:T(8,128)(2,1)S(1)}, u32[]{:S(2)}, u32[]{:S(2)}) collective-permute-start(bf16[3,16,1280]{2,1,0:T(8,128)(2,1)S(1)} %pad_maximum_fusion.6), channel_id=1, source_target_pairs={{0,16},{8,24},{16,0},{24,8},{1,17},{9,25},{17,1},{25,9},{2,18},{10... | collective-permute-start | bytes 368648 | tf_op jit(solution)/shard_map/ppermute | solution.py:434
  29.6 11.6 %collective-permute-start.26 = (bf16[3,16,1280]{2,1,0:T(8,128)(2,1)S(1)}, bf16[3,16,1280]{2,1,0:T(8,128)(2,1)S(1)}, u32[]{:S(2)}, u32[]{:S(2)}) collective-permute-start(bf16[3,16,1280]{2,1,0:T(8,128)(2,1)S(1)} %pad_maximum_fusion.6), channel_id=1, source_target_pairs={{0,8},{8,0},{16,24},{24,16},{1,9},{9,1},{17,25},{25,17},{2,10},{10... | collective-permute-start | bytes 368648 | tf_op jit(solution)/shard_map/ppermute | solution.py:434
  37.0 14.3 %collective-permute-start.1 = (bf16[200,1024]{1,0:T(8,128)(2,1)S(1)}, bf16[200,1024]{1,0:T(8,128)(2,1)}, u32[]{:S(2)}, u32[]{:S(2)}) collective-permute-start(bf16[200,1024]{1,0:T(8,128)(2,1)S(1)} %collective-permute-done.refs_0_), channel_id=1, source_target_pairs={{2,0},{3,1},{4,2},{5,3},{10,8},{11,9},{12,10},{13,11},{18,16},{19,... | collective-permute-start | bytes 1228808 | tf_op jit(solution)/shard_map/ppermute | solution.py:434
  38.3 21.7 %collective-permute-start.20 = (bf16[200,1024]{1,0:T(8,128)(2,1)S(1)}, bf16[200,1024]{1,0:T(8,128)(2,1)S(1)}, u32[]{:S(2)}, u32[]{:S(2)}) collective-permute-start(bf16[200,1024]{1,0:T(8,128)(2,1)S(1)} %collective-permute-done.refs_0_), channel_id=1, source_target_pairs={{0,1},{1,0},{2,3},{3,2},{4,5},{5,4},{6,7},{7,6},{8,9},{9,8},{10,11... | collective-permute-start | bytes 1228808 | tf_op jit(solution)/shard_map/ppermute | solution.py:434
  38.4 19.7 %collective-permute-start.4 = (bf16[200,1024]{1,0:T(8,128)(2,1)S(1)}, bf16[200,1024]{1,0:T(8,128)(2,1)}, u32[]{:S(2)}, u32[]{:S(2)}) collective-permute-start(bf16[200,1024]{1,0:T(8,128)(2,1)S(1)} %collective-permute-done.3.refs_1_), channel_id=1, source_target_pairs={{2,0},{3,1},{4,2},{5,3},{10,8},{11,9},{12,10},{13,11},{18,16},{19,... | collective-permute-start | bytes 1228808 | tf_op jit(solution)/shard_map/ppermute | solution.py:434
  39.7 18.4 %collective-permute-start.9 = (bf16[200,1024]{1,0:T(8,128)(2,1)S(1)}, bf16[200,1024]{1,0:T(8,128)(2,1)}, u32[]{:S(2)}, u32[]{:S(2)}) collective-permute-start(bf16[200,1024]{1,0:T(8,128)(2,1)S(1)} %collective-permute-done.8.refs_4_), channel_id=1, source_target_pairs={{2,4},{3,5},{4,6},{5,7},{10,12},{11,13},{12,14},{13,15},{18,20},{1... | collective-permute-start | bytes 1228808 | tf_op jit(solution)/shard_map/ppermute | solution.py:434
  41.2 17.5 %collective-permute-start.12 = (bf16[200,1024]{1,0:T(8,128)(2,1)}, bf16[200,1024]{1,0:T(8,128)(2,1)}, u32[]{:S(2)}, u32[]{:S(2)}) collective-permute-start(bf16[200,1024]{1,0:T(8,128)(2,1)} %collective-permute-done.11.refs_5_), channel_id=1, source_target_pairs={{2,4},{3,5},{4,6},{5,7},{10,12},{11,13},{12,14},{13,15},{18,20},{1... | collective-permute-start | bytes 1228808 | tf_op jit(solution)/shard_map/ppermute | solution.py:434
  50.1 18.0 %copy-start.30 = (f32[4,256]{1,0:T(4,128)S(1)}, f32[4,256]{1,0:T(4,128)}, u32[]{:S(2)}) copy-start(f32[4,256]{1,0:T(4,128)} %param.29) | copy-start | bytes 12292
  50.1 36.7 %copy-start.48 = (f32[16]{0:T(128)S(1)}, f32[16]{0:T(128)}, u32[]{:S(2)}) copy-start(f32[16]{0:T(128)} %param.33) | copy-start | bytes 196
  50.1 37.2 %copy-start.49 = (f32[16]{0:T(128)S(1)}, f32[16]{0:T(128)}, u32[]{:S(2)}) copy-start(f32[16]{0:T(128)} %param.32) | copy-start | bytes 196
  50.1 37.9 %copy-start = (bf16[8192,16]{0,1:T(8,128)(2,1)S(1)}, bf16[8192,16]{0,1:T(8,128)(2,1)}, u32[]{:S(2)}) copy-start(bf16[8192,16]{0,1:T(8,128)(2,1)} %param.26) | copy-start | bytes 786436
  51.3 17.3 %collective-permute-start.21 = (bf16[200,1024]{1,0:T(8,128)(2,1)S(1)}, bf16[200,1024]{1,0:T(8,128)(2,1)S(1)}, u32[]{:S(2)}, u32[]{:S(2)}) collective-permute-start(bf16[200,1024]{1,0:T(8,128)(2,1)S(1)} %collective-permute-done.3.refs_1_), channel_id=1, source_target_pairs={{0,1},{1,0},{2,3},{3,2},{4,5},{5,4},{6,7},{7,6},{8,9},{9,8},{10,11... | collective-permute-start | bytes 1228808 | tf_op jit(solution)/shard_map/ppermute | solution.py:434
  58.1 11.3 %collective-permute-start.22 = (bf16[200,1024]{1,0:T(8,128)(2,1)S(1)}, bf16[200,1024]{1,0:T(8,128)(2,1)S(1)}, u32[]{:S(2)}, u32[]{:S(2)}) collective-permute-start(bf16[200,1024]{1,0:T(8,128)(2,1)S(1)} %collective-permute-done.8.refs_4_), channel_id=1, source_target_pairs={{0,1},{1,0},{2,3},{3,2},{4,5},{5,4},{6,7},{7,6},{8,9},{9,8},{10,11... | collective-permute-start | bytes 1228808 | tf_op jit(solution)/shard_map/ppermute | solution.py:434
  58.1 12.6 %collective-permute-start.23 = (bf16[200,1024]{1,0:T(8,128)(2,1)}, bf16[200,1024]{1,0:T(8,128)(2,1)S(1)}, u32[]{:S(2)}, u32[]{:S(2)}) collective-permute-start(bf16[200,1024]{1,0:T(8,128)(2,1)} %collective-permute-done.11.refs_5_), channel_id=1, source_target_pairs={{0,1},{1,0},{2,3},{3,2},{4,5},{5,4},{6,7},{7,6},{8,9},{9,8},{10,11... | collective-permute-start | bytes 1228808 | tf_op jit(solution)/shard_map/ppermute | solution.py:434
  58.7 19.1 %collective-permute-start.2 = (bf16[200,1024]{1,0:T(8,128)(2,1)}, bf16[200,1024]{1,0:T(8,128)(2,1)}, u32[]{:S(2)}, u32[]{:S(2)}) collective-permute-start(bf16[200,1024]{1,0:T(8,128)(2,1)} %collective-permute-done.1.refs_0_), channel_id=1, source_target_pairs={{2,0},{3,1},{10,8},{11,9},{18,16},{19,17},{26,24},{27,25}} | collective-permute-start | bytes 1228808 | tf_op jit(solution)/shard_map/ppermute | solution.py:434
  60.0 25.4 %collective-permute-start.5 = (bf16[200,1024]{1,0:T(8,128)(2,1)}, bf16[200,1024]{1,0:T(8,128)(2,1)}, u32[]{:S(2)}, u32[]{:S(2)}) collective-permute-start(bf16[200,1024]{1,0:T(8,128)(2,1)} %collective-permute-done.4.refs_1_), channel_id=1, source_target_pairs={{2,0},{3,1},{10,8},{11,9},{18,16},{19,17},{26,24},{27,25}} | collective-permute-start | bytes 1228808 | tf_op jit(solution)/shard_map/ppermute | solution.py:434
  69.4 23.3 %collective-permute-start.16 = (bf16[200,1024]{1,0:T(8,128)(2,1)}, bf16[200,1024]{1,0:T(8,128)(2,1)}, u32[]{:S(2)}, u32[]{:S(2)}) collective-permute-start(bf16[200,1024]{1,0:T(8,128)(2,1)} %collective-permute-done.1.refs_0_), channel_id=1, source_target_pairs={{0,1},{1,0},{2,3},{3,2},{4,5},{5,4},{6,7},{7,6},{8,9},{9,8},{10,11... | collective-permute-start | bytes 1228808 | tf_op jit(solution)/shard_map/ppermute | solution.py:434
  70.2 22.6 %collective-permute-start.17 = (bf16[200,1024]{1,0:T(8,128)(2,1)}, bf16[200,1024]{1,0:T(8,128)(2,1)}, u32[]{:S(2)}, u32[]{:S(2)}) collective-permute-start(bf16[200,1024]{1,0:T(8,128)(2,1)} %collective-permute-done.4.refs_1_), channel_id=1, source_target_pairs={{0,1},{1,0},{2,3},{3,2},{4,5},{5,4},{6,7},{7,6},{8,9},{9,8},{10,11... | collective-permute-start | bytes 1228808 | tf_op jit(solution)/shard_map/ppermute | solution.py:434
  71.5 20.7 %collective-permute-start.10 = (bf16[200,1024]{1,0:T(8,128)(2,1)}, bf16[200,1024]{1,0:T(8,128)(2,1)}, u32[]{:S(2)}, u32[]{:S(2)}) collective-permute-start(bf16[200,1024]{1,0:T(8,128)(2,1)} %collective-permute-done.9.refs_4_), channel_id=1, source_target_pairs={{4,6},{5,7},{12,14},{13,15},{20,22},{21,23},{28,30},{29,31}} | collective-permute-start | bytes 1228808 | tf_op jit(solution)/shard_map/ppermute | solution.py:434
  77.7 15.5 %collective-permute-start.18 = (bf16[200,1024]{1,0:T(8,128)(2,1)}, bf16[200,1024]{1,0:T(8,128)(2,1)}, u32[]{:S(2)}, u32[]{:S(2)}) collective-permute-start(bf16[200,1024]{1,0:T(8,128)(2,1)} %collective-permute-done.9.refs_4_), channel_id=1, source_target_pairs={{0,1},{1,0},{2,3},{3,2},{4,5},{5,4},{6,7},{7,6},{8,9},{9,8},{10,11... | collective-permute-start | bytes 1228808 | tf_op jit(solution)/shard_map/ppermute | solution.py:434
  85.4 6.9 %collective-permute-start.13 = (bf16[200,1024]{1,0:T(8,128)(2,1)}, bf16[200,1024]{1,0:T(8,128)(2,1)}, u32[]{:S(2)}, u32[]{:S(2)}) collective-permute-start(bf16[200,1024]{1,0:T(8,128)(2,1)} %collective-permute-done.12.refs_5_), channel_id=1, source_target_pairs={{4,6},{5,7},{12,14},{13,15},{20,22},{21,23},{28,30},{29,31}} | collective-permute-start | bytes 1228808 | tf_op jit(solution)/shard_map/ppermute | solution.py:434
  92.2 5.8 %collective-permute-start.19 = (bf16[200,1024]{1,0:T(8,128)(2,1)}, bf16[200,1024]{1,0:T(8,128)(2,1)S(1)}, u32[]{:S(2)}, u32[]{:S(2)}) collective-permute-start(bf16[200,1024]{1,0:T(8,128)(2,1)} %collective-permute-done.12.refs_5_), channel_id=1, source_target_pairs={{0,1},{1,0},{2,3},{3,2},{4,5},{5,4},{6,7},{7,6},{8,9},{9,8},{10,11... | collective-permute-start | bytes 1228808 | tf_op jit(solution)/shard_map/ppermute | solution.py:434
  92.3 10.5 %collective-permute-start.6 = (bf16[200,1024]{1,0:T(8,128)(2,1)}, bf16[200,1024]{1,0:T(8,128)(2,1)S(1)}, u32[]{:S(2)}, u32[]{:S(2)}) collective-permute-start(bf16[200,1024]{1,0:T(8,128)(2,1)} %collective-permute-done.2.refs_0_), channel_id=1, source_target_pairs={{0,1},{1,0},{2,3},{3,2},{4,5},{5,4},{6,7},{7,6},{8,9},{9,8},{10,11... | collective-permute-start | bytes 1228808 | tf_op jit(solution)/shard_map/ppermute | solution.py:434
  92.8 10.0 %collective-permute-start.7 = (bf16[200,1024]{1,0:T(8,128)(2,1)}, bf16[200,1024]{1,0:T(8,128)(2,1)S(1)}, u32[]{:S(2)}, u32[]{:S(2)}) collective-permute-start(bf16[200,1024]{1,0:T(8,128)(2,1)} %collective-permute-done.5.refs_1_), channel_id=1, source_target_pairs={{0,1},{1,0},{2,3},{3,2},{4,5},{5,4},{6,7},{7,6},{8,9},{9,8},{10,11... | collective-permute-start | bytes 1228808 | tf_op jit(solution)/shard_map/ppermute | solution.py:434
  92.8 9.9 %collective-permute-start.14 = (bf16[200,1024]{1,0:T(8,128)(2,1)}, bf16[200,1024]{1,0:T(8,128)(2,1)S(1)}, u32[]{:S(2)}, u32[]{:S(2)}) collective-permute-start(bf16[200,1024]{1,0:T(8,128)(2,1)} %collective-permute-done.10.refs_4_), channel_id=1, source_target_pairs={{0,1},{1,0},{2,3},{3,2},{4,5},{5,4},{6,7},{7,6},{8,9},{9,8},{10,11... | collective-permute-start | bytes 1228808 | tf_op jit(solution)/shard_map/ppermute | solution.py:434
  93.3 9.5 %collective-permute-start.15 = (bf16[200,1024]{1,0:T(8,128)(2,1)}, bf16[200,1024]{1,0:T(8,128)(2,1)S(1)}, u32[]{:S(2)}, u32[]{:S(2)}) collective-permute-start(bf16[200,1024]{1,0:T(8,128)(2,1)} %collective-permute-done.13.refs_5_), channel_id=1, source_target_pairs={{0,1},{1,0},{2,3},{3,2},{4,5},{5,4},{6,7},{7,6},{8,9},{9,8},{10,11... | collective-permute-start | bytes 1228808 | tf_op jit(solution)/shard_map/ppermute | solution.py:434
  108.9 30.5 %collective-permute-start.29 = (bf16[2,24,8,256]{3,2,1,0:T(8,128)(2,1)}, bf16[2,24,8,256]{3,2,1,0:T(8,128)(2,1)}, u32[]{:S(2)}, u32[]{:S(2)}) collective-permute-start(bf16[2,24,8,256]{3,2,1,0:T(8,128)(2,1)} %pad_maximum_fusion.5), channel_id=1, source_target_pairs={{0,0},{1,2},{2,4},{3,6},{4,1},{5,3},{6,5},{7,7},{8,8},{9,10},{10,1... | collective-permute-start | bytes 589832 | tf_op jit(solution)/shard_map/ppermute | solution.py:434
  139.4 1.7 collective-permute-start.30
  142.1 8.8 %collective-permute-start.33 = (bf16[2,8,24,256]{3,1,2,0:T(8,128)(2,1)S(1)}, bf16[2,8,24,256]{3,1,2,0:T(8,128)(2,1)S(1)}, u32[]{:S(2)}, u32[]{:S(2)}) collective-permute-start(bf16[2,8,24,256]{3,1,2,0:T(8,128)(2,1)S(1)} %bitcast.181), channel_id=1, source_target_pairs={{0,24},{8,16},{16,8},{24,0},{1,25},{9,17},{17,9},{25,1},{2,26},{10... | collective-permute-start | bytes 589832 | tf_op jit(solution)/shard_map/ppermute | solution.py:434
  144.3 9.9 %collective-permute-start.32 = (bf16[2,8,24,256]{3,1,2,0:T(8,128)(2,1)S(1)}, bf16[2,8,24,256]{3,1,2,0:T(8,128)(2,1)S(1)}, u32[]{:S(2)}, u32[]{:S(2)}) collective-permute-start(bf16[2,8,24,256]{3,1,2,0:T(8,128)(2,1)S(1)} %bitcast.182), channel_id=1, source_target_pairs={{0,16},{8,24},{16,0},{24,8},{1,17},{9,25},{17,1},{25,9},{2,18},{10... | collective-permute-start | bytes 589832 | tf_op jit(solution)/shard_map/ppermute | solution.py:434
  144.8 9.4 %collective-permute-start.31 = (bf16[2,8,24,256]{3,1,2,0:T(8,128)(2,1)S(1)}, bf16[2,8,24,256]{3,1,2,0:T(8,128)(2,1)S(1)}, u32[]{:S(2)}, u32[]{:S(2)}) collective-permute-start(bf16[2,8,24,256]{3,1,2,0:T(8,128)(2,1)S(1)} %bitcast.183), channel_id=1, source_target_pairs={{0,8},{8,0},{16,24},{24,16},{1,9},{9,1},{17,25},{25,17},{2,10},{10... | collective-permute-start | bytes 589832 | tf_op jit(solution)/shard_map/ppermute | solution.py:434
  162.4 19.5 %collective-permute-start.34 = (bf16[8,24,1024]{2,0,1:T(8,128)(2,1)S(1)}, bf16[8,24,1024]{2,0,1:T(8,128)(2,1)S(1)}, u32[]{:S(2)}, u32[]{:S(2)}) collective-permute-start(bf16[8,24,1024]{2,0,1:T(8,128)(2,1)S(1)} %bitcast.186), channel_id=1, source_target_pairs={{0,24},{8,16},{16,8},{24,0},{1,25},{9,17},{17,9},{25,1},{2,26},{10... | collective-permute-start | bytes 1179656 | tf_op jit(solution)/shard_map/ppermute | solution.py:434
  168.0 18.3 %collective-permute-start.35 = (bf16[8,24,1024]{2,0,1:T(8,128)(2,1)S(1)}, bf16[8,24,1024]{2,0,1:T(8,128)(2,1)S(1)}, u32[]{:S(2)}, u32[]{:S(2)}) collective-permute-start(bf16[8,24,1024]{2,0,1:T(8,128)(2,1)S(1)} %bitcast.185), channel_id=1, source_target_pairs={{0,16},{8,24},{16,0},{24,8},{1,17},{9,25},{17,1},{25,9},{2,18},{10... | collective-permute-start | bytes 1179656 | tf_op jit(solution)/shard_map/ppermute | solution.py:434
  168.3 17.9 %collective-permute-start.36 = (bf16[8,24,1024]{2,0,1:T(8,128)(2,1)S(1)}, bf16[8,24,1024]{2,0,1:T(8,128)(2,1)S(1)}, u32[]{:S(2)}, u32[]{:S(2)}) collective-permute-start(bf16[8,24,1024]{2,0,1:T(8,128)(2,1)S(1)} %bitcast.187), channel_id=1, source_target_pairs={{0,8},{8,0},{16,24},{24,16},{1,9},{9,1},{17,25},{25,17},{2,10},{10... | collective-permute-start | bytes 1179656 | tf_op jit(solution)/shard_map/ppermute | solution.py:434
  178.4 16.2 %collective-permute-start.45 = (bf16[8,24,1024]{2,0,1:T(8,128)(2,1)S(1)}, bf16[8,24,1024]{2,0,1:T(8,128)(2,1)S(1)}, u32[]{:S(2)}, u32[]{:S(2)}) collective-permute-start(bf16[8,24,1024]{2,0,1:T(8,128)(2,1)S(1)} %bitcast.188), channel_id=1, source_target_pairs={{0,24},{8,16},{16,8},{24,0},{1,25},{9,17},{17,9},{25,1},{2,26},{10... | collective-permute-start | bytes 1179656 | tf_op jit(solution)/shard_map/ppermute | solution.py:434
  181.6 20.3 %collective-permute-start.46 = (bf16[8,24,1024]{2,0,1:T(8,128)(2,1)S(1)}, bf16[8,24,1024]{2,0,1:T(8,128)(2,1)S(1)}, u32[]{:S(2)}, u32[]{:S(2)}) collective-permute-start(bf16[8,24,1024]{2,0,1:T(8,128)(2,1)S(1)} %bitcast.189), channel_id=1, source_target_pairs={{0,16},{8,24},{16,0},{24,8},{1,17},{9,25},{17,1},{25,9},{2,18},{10... | collective-permute-start | bytes 1179656 | tf_op jit(solution)/shard_map/ppermute | solution.py:434
  182.0 20.0 %collective-permute-start.47 = (bf16[8,24,1024]{2,0,1:T(8,128)(2,1)S(1)}, bf16[8,24,1024]{2,0,1:T(8,128)(2,1)S(1)}, u32[]{:S(2)}, u32[]{:S(2)}) collective-permute-start(bf16[8,24,1024]{2,0,1:T(8,128)(2,1)S(1)} %bitcast.190), channel_id=1, source_target_pairs={{0,8},{8,0},{16,24},{24,16},{1,9},{9,1},{17,25},{25,17},{2,10},{10... | collective-permute-start | bytes 1179656 | tf_op jit(solution)/shard_map/ppermute | solution.py:434
  186.6 15.4 %copy-start.31 = (pred[8]{0:T(512)(128)(4,1)S(1)}, pred[8]{0:T(512)(128)(4,1)}, u32[]{:S(2)}) copy-start(pred[8]{0:T(512)(128)(4,1)} %get-tuple-element.115) | copy-start | bytes 28
  186.6 15.3 %copy-start.32 = (pred[8]{0:T(512)(128)(4,1)S(1)}, pred[8]{0:T(512)(128)(4,1)}, u32[]{:S(2)}) copy-start(pred[8]{0:T(512)(128)(4,1)} %get-tuple-element.117) | copy-start | bytes 28
  186.6 15.3 %copy-start.33 = (pred[8]{0:T(512)(128)(4,1)S(1)}, pred[8]{0:T(512)(128)(4,1)}, u32[]{:S(2)}) copy-start(pred[8]{0:T(512)(128)(4,1)} %get-tuple-element.118) | copy-start | bytes 28
  187.1 15.1 %collective-permute-start.37 = (f32[24,8]{1,0:T(8,128)S(1)}, f32[24,8]{1,0:T(8,128)S(1)}, u32[]{:S(2)}, u32[]{:S(2)}) collective-permute-start(f32[24,8]{1,0:T(8,128)S(1)} %get-tuple-element.55), channel_id=1, source_target_pairs={{0,1},{1,0},{2,3},{3,2},{4,5},{5,4},{6,7},{7,6},{8,9},{9,8},{10,11... | collective-permute-start | bytes 2312 | tf_op jit(solution)/shard_map/ppermute | solution.py:434
  202.9 6.3 %collective-permute-start.48 = (f32[24,8]{1,0:T(8,128)S(1)}, f32[24,8]{1,0:T(8,128)S(1)}, u32[]{:S(2)}, u32[]{:S(2)}) collective-permute-start(f32[24,8]{1,0:T(8,128)S(1)} %get-tuple-element.53), channel_id=1, source_target_pairs={{0,1},{1,0},{2,3},{3,2},{4,5},{5,4},{6,7},{7,6},{8,9},{9,8},{10,11... | collective-permute-start | bytes 2312 | tf_op jit(solution)/shard_map/ppermute | solution.py:434
  208.7 19.0 %collective-permute-start.38 = (bf16[4,192,1024]{2,1,0:T(8,128)(2,1)S(1)}, bf16[4,192,1024]{2,1,0:T(8,128)(2,1)}, u32[]{:S(2)}, u32[]{:S(2)}) collective-permute-start(bf16[4,192,1024]{2,1,0:T(8,128)(2,1)S(1)} %project_out.5), channel_id=1, source_target_pairs={{0,1},{1,0},{2,3},{3,2},{4,5},{5,4},{6,7},{7,6},{8,9},{9,8},{10,11... | collective-permute-start | bytes 4718600 | tf_op jit(solution)/shard_map/ppermute | solution.py:434
  216.2 16.2 %collective-permute-start.49 = (bf16[4,192,1024]{2,1,0:T(8,128)(2,1)}, bf16[4,192,1024]{2,1,0:T(8,128)(2,1)}, u32[]{:S(2)}, u32[]{:S(2)}) collective-permute-start(bf16[4,192,1024]{2,1,0:T(8,128)(2,1)} %project_out.7), channel_id=1, source_target_pairs={{0,1},{1,0},{2,3},{3,2},{4,5},{5,4},{6,7},{7,6},{8,9},{9,8},{10,11... | collective-permute-start | bytes 4718600 | tf_op jit(solution)/shard_map/ppermute | solution.py:434
  230.7 18.9 %collective-permute-start.39 = (bf16[192,1024]{1,0:T(8,128)(2,1)}, bf16[192,1024]{1,0:T(8,128)(2,1)}, u32[]{:S(2)}, u32[]{:S(2)}) collective-permute-start(bf16[192,1024]{1,0:T(8,128)(2,1)} %get-tuple-element.69), channel_id=1, source_target_pairs={{6,4},{7,5},{14,12},{15,13},{22,20},{23,21},{30,28},{31,29}} | collective-permute-start | bytes 1179656 | tf_op jit(solution)/shard_map/ppermute | solution.py:434
  235.3 19.7 %collective-permute-start.50 = (bf16[192,1024]{1,0:T(8,128)(2,1)}, bf16[192,1024]{1,0:T(8,128)(2,1)}, u32[]{:S(2)}, u32[]{:S(2)}) collective-permute-start(bf16[192,1024]{1,0:T(8,128)(2,1)} %get-tuple-element.73), channel_id=1, source_target_pairs={{6,4},{7,5},{14,12},{15,13},{22,20},{23,21},{30,28},{31,29}} | collective-permute-start | bytes 1179656 | tf_op jit(solution)/shard_map/ppermute | solution.py:434
  236.7 22.0 %collective-permute-start.42 = (bf16[192,1024]{1,0:T(8,128)(2,1)}, bf16[192,1024]{1,0:T(8,128)(2,1)}, u32[]{:S(2)}, u32[]{:S(2)}) collective-permute-start(bf16[192,1024]{1,0:T(8,128)(2,1)} %get-tuple-element.70), channel_id=1, source_target_pairs={{0,2},{1,3},{8,10},{9,11},{16,18},{17,19},{24,26},{25,27}} | collective-permute-start | bytes 1179656 | tf_op jit(solution)/shard_map/ppermute | solution.py:434
  251.6 7.1 %collective-permute-start.40 = (bf16[192,1024]{1,0:T(8,128)(2,1)}, bf16[192,1024]{1,0:T(8,128)(2,1)}, u32[]{:S(2)}, u32[]{:S(2)}) collective-permute-start(bf16[192,1024]{1,0:T(8,128)(2,1)} %fusion.10), channel_id=1, source_target_pairs={{4,2},{5,3},{6,4},{7,5},{12,10},{13,11},{14,12},{15,13},{20,18},{2... | collective-permute-start | bytes 1179656 | tf_op jit(solution)/shard_map/ppermute | solution.py:434
  253.0 19.3 %collective-permute-start.53 = (bf16[192,1024]{1,0:T(8,128)(2,1)S(1)}, bf16[192,1024]{1,0:T(8,128)(2,1)}, u32[]{:S(2)}, u32[]{:S(2)}) collective-permute-start(bf16[192,1024]{1,0:T(8,128)(2,1)S(1)} %get-tuple-element.74), channel_id=1, source_target_pairs={{0,2},{1,3},{8,10},{9,11},{16,18},{17,19},{24,26},{25,27}} | collective-permute-start | bytes 1179656 | tf_op jit(solution)/shard_map/ppermute | solution.py:434
  256.9 15.4 %collective-permute-start.51 = (bf16[192,1024]{1,0:T(8,128)(2,1)}, bf16[192,1024]{1,0:T(8,128)(2,1)}, u32[]{:S(2)}, u32[]{:S(2)}) collective-permute-start(bf16[192,1024]{1,0:T(8,128)(2,1)} %fusion.4), channel_id=1, source_target_pairs={{4,2},{5,3},{6,4},{7,5},{12,10},{13,11},{14,12},{15,13},{20,18},{2... | collective-permute-start | bytes 1179656 | tf_op jit(solution)/shard_map/ppermute | solution.py:434
  261.0 20.9 %collective-permute-start.43 = (bf16[192,1024]{1,0:T(8,128)(2,1)}, bf16[192,1024]{1,0:T(8,128)(2,1)}, u32[]{:S(2)}, u32[]{:S(2)}) collective-permute-start(bf16[192,1024]{1,0:T(8,128)(2,1)} %get-tuple-element.68), channel_id=1, source_target_pairs={{0,2},{1,3},{2,4},{3,5},{8,10},{9,11},{10,12},{11,13},{16,18},{17,... | collective-permute-start | bytes 1179656 | tf_op jit(solution)/shard_map/ppermute | solution.py:434
  274.6 16.6 %collective-permute-start.54 = (bf16[192,1024]{1,0:T(8,128)(2,1)}, bf16[192,1024]{1,0:T(8,128)(2,1)}, u32[]{:S(2)}, u32[]{:S(2)}) collective-permute-start(bf16[192,1024]{1,0:T(8,128)(2,1)} %get-tuple-element.72), channel_id=1, source_target_pairs={{0,2},{1,3},{2,4},{3,5},{8,10},{9,11},{10,12},{11,13},{16,18},{17,... | collective-permute-start | bytes 1179656 | tf_op jit(solution)/shard_map/ppermute | solution.py:434
  280.6 17.8 %collective-permute-start.41 = (bf16[192,1024]{1,0:T(8,128)(2,1)}, bf16[192,1024]{1,0:T(8,128)(2,1)S(1)}, u32[]{:S(2)}, u32[]{:S(2)}) collective-permute-start(bf16[192,1024]{1,0:T(8,128)(2,1)} %get-tuple-element.67), channel_id=1, source_target_pairs={{2,0},{3,1},{4,2},{5,3},{6,4},{7,5},{10,8},{11,9},{12,10},{13,11},... | collective-permute-start | bytes 1179656 | tf_op jit(solution)/shard_map/ppermute | solution.py:434
  283.8 14.6 %collective-permute-start.44 = (bf16[192,1024]{1,0:T(8,128)(2,1)}, bf16[192,1024]{1,0:T(8,128)(2,1)}, u32[]{:S(2)}, u32[]{:S(2)}) collective-permute-start(bf16[192,1024]{1,0:T(8,128)(2,1)} %fusion.9), channel_id=1, source_target_pairs={{0,2},{1,3},{2,4},{3,5},{4,6},{5,7},{8,10},{9,11},{10,12},{11,13},... | collective-permute-start | bytes 1179656 | tf_op jit(solution)/shard_map/ppermute | solution.py:434
  289.9 13.1 %collective-permute-start.52 = (bf16[192,1024]{1,0:T(8,128)(2,1)}, bf16[192,1024]{1,0:T(8,128)(2,1)}, u32[]{:S(2)}, u32[]{:S(2)}) collective-permute-start(bf16[192,1024]{1,0:T(8,128)(2,1)} %get-tuple-element.71), channel_id=1, source_target_pairs={{2,0},{3,1},{4,2},{5,3},{6,4},{7,5},{10,8},{11,9},{12,10},{13,11},... | collective-permute-start | bytes 1179656 | tf_op jit(solution)/shard_map/ppermute | solution.py:434
  293.1 13.0 %collective-permute-start.55 = (bf16[192,1024]{1,0:T(8,128)(2,1)}, bf16[192,1024]{1,0:T(8,128)(2,1)}, u32[]{:S(2)}, u32[]{:S(2)}) collective-permute-start(bf16[192,1024]{1,0:T(8,128)(2,1)} %fusion.3), channel_id=1, source_target_pairs={{0,2},{1,3},{2,4},{3,5},{4,6},{5,7},{8,10},{9,11},{10,12},{11,13},... | collective-permute-start | bytes 1179656 | tf_op jit(solution)/shard_map/ppermute | solution.py:434
  (42 other events, 238.9 us)

commit v2 on v1

--- a/solution.py
+++ b/solution.py
@@ -582,13 +582,15 @@
         both = here.astype(F32) + swap(away).astype(F32)
         both = both.astype(BF16)
 
-        def block(d):
-            return lax.dynamic_index_in_dim(both, jnp.clip(d, 0, pairs - 1), 0, False).astype(F32)
+        both_up = lax.optimization_barrier(both)
+
+        def block(d, sums=both):
+            return lax.dynamic_index_in_dim(sums, jnp.clip(d, 0, pairs - 1), 0, False).astype(F32)
 
         above = below = None
         for s in range(1, pairs):
             to_down = block(z - (pairs - s))
-            to_up = block(z + (pairs - s))
+            to_up = block(z + (pairs - s), both_up)
             if s > 1:
                 to_down, to_up = to_down + above.astype(F32), to_up + below.astype(F32)
             above = down(to_down.astype(BF16), pairs - s, pairs)

time: 311 us -> 299 us (0.961)
  starting transfers between devices: 99.3 us -> 84.6 us
  waiting for transfers between devices: 57 us -> 70.6 us
  other arithmetic: 26.1 us -> 18.1 us
    ppermute x56, starting transfers between devices: 99.3 us -> 84.6 us  [permute(): return lax.ppermute(x, axis, pairs_of)]
    ppermute x56, waiting for transfers between devices: 57 us -> 70.6 us  [permute(): return lax.ppermute(x, axis, pairs_of)]
    convert_element_type x4, other arithmetic: 8.42 us -> 2.06 us  [scatter(): above = down(to_down.astype(BF16), pairs - s, pairs)]
  transfers between devices with their start and end apart: 56 -> 56, of which waited for: 15 -> 20; matrix products, arithmetic and copies ran while one was open for 9% -> 6% of each run, Pallas kernels for 32% -> 34%
where the time goes in v2:
time: 299 us; the launch traced here: 298 us
  Pallas kernels  112 us (37%)
  starting transfers between devices  84.6 us (28%)
  waiting for transfers between devices  70.6 us (24%)
  other arithmetic  18.1 us (6%)
  local copies, waits for them, and re-layouts  10.8 us (4%)
    ppermute x56, starting transfers between devices, permute(): return lax.ppermute(x, axis, pairs_of)  84.6 us
    ppermute x56, waiting for transfers between devices, permute(): return lax.ppermute(x, axis, pairs_of)  70.6 us
    pallas_call x4, Pallas kernels, split_weights(): pl.pallas_call(split_kernel, grid=(2,), in_specs=[pl.BlockSpec((block, 2,...  27.9 us
    pallas_call x2, Pallas kernels, project_wide(): pl.pallas_call(wide_kernel, grid=(blocks,), in_specs=[pl.BlockSpec((1, CH...  26.8 us
    pallas_call x4, Pallas kernels, project_out(): pl.pallas_call(out_kernel, grid_spec=grid_spec, out_shape=jax.ShapeDtypeS...  23.9 us
    pallas_call x4, Pallas kernels, project_narrow(): pl.pallas_call(functools.partial(narrow_kernel, len(arrays), bool(sums),...  16.7 us
    pallas_call x2, Pallas kernels, local_reads(): pl.pallas_call(functools.partial(local_kernel_entry, head_width), out_sha...  8.84 us
    pallas_call x1, Pallas kernels, owner_reads(): pl.pallas_call(owner_kernel, grid_spec=grid_spec, out_shape=jax.ShapeDtyp...  6.72 us
  transfers between devices with their start and end apart: 56, of which 20 were waited for; matrix products, arithmetic and copies ran while one was open for 6% of the time, Pallas kernels for 34%

profile of v2, /device:TPU:0, one launch (start us, length us, event | category | flops | bytes accessed | tf_op | source)
XLA Modules:
  0.0 298.0 jit_solution(7417534142451945)
XLA Ops:
  0.0 1.1 copy-done.1
  1.8 1.4 prepare.1
  3.3 1.3 collective-permute-start
  4.6 5.6 %collective-permute-start.8 = (bf16[200,1024]{1,0:T(8,128)(2,1)S(1)}, bf16[200,1024]{1,0:T(8,128)(2,1)S(1)}, u32[]{:S(2)}, u32[]{:S(2)}) collective-permute-start(bf16[200,1024]{1,0:T(8,128)(2,1)S(1)} %get-tuple-element.78.refs_0_), channel_id=1, source_target_pairs={{0,2},{1,3},{2,4},{3,5},{4,6},{5,7},{8,10},{9,11},{10,12},{11,13},... | collective-permute-start | bytes 1228808 | tf_op jit(solution)/shard_map/ppermute | solution.py:434
  10.2 1.3 collective-permute-start.3
  11.5 5.3 %collective-permute-start.11 = (bf16[200,1024]{1,0:T(8,128)(2,1)S(1)}, bf16[200,1024]{1,0:T(8,128)(2,1)}, u32[]{:S(2)}, u32[]{:S(2)}) collective-permute-start(bf16[200,1024]{1,0:T(8,128)(2,1)S(1)} %get-tuple-element.77.refs_1_), channel_id=1, source_target_pairs={{0,2},{1,3},{2,4},{3,5},{4,6},{5,7},{8,10},{9,11},{10,12},{11,13},... | collective-permute-start | bytes 1228808 | tf_op jit(solution)/shard_map/ppermute | solution.py:434
  18.7 7.0 %split_weights.4.refs_1_ = bf16[2,8192,1024]{2,1,0:T(8,128)(2,1)} custom-call(bf16[8192,2,1024]{2,1,0:T(2,128)(2,1)} %refs_0_.7), custom_call_target="tpu_custom_call" | custom-call | flops 2147483648 | bytes 16777216 | tf_op jit(solution)/shard_map/split_weights/pallas_call | solution.py:147
  26.5 2.6 collective-permute-start.28
  30.0 7.0 %split_weights.5.refs_1_ = bf16[2,8192,1024]{2,1,0:T(8,128)(2,1)} custom-call(bf16[8192,2,1024]{2,1,0:T(2,128)(2,1)} %refs_0_.7, bf16[2,8192,1024]{2,1,0:T(8,128)(2,1)} %split_weights.4.refs_1_), custom_call_target="tpu_custom_call", output_to_operand_aliasing={{}: (1, {})} | custom-call | flops 2147483648 | bytes 16777216 | tf_op jit(solution)/shard_map/split_weights/pallas_call | solution.py:147
  37.0 1.3 collective-permute-start.1
  38.4 1.3 collective-permute-start.4
  39.7 1.4 collective-permute-start.9
  41.2 1.4 collective-permute-start.12
  42.6 7.0 %split_weights.6.refs_1_ = bf16[2,8192,1024]{2,1,0:T(8,128)(2,1)} custom-call(bf16[8192,2,1024]{2,1,0:T(2,128)(2,1)} %refs_0_.7, bf16[2,8192,1024]{2,1,0:T(8,128)(2,1)} %split_weights.5.refs_1_), custom_call_target="tpu_custom_call", output_to_operand_aliasing={{}: (1, {})} | custom-call | flops 2147483648 | bytes 16777216 | tf_op jit(solution)/shard_map/split_weights/pallas_call | solution.py:147
  50.2 1.1 collective-permute-done.1.refs_0_
  51.3 6.9 %collective-permute-done.4.refs_1_ = bf16[200,1024]{1,0:T(8,128)(2,1)} collective-permute-done((bf16[200,1024]{1,0:T(8,128)(2,1)S(1)}, bf16[200,1024]{1,0:T(8,128)(2,1)}, u32[]{:S(2)}, u32[]{:S(2)}) %collective-permute-start.4) | collective-permute-done | bytes 409632 | tf_op jit(solution)/shard_map/ppermute | solution.py:434
  58.7 1.3 collective-permute-start.2
  60.0 1.3 collective-permute-start.5
  61.3 6.8 %split_weights.7.w_ref = bf16[2,8192,1024]{2,1,0:T(8,128)(2,1)} custom-call(bf16[8192,2,1024]{2,1,0:T(2,128)(2,1)} %refs_0_.7, bf16[2,8192,1024]{2,1,0:T(8,128)(2,1)} %split_weights.6.refs_1_), custom_call_target="tpu_custom_call", output_to_operand_aliasing={{}: (1, {})} | custom-call | flops 2147483648 | bytes 16777216 | tf_op jit(solution)/shard_map/split_weights/pallas_call | solution.py:147
  71.5 1.4 collective-permute-start.10
  72.9 4.8 %collective-permute-done.2.refs_0_ = bf16[200,1024]{1,0:T(8,128)(2,1)} collective-permute-done((bf16[200,1024]{1,0:T(8,128)(2,1)}, bf16[200,1024]{1,0:T(8,128)(2,1)}, u32[]{:S(2)}, u32[]{:S(2)}) %collective-permute-start.2) | collective-permute-done | bytes 409632 | tf_op jit(solution)/shard_map/ppermute | solution.py:434
  77.7 7.6 %collective-permute-done.5.refs_1_ = bf16[200,1024]{1,0:T(8,128)(2,1)} collective-permute-done((bf16[200,1024]{1,0:T(8,128)(2,1)}, bf16[200,1024]{1,0:T(8,128)(2,1)}, u32[]{:S(2)}, u32[]{:S(2)}) %collective-permute-start.5) | collective-permute-done | bytes 409632 | tf_op jit(solution)/shard_map/ppermute | solution.py:434
  85.4 1.4 collective-permute-start.13
  88.0 3.8 %project_narrow.4 = (f32[2,192,256]{2,1,0:T(8,128)S(1)}, f32[2,192,16]{2,1,0:T(8,128)S(1)}, f32[2,8,1024]{2,1,0:T(8,128)S(1)}, bf16[8,2,200,1024]{3,2,1,0:T(8,128)(2,1)}) custom-call(s32[1]{0:T(128)} %bitcast.rank, bf16[200,1024]{1,0:T(8,128)(2,1)S(1)} %get-tuple-element.78.refs_0_, bf16[200,1024]{1,0:T(8,128)(2,1)S(1)} %get-tuple-element.77.refs_1_, ...), custom_call_target="tpu_custom_call" | custom-call | flops 427819008 | bytes 1048576 | tf_op jit(solution)/shard_map/project_narrow/pallas_call | solution.py:218
  94.0 4.0 %project_narrow.5 = (f32[2,192,256]{2,1,0:T(8,128)S(1)}, f32[2,192,16]{2,1,0:T(8,128)S(1)}, f32[2,8,1024]{2,1,0:T(8,128)S(1)}, bf16[8,2,200,1024]{3,2,1,0:T(8,128)(2,1)}) custom-call(s32[1]{0:T(128)} %bitcast.rank, bf16[200,1024]{1,0:T(8,128)(2,1)S(1)} %collective-permute-done.refs_0_, ...), custom_call_target="tpu_custom_call", output_to_operand_aliasing={{0}: (11, {}), {1}: (12, {}), {2}: (13, {}), {3}: (14, {})} | custom-call | flops 855638016 | bytes 2097152 | tf_op jit(solution)/shard_map/project_narrow/pallas_call | solution.py:218
  98.0 4.7 %project_narrow.6 = (f32[2,192,256]{2,1,0:T(8,128)S(1)}, f32[2,192,16]{2,1,0:T(8,128)S(1)}, f32[2,8,1024]{2,1,0:T(8,128)S(1)}, bf16[8,2,200,1024]{3,2,1,0:T(8,128)(2,1)}) custom-call(s32[1]{0:T(128)} %bitcast.rank, bf16[200,1024]{1,0:T(8,128)(2,1)} %collective-permute-done.1.refs_0_, ...), custom_call_target="tpu_custom_call", output_to_operand_aliasing={{0}: (11, {}), {1}: (12, {}), {2}: (13, {}), {3}: (14, {})} | custom-call | flops 855638016 | bytes 2097152 | tf_op jit(solution)/shard_map/project_narrow/pallas_call | solution.py:218
  102.8 4.3 %project_narrow.7 = (f32[2,192,256]{2,1,0:T(8,128)S(1)}, f32[2,192,16]{2,1,0:T(8,128)S(1)}, f32[2,8,1024]{2,1,0:T(8,128)S(1)}, bf16[8,2,200,1024]{3,2,1,0:T(8,128)(2,1)}) custom-call(s32[1]{0:T(128)} %bitcast.rank, bf16[200,1024]{1,0:T(8,128)(2,1)} %collective-permute-done.2.refs_0_, ...), custom_call_target="tpu_custom_call", output_to_operand_aliasing={{0}: (11, {}), {1}: (12, {}), {2}: (13, {}), {3}: (14, {})} | custom-call | flops 855638016 | bytes 2097152 | tf_op jit(solution)/shard_map/project_narrow/pallas_call | solution.py:218
  108.9 3.0 %collective-permute-start.29 = (bf16[2,24,8,256]{3,2,1,0:T(8,128)(2,1)}, bf16[2,24,8,256]{3,2,1,0:T(8,128)(2,1)}, u32[]{:S(2)}, u32[]{:S(2)}) collective-permute-start(bf16[2,24,8,256]{3,2,1,0:T(8,128)(2,1)} %pad_maximum_fusion.5), channel_id=1, source_target_pairs={{0,0},{1,2},{2,4},{3,6},{4,1},{5,3},{6,5},{7,7},{8,8},{9,10},{10,1... | collective-permute-start | bytes 589832 | tf_op jit(solution)/shard_map/ppermute | solution.py:434
  111.9 13.4 %project_wide.3 = f32[2,192,1024]{2,1,0:T(8,128)S(1)} custom-call(bf16[8,2,200,1024]{3,2,1,0:T(8,128)(2,1)} %get-tuple-element.39.x_ref, bf16[2,8192,1024]{2,1,0:T(8,128)(2,1)} %split_weights.7.w_ref), custom_call_target="tpu_custom_call" | custom-call | flops 6442450944 | bytes 16777216 | tf_op jit(solution)/shard_map/project_wide/pallas_call | solution.py:181
  125.3 13.4 %project_wide.2 = f32[2,192,1024]{2,1,0:T(8,128)S(1)} custom-call(bf16[8,2,200,1024]{3,2,1,0:T(8,128)(2,1)} %get-tuple-element.39.x_ref, bf16[2,8192,1024]{2,1,0:T(8,128)(2,1)} %split_weights.7.w_ref), custom_call_target="tpu_custom_call" | custom-call | flops 6442450944 | bytes 16777216 | tf_op jit(solution)/shard_map/project_wide/pallas_call | solution.py:181
  139.6 1.5 collective-permute-done.30
  142.1 2.2 collective-permute-start.33
  145.9 5.0 %collective-permute-done.33 = bf16[2,8,24,256]{3,1,2,0:T(8,128)(2,1)S(1)} collective-permute-done((bf16[2,8,24,256]{3,1,2,0:T(8,128)(2,1)S(1)}, bf16[2,8,24,256]{3,1,2,0:T(8,128)(2,1)S(1)}, u32[]{:S(2)}, u32[]{:S(2)}) %collective-permute-start.33) | collective-permute-done | bytes 196640 | tf_op jit(solution)/shard_map/ppermute | solution.py:434
  150.8 3.3 %collective-permute-done.32 = bf16[2,8,24,256]{3,1,2,0:T(8,128)(2,1)S(1)} collective-permute-done((bf16[2,8,24,256]{3,1,2,0:T(8,128)(2,1)S(1)}, bf16[2,8,24,256]{3,1,2,0:T(8,128)(2,1)S(1)}, u32[]{:S(2)}, u32[]{:S(2)}) %collective-permute-start.32) | collective-permute-done | bytes 196640 | tf_op jit(solution)/shard_map/ppermute | solution.py:434
  154.7 6.7 %owner_reads.1 = bf16[64,24,1024]{2,1,0:T(8,128)(2,1)S(1)} custom-call(s32[16]{0:T(128)S(1)} %get-tuple-element.52.low, s32[16]{0:T(128)S(1)} %get-tuple-element.51.high, bf16[68,24,256]{2,1,0:T(8,128)(2,1)S(1)} %pad.25.c_ref, f32[16,16,64,256]{3,2,1,0:T(8,128)} %s_ref.1), custom_call_target="tpu_custom_call" | custom-call | flops 805306368 | bytes 16777216 | tf_op jit(solution)/shard_map/owner_reads/pallas_call | solution.py:285
  162.4 5.3 %collective-permute-start.34 = (bf16[8,24,1024]{2,0,1:T(8,128)(2,1)S(1)}, bf16[8,24,1024]{2,0,1:T(8,128)(2,1)S(1)}, u32[]{:S(2)}, u32[]{:S(2)}) collective-permute-start(bf16[8,24,1024]{2,0,1:T(8,128)(2,1)S(1)} %bitcast.186), channel_id=1, source_target_pairs={{0,24},{8,16},{16,8},{24,0},{1,25},{9,17},{17,9},{25,1},{2,26},{10... | collective-permute-start | bytes 1179656 | tf_op jit(solution)/shard_map/ppermute | solution.py:434
  169.1 4.4 %local_reads.3 = (f32[24,8,1024]{2,1,0:T(8,128)S(1)}, f32[24,8,1024]{2,1,0:T(8,128)S(1)}) custom-call(f32[24,8,1024]{2,1,0:T(8,128)S(1)} %get-tuple-element.72.refs_0_, f32[24,8,128]{2,1,0:T(8,128)S(1)} %broadcast_in_dim.81.refs_1_, f32[3,8,1024]{2,1,0:T(8,128)S(1)} %get-tuple-element.88.refs_2_, f32[4,1024]{1,0:T(4,128)S(1)} %copy-done.12, ...), custom_call_target="tpu_custom_call" | custom-call | flops 75497472 | bytes 2359296 | tf_op jit(solution)/shard_map/local_reads/pallas_call | solution.py:347
  173.7 4.4 %local_reads.2 = (f32[24,8,1024]{2,1,0:T(8,128)S(1)}, f32[24,8,1024]{2,1,0:T(8,128)S(1)}) custom-call(f32[24,8,1024]{2,1,0:T(8,128)S(1)} %get-tuple-element.71.refs_0_, f32[24,8,128]{2,1,0:T(8,128)S(1)} %broadcast_in_dim.75.refs_1_, f32[3,8,1024]{2,1,0:T(8,128)S(1)} %get-tuple-element.87.refs_2_, f32[4,1024]{1,0:T(4,128)S(1)} %copy-done.12, ...), custom_call_target="tpu_custom_call" | custom-call | flops 75497472 | bytes 2359296 | tf_op jit(solution)/shard_map/local_reads/pallas_call | solution.py:347
  178.3 3.0 collective-permute-start.45
  182.5 3.7 %collective-permute-done.35 = bf16[8,24,1024]{2,0,1:T(8,128)(2,1)S(1)} collective-permute-done((bf16[8,24,1024]{2,0,1:T(8,128)(2,1)S(1)}, bf16[8,24,1024]{2,0,1:T(8,128)(2,1)S(1)}, u32[]{:S(2)}, u32[]{:S(2)}) %collective-permute-start.35) | collective-permute-done | bytes 393248 | tf_op jit(solution)/shard_map/ppermute | solution.py:434
  187.1 7.5 %collective-permute-done.45 = bf16[8,24,1024]{2,0,1:T(8,128)(2,1)S(1)} collective-permute-done((bf16[8,24,1024]{2,0,1:T(8,128)(2,1)S(1)}, bf16[8,24,1024]{2,0,1:T(8,128)(2,1)S(1)}, u32[]{:S(2)}, u32[]{:S(2)}) %collective-permute-start.45) | collective-permute-done | bytes 393248 | tf_op jit(solution)/shard_map/ppermute | solution.py:434
  194.6 7.3 %collective-permute-done.46 = bf16[8,24,1024]{2,0,1:T(8,128)(2,1)S(1)} collective-permute-done((bf16[8,24,1024]{2,0,1:T(8,128)(2,1)S(1)}, bf16[8,24,1024]{2,0,1:T(8,128)(2,1)S(1)}, u32[]{:S(2)}, u32[]{:S(2)}) %collective-permute-start.46) | collective-permute-done | bytes 393248 | tf_op jit(solution)/shard_map/ppermute | solution.py:434
  202.9 6.7 %project_out.5 = bf16[4,192,1024]{2,1,0:T(8,128)(2,1)} custom-call(s32[4]{0:T(128)S(1)} %add_subtract_fusion.idx, bf16[192,1024]{1,0:T(8,128)(2,1)S(1)} %fusion.21.x_ref, bf16[1024,8192]{1,0:T(8,128)(2,1)} %w_ref.7), custom_call_target="tpu_custom_call" | custom-call | flops 1610612736 | bytes 8388608 | tf_op jit(solution)/shard_map/project_out/pallas_call | solution.py:377
  210.3 5.7 %project_out.7 = bf16[4,192,1024]{2,1,0:T(8,128)(2,1)S(1)} custom-call(s32[4]{0:T(128)S(1)} %add_subtract_fusion.idx, bf16[192,1024]{1,0:T(8,128)(2,1)S(1)} %fusion.22.x_ref, bf16[1024,8192]{1,0:T(8,128)(2,1)} %w_ref.7), custom_call_target="tpu_custom_call" | custom-call | flops 1610612736 | bytes 8388608 | tf_op jit(solution)/shard_map/project_out/pallas_call | solution.py:377
  216.2 5.7 %project_out.4 = bf16[4,192,1024]{2,1,0:T(8,128)(2,1)S(1)} custom-call(s32[4]{0:T(128)S(1)} %fusion.60.idx, bf16[192,1024]{1,0:T(8,128)(2,1)S(1)} %fusion.21.x_ref, bf16[1024,8192]{1,0:T(8,128)(2,1)} %w_ref.7), custom_call_target="tpu_custom_call" | custom-call | flops 1610612736 | bytes 8388608 | tf_op jit(solution)/shard_map/project_out/pallas_call | solution.py:377
  221.9 5.7 %project_out.6 = bf16[4,192,1024]{2,1,0:T(8,128)(2,1)S(1)} custom-call(s32[4]{0:T(128)S(1)} %fusion.60.idx, bf16[192,1024]{1,0:T(8,128)(2,1)S(1)} %fusion.22.x_ref, bf16[1024,8192]{1,0:T(8,128)(2,1)} %w_ref.7), custom_call_target="tpu_custom_call" | custom-call | flops 1610612736 | bytes 8388608 | tf_op jit(solution)/shard_map/project_out/pallas_call | solution.py:377
  227.7 2.1 add_convert_fusion.1
  229.8 12.4 %collective-permute-start.42 = (bf16[192,1024]{1,0:T(8,128)(2,1)S(1)}, bf16[192,1024]{1,0:T(8,128)(2,1)S(1)}, u32[]{:S(2)}, u32[]{:S(2)}) collective-permute-start(bf16[192,1024]{1,0:T(8,128)(2,1)S(1)} %dynamic-slice_bitcast_fusion.2), channel_id=1, source_target_pairs={{0,2},{1,3},{8,10},{9,11},{16,18},{17,19},{24,26},{25,27}} | collective-permute-start | bytes 1179656 | tf_op jit(solution)/shard_map/ppermute | solution.py:434
  243.0 2.1 add_convert_fusion
  245.1 1.3 collective-permute-start.53
  247.2 4.3 %collective-permute-done.42 = bf16[192,1024]{1,0:T(8,128)(2,1)S(1)} collective-permute-done((bf16[192,1024]{1,0:T(8,128)(2,1)S(1)}, bf16[192,1024]{1,0:T(8,128)(2,1)S(1)}, u32[]{:S(2)}, u32[]{:S(2)}) %collective-permute-start.42) | collective-permute-done | bytes 393248 | tf_op jit(solution)/shard_map/ppermute | solution.py:434
  251.6 4.4 %collective-permute-start.43 = (bf16[192,1024]{1,0:T(8,128)(2,1)S(1)}, bf16[192,1024]{1,0:T(8,128)(2,1)S(1)}, u32[]{:S(2)}, u32[]{:S(2)}) collective-permute-start(bf16[192,1024]{1,0:T(8,128)(2,1)S(1)} %fusion.8), channel_id=1, source_target_pairs={{0,2},{1,3},{2,4},{3,5},{8,10},{9,11},{10,12},{11,13},{16,18},{17,... | collective-permute-start | bytes 1179656 | tf_op jit(solution)/shard_map/ppermute | solution.py:434
  256.9 3.0 %collective-permute-done.53 = bf16[192,1024]{1,0:T(8,128)(2,1)S(1)} collective-permute-done((bf16[192,1024]{1,0:T(8,128)(2,1)S(1)}, bf16[192,1024]{1,0:T(8,128)(2,1)S(1)}, u32[]{:S(2)}, u32[]{:S(2)}) %collective-permute-start.53) | collective-permute-done | bytes 393248 | tf_op jit(solution)/shard_map/ppermute | solution.py:434
  260.1 4.4 %collective-permute-start.54 = (bf16[192,1024]{1,0:T(8,128)(2,1)S(1)}, bf16[192,1024]{1,0:T(8,128)(2,1)S(1)}, u32[]{:S(2)}, u32[]{:S(2)}) collective-permute-start(bf16[192,1024]{1,0:T(8,128)(2,1)S(1)} %fusion.2), channel_id=1, source_target_pairs={{0,2},{1,3},{2,4},{3,5},{8,10},{9,11},{10,12},{11,13},{16,18},{17,... | collective-permute-start | bytes 1179656 | tf_op jit(solution)/shard_map/ppermute | solution.py:434
  265.3 3.0 %collective-permute-done.43 = bf16[192,1024]{1,0:T(8,128)(2,1)S(1)} collective-permute-done((bf16[192,1024]{1,0:T(8,128)(2,1)S(1)}, bf16[192,1024]{1,0:T(8,128)(2,1)S(1)}, u32[]{:S(2)}, u32[]{:S(2)}) %collective-permute-start.43) | collective-permute-done | bytes 393248 | tf_op jit(solution)/shard_map/ppermute | solution.py:434
  269.2 4.4 %collective-permute-start.44 = (bf16[192,1024]{1,0:T(8,128)(2,1)}, bf16[192,1024]{1,0:T(8,128)(2,1)S(1)}, u32[]{:S(2)}, u32[]{:S(2)}) collective-permute-start(bf16[192,1024]{1,0:T(8,128)(2,1)} %fusion.9), channel_id=1, source_target_pairs={{0,2},{1,3},{2,4},{3,5},{4,6},{5,7},{8,10},{9,11},{10,12},{11,13},... | collective-permute-start | bytes 1179656 | tf_op jit(solution)/shard_map/ppermute | solution.py:434
  274.6 1.3 collective-permute-start.41
  277.6 5.2 %collective-permute-start.55 = (bf16[192,1024]{1,0:T(8,128)(2,1)}, bf16[192,1024]{1,0:T(8,128)(2,1)}, u32[]{:S(2)}, u32[]{:S(2)}) collective-permute-start(bf16[192,1024]{1,0:T(8,128)(2,1)} %fusion.3), channel_id=1, source_target_pairs={{0,2},{1,3},{2,4},{3,5},{4,6},{5,7},{8,10},{9,11},{10,12},{11,13},... | collective-permute-start | bytes 1179656 | tf_op jit(solution)/shard_map/ppermute | solution.py:434
  283.7 1.3 collective-permute-start.52
  285.3 1.3 collective-permute-done.41
  286.6 1.2 fusion.23
  287.8 5.4 %collective-permute-done.55 = bf16[192,1024]{1,0:T(8,128)(2,1)} collective-permute-done((bf16[192,1024]{1,0:T(8,128)(2,1)}, bf16[192,1024]{1,0:T(8,128)(2,1)}, u32[]{:S(2)}, u32[]{:S(2)}) %collective-permute-start.55) | collective-permute-done | bytes 393248 | tf_op jit(solution)/shard_map/ppermute | solution.py:434
  293.2 2.5 collective-permute-done.52
  295.7 1.3 fusion.24
  (244 shorter events, 33.3 us)
Async XLA Ops:
  3.3 15.3 %collective-permute-start = (bf16[200,1024]{1,0:T(8,128)(2,1)S(1)}, bf16[200,1024]{1,0:T(8,128)(2,1)S(1)}, u32[]{:S(2)}, u32[]{:S(2)}) collective-permute-start(bf16[200,1024]{1,0:T(8,128)(2,1)S(1)} %get-tuple-element.78.refs_0_), channel_id=1, source_target_pairs={{2,0},{3,1},{4,2},{5,3},{6,4},{7,5},{10,8},{11,9},{12,10},{13,11},... | collective-permute-start | bytes 1228808 | tf_op jit(solution)/shard_map/ppermute | solution.py:434
  4.6 24.5 %collective-permute-start.8 = (bf16[200,1024]{1,0:T(8,128)(2,1)S(1)}, bf16[200,1024]{1,0:T(8,128)(2,1)S(1)}, u32[]{:S(2)}, u32[]{:S(2)}) collective-permute-start(bf16[200,1024]{1,0:T(8,128)(2,1)S(1)} %get-tuple-element.78.refs_0_), channel_id=1, source_target_pairs={{0,2},{1,3},{2,4},{3,5},{4,6},{5,7},{8,10},{9,11},{10,12},{11,13},... | collective-permute-start | bytes 1228808 | tf_op jit(solution)/shard_map/ppermute | solution.py:434
  10.2 16.3 %collective-permute-start.3 = (bf16[200,1024]{1,0:T(8,128)(2,1)S(1)}, bf16[200,1024]{1,0:T(8,128)(2,1)S(1)}, u32[]{:S(2)}, u32[]{:S(2)}) collective-permute-start(bf16[200,1024]{1,0:T(8,128)(2,1)S(1)} %get-tuple-element.77.refs_1_), channel_id=1, source_target_pairs={{2,0},{3,1},{4,2},{5,3},{6,4},{7,5},{10,8},{11,9},{12,10},{13,11},... | collective-permute-start | bytes 1228808 | tf_op jit(solution)/shard_map/ppermute | solution.py:434
  11.5 18.1 %collective-permute-start.11 = (bf16[200,1024]{1,0:T(8,128)(2,1)S(1)}, bf16[200,1024]{1,0:T(8,128)(2,1)}, u32[]{:S(2)}, u32[]{:S(2)}) collective-permute-start(bf16[200,1024]{1,0:T(8,128)(2,1)S(1)} %get-tuple-element.77.refs_1_), channel_id=1, source_target_pairs={{0,2},{1,3},{2,4},{3,5},{4,6},{5,7},{8,10},{9,11},{10,12},{11,13},... | collective-permute-start | bytes 1228808 | tf_op jit(solution)/shard_map/ppermute | solution.py:434
  16.8 20.2 %collective-permute-start.24 = (bf16[200,1024]{1,0:T(8,128)(2,1)S(1)}, bf16[200,1024]{1,0:T(8,128)(2,1)S(1)}, u32[]{:S(2)}, u32[]{:S(2)}) collective-permute-start(bf16[200,1024]{1,0:T(8,128)(2,1)S(1)} %get-tuple-element.78.refs_0_), channel_id=1, source_target_pairs={{0,1},{1,0},{2,3},{3,2},{4,5},{5,4},{6,7},{7,6},{8,9},{9,8},{10,11... | collective-permute-start | bytes 1228808 | tf_op jit(solution)/shard_map/ppermute | solution.py:434
  18.5 19.8 %collective-permute-start.25 = (bf16[200,1024]{1,0:T(8,128)(2,1)S(1)}, bf16[200,1024]{1,0:T(8,128)(2,1)S(1)}, u32[]{:S(2)}, u32[]{:S(2)}) collective-permute-start(bf16[200,1024]{1,0:T(8,128)(2,1)S(1)} %get-tuple-element.77.refs_1_), channel_id=1, source_target_pairs={{0,1},{1,0},{2,3},{3,2},{4,5},{5,4},{6,7},{7,6},{8,9},{9,8},{10,11... | collective-permute-start | bytes 1228808 | tf_op jit(solution)/shard_map/ppermute | solution.py:434
  26.5 24.9 %copy-start.2 = (bf16[200,1024]{1,0:T(8,128)(2,1)}, bf16[200,1024]{1,0:T(8,128)(2,1)S(1)}, u32[]{:S(2)}) copy-start(bf16[200,1024]{1,0:T(8,128)(2,1)S(1)} %collective-permute-done.3.refs_1_) | copy-start | bytes 1228804
  26.5 11.9 %collective-permute-start.28 = (bf16[3,16,1280]{2,1,0:T(8,128)(2,1)S(1)}, bf16[3,16,1280]{2,1,0:T(8,128)(2,1)S(1)}, u32[]{:S(2)}, u32[]{:S(2)}) collective-permute-start(bf16[3,16,1280]{2,1,0:T(8,128)(2,1)S(1)} %pad_maximum_fusion.6), channel_id=1, source_target_pairs={{0,24},{8,16},{16,8},{24,0},{1,25},{9,17},{17,9},{25,1},{2,26},{10... | collective-permute-start | bytes 368648 | tf_op jit(solution)/shard_map/ppermute | solution.py:434
  29.1 10.6 %collective-permute-start.27 = (bf16[3,16,1280]{2,1,0:T(8,128)(2,1)S(1)}, bf16[3,16,1280]{2,1,0:T(8,128)(2,1)S(1)}, u32[]{:S(2)}, u32[]{:S(2)}) collective-permute-start(bf16[3,16,1280]{2,1,0:T(8,128)(2,1)S(1)} %pad_maximum_fusion.6), channel_id=1, source_target_pairs={{0,16},{8,24},{16,0},{24,8},{1,17},{9,25},{17,1},{25,9},{2,18},{10... | collective-permute-start | bytes 368648 | tf_op jit(solution)/shard_map/ppermute | solution.py:434
  29.6 11.6 %collective-permute-start.26 = (bf16[3,16,1280]{2,1,0:T(8,128)(2,1)S(1)}, bf16[3,16,1280]{2,1,0:T(8,128)(2,1)S(1)}, u32[]{:S(2)}, u32[]{:S(2)}) collective-permute-start(bf16[3,16,1280]{2,1,0:T(8,128)(2,1)S(1)} %pad_maximum_fusion.6), channel_id=1, source_target_pairs={{0,8},{8,0},{16,24},{24,16},{1,9},{9,1},{17,25},{25,17},{2,10},{10... | collective-permute-start | bytes 368648 | tf_op jit(solution)/shard_map/ppermute | solution.py:434
  37.0 14.3 %collective-permute-start.1 = (bf16[200,1024]{1,0:T(8,128)(2,1)S(1)}, bf16[200,1024]{1,0:T(8,128)(2,1)}, u32[]{:S(2)}, u32[]{:S(2)}) collective-permute-start(bf16[200,1024]{1,0:T(8,128)(2,1)S(1)} %collective-permute-done.refs_0_), channel_id=1, source_target_pairs={{2,0},{3,1},{4,2},{5,3},{10,8},{11,9},{12,10},{13,11},{18,16},{19,... | collective-permute-start | bytes 1228808 | tf_op jit(solution)/shard_map/ppermute | solution.py:434
  38.3 21.7 %collective-permute-start.20 = (bf16[200,1024]{1,0:T(8,128)(2,1)S(1)}, bf16[200,1024]{1,0:T(8,128)(2,1)S(1)}, u32[]{:S(2)}, u32[]{:S(2)}) collective-permute-start(bf16[200,1024]{1,0:T(8,128)(2,1)S(1)} %collective-permute-done.refs_0_), channel_id=1, source_target_pairs={{0,1},{1,0},{2,3},{3,2},{4,5},{5,4},{6,7},{7,6},{8,9},{9,8},{10,11... | collective-permute-start | bytes 1228808 | tf_op jit(solution)/shard_map/ppermute | solution.py:434
  38.4 19.8 %collective-permute-start.4 = (bf16[200,1024]{1,0:T(8,128)(2,1)S(1)}, bf16[200,1024]{1,0:T(8,128)(2,1)}, u32[]{:S(2)}, u32[]{:S(2)}) collective-permute-start(bf16[200,1024]{1,0:T(8,128)(2,1)S(1)} %collective-permute-done.3.refs_1_), channel_id=1, source_target_pairs={{2,0},{3,1},{4,2},{5,3},{10,8},{11,9},{12,10},{13,11},{18,16},{19,... | collective-permute-start | bytes 1228808 | tf_op jit(solution)/shard_map/ppermute | solution.py:434
  39.7 18.5 %collective-permute-start.9 = (bf16[200,1024]{1,0:T(8,128)(2,1)S(1)}, bf16[200,1024]{1,0:T(8,128)(2,1)}, u32[]{:S(2)}, u32[]{:S(2)}) collective-permute-start(bf16[200,1024]{1,0:T(8,128)(2,1)S(1)} %collective-permute-done.8.refs_4_), channel_id=1, source_target_pairs={{2,4},{3,5},{4,6},{5,7},{10,12},{11,13},{12,14},{13,15},{18,20},{1... | collective-permute-start | bytes 1228808 | tf_op jit(solution)/shard_map/ppermute | solution.py:434
  41.2 17.5 %collective-permute-start.12 = (bf16[200,1024]{1,0:T(8,128)(2,1)}, bf16[200,1024]{1,0:T(8,128)(2,1)}, u32[]{:S(2)}, u32[]{:S(2)}) collective-permute-start(bf16[200,1024]{1,0:T(8,128)(2,1)} %collective-permute-done.11.refs_5_), channel_id=1, source_target_pairs={{2,4},{3,5},{4,6},{5,7},{10,12},{11,13},{12,14},{13,15},{18,20},{1... | collective-permute-start | bytes 1228808 | tf_op jit(solution)/shard_map/ppermute | solution.py:434
  50.2 17.9 %copy-start.30 = (f32[4,256]{1,0:T(4,128)S(1)}, f32[4,256]{1,0:T(4,128)}, u32[]{:S(2)}) copy-start(f32[4,256]{1,0:T(4,128)} %param.29) | copy-start | bytes 12292
  50.2 36.6 %copy-start.48 = (f32[16]{0:T(128)S(1)}, f32[16]{0:T(128)}, u32[]{:S(2)}) copy-start(f32[16]{0:T(128)} %param.33) | copy-start | bytes 196
  50.2 37.1 %copy-start.49 = (f32[16]{0:T(128)S(1)}, f32[16]{0:T(128)}, u32[]{:S(2)}) copy-start(f32[16]{0:T(128)} %param.32) | copy-start | bytes 196
  50.2 37.7 %copy-start = (bf16[8192,16]{0,1:T(8,128)(2,1)S(1)}, bf16[8192,16]{0,1:T(8,128)(2,1)}, u32[]{:S(2)}) copy-start(bf16[8192,16]{0,1:T(8,128)(2,1)} %param.26) | copy-start | bytes 786436
  51.3 17.4 %collective-permute-start.21 = (bf16[200,1024]{1,0:T(8,128)(2,1)S(1)}, bf16[200,1024]{1,0:T(8,128)(2,1)S(1)}, u32[]{:S(2)}, u32[]{:S(2)}) collective-permute-start(bf16[200,1024]{1,0:T(8,128)(2,1)S(1)} %collective-permute-done.3.refs_1_), channel_id=1, source_target_pairs={{0,1},{1,0},{2,3},{3,2},{4,5},{5,4},{6,7},{7,6},{8,9},{9,8},{10,11... | collective-permute-start | bytes 1228808 | tf_op jit(solution)/shard_map/ppermute | solution.py:434
  58.2 11.3 %collective-permute-start.22 = (bf16[200,1024]{1,0:T(8,128)(2,1)S(1)}, bf16[200,1024]{1,0:T(8,128)(2,1)S(1)}, u32[]{:S(2)}, u32[]{:S(2)}) collective-permute-start(bf16[200,1024]{1,0:T(8,128)(2,1)S(1)} %collective-permute-done.8.refs_4_), channel_id=1, source_target_pairs={{0,1},{1,0},{2,3},{3,2},{4,5},{5,4},{6,7},{7,6},{8,9},{9,8},{10,11... | collective-permute-start | bytes 1228808 | tf_op jit(solution)/shard_map/ppermute | solution.py:434
  58.2 12.6 %collective-permute-start.23 = (bf16[200,1024]{1,0:T(8,128)(2,1)}, bf16[200,1024]{1,0:T(8,128)(2,1)S(1)}, u32[]{:S(2)}, u32[]{:S(2)}) collective-permute-start(bf16[200,1024]{1,0:T(8,128)(2,1)} %collective-permute-done.11.refs_5_), channel_id=1, source_target_pairs={{0,1},{1,0},{2,3},{3,2},{4,5},{5,4},{6,7},{7,6},{8,9},{9,8},{10,11... | collective-permute-start | bytes 1228808 | tf_op jit(solution)/shard_map/ppermute | solution.py:434
  58.7 19.0 %collective-permute-start.2 = (bf16[200,1024]{1,0:T(8,128)(2,1)}, bf16[200,1024]{1,0:T(8,128)(2,1)}, u32[]{:S(2)}, u32[]{:S(2)}) collective-permute-start(bf16[200,1024]{1,0:T(8,128)(2,1)} %collective-permute-done.1.refs_0_), channel_id=1, source_target_pairs={{2,0},{3,1},{10,8},{11,9},{18,16},{19,17},{26,24},{27,25}} | collective-permute-start | bytes 1228808 | tf_op jit(solution)/shard_map/ppermute | solution.py:434
  60.0 25.3 %collective-permute-start.5 = (bf16[200,1024]{1,0:T(8,128)(2,1)}, bf16[200,1024]{1,0:T(8,128)(2,1)}, u32[]{:S(2)}, u32[]{:S(2)}) collective-permute-start(bf16[200,1024]{1,0:T(8,128)(2,1)} %collective-permute-done.4.refs_1_), channel_id=1, source_target_pairs={{2,0},{3,1},{10,8},{11,9},{18,16},{19,17},{26,24},{27,25}} | collective-permute-start | bytes 1228808 | tf_op jit(solution)/shard_map/ppermute | solution.py:434
  69.5 23.2 %collective-permute-start.16 = (bf16[200,1024]{1,0:T(8,128)(2,1)}, bf16[200,1024]{1,0:T(8,128)(2,1)}, u32[]{:S(2)}, u32[]{:S(2)}) collective-permute-start(bf16[200,1024]{1,0:T(8,128)(2,1)} %collective-permute-done.1.refs_0_), channel_id=1, source_target_pairs={{0,1},{1,0},{2,3},{3,2},{4,5},{5,4},{6,7},{7,6},{8,9},{9,8},{10,11... | collective-permute-start | bytes 1228808 | tf_op jit(solution)/shard_map/ppermute | solution.py:434
  70.3 22.5 %collective-permute-start.17 = (bf16[200,1024]{1,0:T(8,128)(2,1)}, bf16[200,1024]{1,0:T(8,128)(2,1)}, u32[]{:S(2)}, u32[]{:S(2)}) collective-permute-start(bf16[200,1024]{1,0:T(8,128)(2,1)} %collective-permute-done.4.refs_1_), channel_id=1, source_target_pairs={{0,1},{1,0},{2,3},{3,2},{4,5},{5,4},{6,7},{7,6},{8,9},{9,8},{10,11... | collective-permute-start | bytes 1228808 | tf_op jit(solution)/shard_map/ppermute | solution.py:434
  71.5 20.6 %collective-permute-start.10 = (bf16[200,1024]{1,0:T(8,128)(2,1)}, bf16[200,1024]{1,0:T(8,128)(2,1)}, u32[]{:S(2)}, u32[]{:S(2)}) collective-permute-start(bf16[200,1024]{1,0:T(8,128)(2,1)} %collective-permute-done.9.refs_4_), channel_id=1, source_target_pairs={{4,6},{5,7},{12,14},{13,15},{20,22},{21,23},{28,30},{29,31}} | collective-permute-start | bytes 1228808 | tf_op jit(solution)/shard_map/ppermute | solution.py:434
  77.7 15.5 %collective-permute-start.18 = (bf16[200,1024]{1,0:T(8,128)(2,1)}, bf16[200,1024]{1,0:T(8,128)(2,1)}, u32[]{:S(2)}, u32[]{:S(2)}) collective-permute-start(bf16[200,1024]{1,0:T(8,128)(2,1)} %collective-permute-done.9.refs_4_), channel_id=1, source_target_pairs={{0,1},{1,0},{2,3},{3,2},{4,5},{5,4},{6,7},{7,6},{8,9},{9,8},{10,11... | collective-permute-start | bytes 1228808 | tf_op jit(solution)/shard_map/ppermute | solution.py:434
  85.4 6.9 %collective-permute-start.13 = (bf16[200,1024]{1,0:T(8,128)(2,1)}, bf16[200,1024]{1,0:T(8,128)(2,1)}, u32[]{:S(2)}, u32[]{:S(2)}) collective-permute-start(bf16[200,1024]{1,0:T(8,128)(2,1)} %collective-permute-done.12.refs_5_), channel_id=1, source_target_pairs={{4,6},{5,7},{12,14},{13,15},{20,22},{21,23},{28,30},{29,31}} | collective-permute-start | bytes 1228808 | tf_op jit(solution)/shard_map/ppermute | solution.py:434
  92.1 5.8 %collective-permute-start.19 = (bf16[200,1024]{1,0:T(8,128)(2,1)}, bf16[200,1024]{1,0:T(8,128)(2,1)S(1)}, u32[]{:S(2)}, u32[]{:S(2)}) collective-permute-start(bf16[200,1024]{1,0:T(8,128)(2,1)} %collective-permute-done.12.refs_5_), channel_id=1, source_target_pairs={{0,1},{1,0},{2,3},{3,2},{4,5},{5,4},{6,7},{7,6},{8,9},{9,8},{10,11... | collective-permute-start | bytes 1228808 | tf_op jit(solution)/shard_map/ppermute | solution.py:434
  92.2 10.5 %collective-permute-start.6 = (bf16[200,1024]{1,0:T(8,128)(2,1)}, bf16[200,1024]{1,0:T(8,128)(2,1)S(1)}, u32[]{:S(2)}, u32[]{:S(2)}) collective-permute-start(bf16[200,1024]{1,0:T(8,128)(2,1)} %collective-permute-done.2.refs_0_), channel_id=1, source_target_pairs={{0,1},{1,0},{2,3},{3,2},{4,5},{5,4},{6,7},{7,6},{8,9},{9,8},{10,11... | collective-permute-start | bytes 1228808 | tf_op jit(solution)/shard_map/ppermute | solution.py:434
  92.7 10.0 %collective-permute-start.7 = (bf16[200,1024]{1,0:T(8,128)(2,1)}, bf16[200,1024]{1,0:T(8,128)(2,1)S(1)}, u32[]{:S(2)}, u32[]{:S(2)}) collective-permute-start(bf16[200,1024]{1,0:T(8,128)(2,1)} %collective-permute-done.5.refs_1_), channel_id=1, source_target_pairs={{0,1},{1,0},{2,3},{3,2},{4,5},{5,4},{6,7},{7,6},{8,9},{9,8},{10,11... | collective-permute-start | bytes 1228808 | tf_op jit(solution)/shard_map/ppermute | solution.py:434
  92.8 9.9 %collective-permute-start.14 = (bf16[200,1024]{1,0:T(8,128)(2,1)}, bf16[200,1024]{1,0:T(8,128)(2,1)S(1)}, u32[]{:S(2)}, u32[]{:S(2)}) collective-permute-start(bf16[200,1024]{1,0:T(8,128)(2,1)} %collective-permute-done.10.refs_4_), channel_id=1, source_target_pairs={{0,1},{1,0},{2,3},{3,2},{4,5},{5,4},{6,7},{7,6},{8,9},{9,8},{10,11... | collective-permute-start | bytes 1228808 | tf_op jit(solution)/shard_map/ppermute | solution.py:434
  93.2 9.5 %collective-permute-start.15 = (bf16[200,1024]{1,0:T(8,128)(2,1)}, bf16[200,1024]{1,0:T(8,128)(2,1)S(1)}, u32[]{:S(2)}, u32[]{:S(2)}) collective-permute-start(bf16[200,1024]{1,0:T(8,128)(2,1)} %collective-permute-done.13.refs_5_), channel_id=1, source_target_pairs={{0,1},{1,0},{2,3},{3,2},{4,5},{5,4},{6,7},{7,6},{8,9},{9,8},{10,11... | collective-permute-start | bytes 1228808 | tf_op jit(solution)/shard_map/ppermute | solution.py:434
  108.9 30.5 %collective-permute-start.29 = (bf16[2,24,8,256]{3,2,1,0:T(8,128)(2,1)}, bf16[2,24,8,256]{3,2,1,0:T(8,128)(2,1)}, u32[]{:S(2)}, u32[]{:S(2)}) collective-permute-start(bf16[2,24,8,256]{3,2,1,0:T(8,128)(2,1)} %pad_maximum_fusion.5), channel_id=1, source_target_pairs={{0,0},{1,2},{2,4},{3,6},{4,1},{5,3},{6,5},{7,7},{8,8},{9,10},{10,1... | collective-permute-start | bytes 589832 | tf_op jit(solution)/shard_map/ppermute | solution.py:434
  139.4 1.7 collective-permute-start.30
  142.1 8.8 %collective-permute-start.33 = (bf16[2,8,24,256]{3,1,2,0:T(8,128)(2,1)S(1)}, bf16[2,8,24,256]{3,1,2,0:T(8,128)(2,1)S(1)}, u32[]{:S(2)}, u32[]{:S(2)}) collective-permute-start(bf16[2,8,24,256]{3,1,2,0:T(8,128)(2,1)S(1)} %bitcast.181), channel_id=1, source_target_pairs={{0,24},{8,16},{16,8},{24,0},{1,25},{9,17},{17,9},{25,1},{2,26},{10... | collective-permute-start | bytes 589832 | tf_op jit(solution)/shard_map/ppermute | solution.py:434
  144.3 9.9 %collective-permute-start.32 = (bf16[2,8,24,256]{3,1,2,0:T(8,128)(2,1)S(1)}, bf16[2,8,24,256]{3,1,2,0:T(8,128)(2,1)S(1)}, u32[]{:S(2)}, u32[]{:S(2)}) collective-permute-start(bf16[2,8,24,256]{3,1,2,0:T(8,128)(2,1)S(1)} %bitcast.182), channel_id=1, source_target_pairs={{0,16},{8,24},{16,0},{24,8},{1,17},{9,25},{17,1},{25,9},{2,18},{10... | collective-permute-start | bytes 589832 | tf_op jit(solution)/shard_map/ppermute | solution.py:434
  144.8 9.4 %collective-permute-start.31 = (bf16[2,8,24,256]{3,1,2,0:T(8,128)(2,1)S(1)}, bf16[2,8,24,256]{3,1,2,0:T(8,128)(2,1)S(1)}, u32[]{:S(2)}, u32[]{:S(2)}) collective-permute-start(bf16[2,8,24,256]{3,1,2,0:T(8,128)(2,1)S(1)} %bitcast.183), channel_id=1, source_target_pairs={{0,8},{8,0},{16,24},{24,16},{1,9},{9,1},{17,25},{25,17},{2,10},{10... | collective-permute-start | bytes 589832 | tf_op jit(solution)/shard_map/ppermute | solution.py:434
  162.4 19.5 %collective-permute-start.34 = (bf16[8,24,1024]{2,0,1:T(8,128)(2,1)S(1)}, bf16[8,24,1024]{2,0,1:T(8,128)(2,1)S(1)}, u32[]{:S(2)}, u32[]{:S(2)}) collective-permute-start(bf16[8,24,1024]{2,0,1:T(8,128)(2,1)S(1)} %bitcast.186), channel_id=1, source_target_pairs={{0,24},{8,16},{16,8},{24,0},{1,25},{9,17},{17,9},{25,1},{2,26},{10... | collective-permute-start | bytes 1179656 | tf_op jit(solution)/shard_map/ppermute | solution.py:434
  167.9 18.3 %collective-permute-start.35 = (bf16[8,24,1024]{2,0,1:T(8,128)(2,1)S(1)}, bf16[8,24,1024]{2,0,1:T(8,128)(2,1)S(1)}, u32[]{:S(2)}, u32[]{:S(2)}) collective-permute-start(bf16[8,24,1024]{2,0,1:T(8,128)(2,1)S(1)} %bitcast.185), channel_id=1, source_target_pairs={{0,16},{8,24},{16,0},{24,8},{1,17},{9,25},{17,1},{25,9},{2,18},{10... | collective-permute-start | bytes 1179656 | tf_op jit(solution)/shard_map/ppermute | solution.py:434
  168.2 17.9 %collective-permute-start.36 = (bf16[8,24,1024]{2,0,1:T(8,128)(2,1)S(1)}, bf16[8,24,1024]{2,0,1:T(8,128)(2,1)S(1)}, u32[]{:S(2)}, u32[]{:S(2)}) collective-permute-start(bf16[8,24,1024]{2,0,1:T(8,128)(2,1)S(1)} %bitcast.187), channel_id=1, source_target_pairs={{0,8},{8,0},{16,24},{24,16},{1,9},{9,1},{17,25},{25,17},{2,10},{10... | collective-permute-start | bytes 1179656 | tf_op jit(solution)/shard_map/ppermute | solution.py:434
  178.3 16.2 %collective-permute-start.45 = (bf16[8,24,1024]{2,0,1:T(8,128)(2,1)S(1)}, bf16[8,24,1024]{2,0,1:T(8,128)(2,1)S(1)}, u32[]{:S(2)}, u32[]{:S(2)}) collective-permute-start(bf16[8,24,1024]{2,0,1:T(8,128)(2,1)S(1)} %bitcast.188), channel_id=1, source_target_pairs={{0,24},{8,16},{16,8},{24,0},{1,25},{9,17},{17,9},{25,1},{2,26},{10... | collective-permute-start | bytes 1179656 | tf_op jit(solution)/shard_map/ppermute | solution.py:434
  181.5 20.3 %collective-permute-start.46 = (bf16[8,24,1024]{2,0,1:T(8,128)(2,1)S(1)}, bf16[8,24,1024]{2,0,1:T(8,128)(2,1)S(1)}, u32[]{:S(2)}, u32[]{:S(2)}) collective-permute-start(bf16[8,24,1024]{2,0,1:T(8,128)(2,1)S(1)} %bitcast.189), channel_id=1, source_target_pairs={{0,16},{8,24},{16,0},{24,8},{1,17},{9,25},{17,1},{25,9},{2,18},{10... | collective-permute-start | bytes 1179656 | tf_op jit(solution)/shard_map/ppermute | solution.py:434
  181.9 20.0 %collective-permute-start.47 = (bf16[8,24,1024]{2,0,1:T(8,128)(2,1)S(1)}, bf16[8,24,1024]{2,0,1:T(8,128)(2,1)S(1)}, u32[]{:S(2)}, u32[]{:S(2)}) collective-permute-start(bf16[8,24,1024]{2,0,1:T(8,128)(2,1)S(1)} %bitcast.190), channel_id=1, source_target_pairs={{0,8},{8,0},{16,24},{24,16},{1,9},{9,1},{17,25},{25,17},{2,10},{10... | collective-permute-start | bytes 1179656 | tf_op jit(solution)/shard_map/ppermute | solution.py:434
  186.5 15.3 %copy-start.31 = (pred[8]{0:T(512)(128)(4,1)S(1)}, pred[8]{0:T(512)(128)(4,1)}, u32[]{:S(2)}) copy-start(pred[8]{0:T(512)(128)(4,1)} %get-tuple-element.107) | copy-start | bytes 28
  186.5 15.3 %copy-start.32 = (pred[8]{0:T(512)(128)(4,1)S(1)}, pred[8]{0:T(512)(128)(4,1)}, u32[]{:S(2)}) copy-start(pred[8]{0:T(512)(128)(4,1)} %get-tuple-element.109) | copy-start | bytes 28
  186.5 15.3 %copy-start.33 = (pred[8]{0:T(512)(128)(4,1)S(1)}, pred[8]{0:T(512)(128)(4,1)}, u32[]{:S(2)}) copy-start(pred[8]{0:T(512)(128)(4,1)} %get-tuple-element.110) | copy-start | bytes 28
  187.1 15.1 %collective-permute-start.37 = (f32[24,8]{1,0:T(8,128)S(1)}, f32[24,8]{1,0:T(8,128)S(1)}, u32[]{:S(2)}, u32[]{:S(2)}) collective-permute-start(f32[24,8]{1,0:T(8,128)S(1)} %get-tuple-element.55), channel_id=1, source_target_pairs={{0,1},{1,0},{2,3},{3,2},{4,5},{5,4},{6,7},{7,6},{8,9},{9,8},{10,11... | collective-permute-start | bytes 2312 | tf_op jit(solution)/shard_map/ppermute | solution.py:434
  202.9 7.3 %collective-permute-start.48 = (f32[24,8]{1,0:T(8,128)S(1)}, f32[24,8]{1,0:T(8,128)S(1)}, u32[]{:S(2)}, u32[]{:S(2)}) collective-permute-start(f32[24,8]{1,0:T(8,128)S(1)} %get-tuple-element.53), channel_id=1, source_target_pairs={{0,1},{1,0},{2,3},{3,2},{4,5},{5,4},{6,7},{7,6},{8,9},{9,8},{10,11... | collective-permute-start | bytes 2312 | tf_op jit(solution)/shard_map/ppermute | solution.py:434
  209.6 18.0 %collective-permute-start.38 = (bf16[4,192,1024]{2,1,0:T(8,128)(2,1)}, bf16[4,192,1024]{2,1,0:T(8,128)(2,1)}, u32[]{:S(2)}, u32[]{:S(2)}) collective-permute-start(bf16[4,192,1024]{2,1,0:T(8,128)(2,1)} %project_out.5), channel_id=1, source_target_pairs={{0,1},{1,0},{2,3},{3,2},{4,5},{5,4},{6,7},{7,6},{8,9},{9,8},{10,11... | collective-permute-start | bytes 4718600 | tf_op jit(solution)/shard_map/ppermute | solution.py:434
  216.0 26.9 %collective-permute-start.49 = (bf16[4,192,1024]{2,1,0:T(8,128)(2,1)S(1)}, bf16[4,192,1024]{2,1,0:T(8,128)(2,1)}, u32[]{:S(2)}, u32[]{:S(2)}) collective-permute-start(bf16[4,192,1024]{2,1,0:T(8,128)(2,1)S(1)} %project_out.7), channel_id=1, source_target_pairs={{0,1},{1,0},{2,3},{3,2},{4,5},{5,4},{6,7},{7,6},{8,9},{9,8},{10,11... | collective-permute-start | bytes 4718600 | tf_op jit(solution)/shard_map/ppermute | solution.py:434
  229.8 21.7 %collective-permute-start.42 = (bf16[192,1024]{1,0:T(8,128)(2,1)S(1)}, bf16[192,1024]{1,0:T(8,128)(2,1)S(1)}, u32[]{:S(2)}, u32[]{:S(2)}) collective-permute-start(bf16[192,1024]{1,0:T(8,128)(2,1)S(1)} %dynamic-slice_bitcast_fusion.2), channel_id=1, source_target_pairs={{0,2},{1,3},{8,10},{9,11},{16,18},{17,19},{24,26},{25,27}} | collective-permute-start | bytes 1179656 | tf_op jit(solution)/shard_map/ppermute | solution.py:434
  242.3 13.8 %collective-permute-start.39 = (bf16[192,1024]{1,0:T(8,128)(2,1)S(1)}, bf16[192,1024]{1,0:T(8,128)(2,1)S(1)}, u32[]{:S(2)}, u32[]{:S(2)}) collective-permute-start(bf16[192,1024]{1,0:T(8,128)(2,1)S(1)} %dynamic-slice_bitcast_fusion.3), channel_id=1, source_target_pairs={{6,4},{7,5},{14,12},{15,13},{22,20},{23,21},{30,28},{31,29}} | collective-permute-start | bytes 1179656 | tf_op jit(solution)/shard_map/ppermute | solution.py:434
  245.1 14.8 %collective-permute-start.53 = (bf16[192,1024]{1,0:T(8,128)(2,1)S(1)}, bf16[192,1024]{1,0:T(8,128)(2,1)S(1)}, u32[]{:S(2)}, u32[]{:S(2)}) collective-permute-start(bf16[192,1024]{1,0:T(8,128)(2,1)S(1)} %dynamic-slice_bitcast_fusion), channel_id=1, source_target_pairs={{0,2},{1,3},{8,10},{9,11},{16,18},{17,19},{24,26},{25,27}} | collective-permute-start | bytes 1179656 | tf_op jit(solution)/shard_map/ppermute | solution.py:434
  246.5 18.0 %collective-permute-start.50 = (bf16[192,1024]{1,0:T(8,128)(2,1)S(1)}, bf16[192,1024]{1,0:T(8,128)(2,1)S(1)}, u32[]{:S(2)}, u32[]{:S(2)}) collective-permute-start(bf16[192,1024]{1,0:T(8,128)(2,1)S(1)} %dynamic-slice_bitcast_fusion.1), channel_id=1, source_target_pairs={{6,4},{7,5},{14,12},{15,13},{22,20},{23,21},{30,28},{31,29}} | collective-permute-start | bytes 1179656 | tf_op jit(solution)/shard_map/ppermute | solution.py:434
  251.6 16.7 %collective-permute-start.43 = (bf16[192,1024]{1,0:T(8,128)(2,1)S(1)}, bf16[192,1024]{1,0:T(8,128)(2,1)S(1)}, u32[]{:S(2)}, u32[]{:S(2)}) collective-permute-start(bf16[192,1024]{1,0:T(8,128)(2,1)S(1)} %fusion.8), channel_id=1, source_target_pairs={{0,2},{1,3},{2,4},{3,5},{8,10},{9,11},{10,12},{11,13},{16,18},{17,... | collective-permute-start | bytes 1179656 | tf_op jit(solution)/shard_map/ppermute | solution.py:434
  256.2 17.4 %collective-permute-start.40 = (bf16[192,1024]{1,0:T(8,128)(2,1)S(1)}, bf16[192,1024]{1,0:T(8,128)(2,1)S(1)}, u32[]{:S(2)}, u32[]{:S(2)}) collective-permute-start(bf16[192,1024]{1,0:T(8,128)(2,1)S(1)} %fusion.10), channel_id=1, source_target_pairs={{4,2},{5,3},{6,4},{7,5},{12,10},{13,11},{14,12},{15,13},{20,18},{2... | collective-permute-start | bytes 1179656 | tf_op jit(solution)/shard_map/ppermute | solution.py:434
  260.1 16.7 %collective-permute-start.54 = (bf16[192,1024]{1,0:T(8,128)(2,1)S(1)}, bf16[192,1024]{1,0:T(8,128)(2,1)S(1)}, u32[]{:S(2)}, u32[]{:S(2)}) collective-permute-start(bf16[192,1024]{1,0:T(8,128)(2,1)S(1)} %fusion.2), channel_id=1, source_target_pairs={{0,2},{1,3},{2,4},{3,5},{8,10},{9,11},{10,12},{11,13},{16,18},{17,... | collective-permute-start | bytes 1179656 | tf_op jit(solution)/shard_map/ppermute | solution.py:434
  264.6 18.2 %collective-permute-start.51 = (bf16[192,1024]{1,0:T(8,128)(2,1)S(1)}, bf16[192,1024]{1,0:T(8,128)(2,1)S(1)}, u32[]{:S(2)}, u32[]{:S(2)}) collective-permute-start(bf16[192,1024]{1,0:T(8,128)(2,1)S(1)} %fusion.4), channel_id=1, source_target_pairs={{4,2},{5,3},{6,4},{7,5},{12,10},{13,11},{14,12},{15,13},{20,18},{2... | collective-permute-start | bytes 1179656 | tf_op jit(solution)/shard_map/ppermute | solution.py:434
  269.2 16.1 %collective-permute-start.44 = (bf16[192,1024]{1,0:T(8,128)(2,1)}, bf16[192,1024]{1,0:T(8,128)(2,1)S(1)}, u32[]{:S(2)}, u32[]{:S(2)}) collective-permute-start(bf16[192,1024]{1,0:T(8,128)(2,1)} %fusion.9), channel_id=1, source_target_pairs={{0,2},{1,3},{2,4},{3,5},{4,6},{5,7},{8,10},{9,11},{10,12},{11,13},... | collective-permute-start | bytes 1179656 | tf_op jit(solution)/shard_map/ppermute | solution.py:434
  274.6 12.0 %collective-permute-start.41 = (bf16[192,1024]{1,0:T(8,128)(2,1)}, bf16[192,1024]{1,0:T(8,128)(2,1)}, u32[]{:S(2)}, u32[]{:S(2)}) collective-permute-start(bf16[192,1024]{1,0:T(8,128)(2,1)} %fusion.11), channel_id=1, source_target_pairs={{2,0},{3,1},{4,2},{5,3},{6,4},{7,5},{10,8},{11,9},{12,10},{13,11},... | collective-permute-start | bytes 1179656 | tf_op jit(solution)/shard_map/ppermute | solution.py:434
  277.6 15.6 %collective-permute-start.55 = (bf16[192,1024]{1,0:T(8,128)(2,1)}, bf16[192,1024]{1,0:T(8,128)(2,1)}, u32[]{:S(2)}, u32[]{:S(2)}) collective-permute-start(bf16[192,1024]{1,0:T(8,128)(2,1)} %fusion.3), channel_id=1, source_target_pairs={{0,2},{1,3},{2,4},{3,5},{4,6},{5,7},{8,10},{9,11},{10,12},{11,13},... | collective-permute-start | bytes 1179656 | tf_op jit(solution)/shard_map/ppermute | solution.py:434
  283.7 12.0 %collective-permute-start.52 = (bf16[192,1024]{1,0:T(8,128)(2,1)}, bf16[192,1024]{1,0:T(8,128)(2,1)}, u32[]{:S(2)}, u32[]{:S(2)}) collective-permute-start(bf16[192,1024]{1,0:T(8,128)(2,1)} %fusion.5), channel_id=1, source_target_pairs={{2,0},{3,1},{4,2},{5,3},{6,4},{7,5},{10,8},{11,9},{12,10},{13,11},... | collective-permute-start | bytes 1179656 | tf_op jit(solution)/shard_map/ppermute | solution.py:434
  (42 other events, 239.0 us)
